TPU v7x, 32 devices: a whole 2x2x4 slice. The times are simulated.
32 devices in a mesh: dp: 8 (over y, x, core), mp: 4 (over z).
Axes of the slice: x: 2, y: 2, z: 4, core: 2. Of those that a mesh axis runs over, the one named last changes fastest.
Arguments:
- latents: bfloat16 [8, 1023, 1536], P('dp'), may hold values from -6 to 6
- prompt_tokens: bfloat16 [8, 128, 768], P('dp'), may hold values from -6 to 6
- prompt_lengths: int32 [8], P('dp'), may hold values from 4 to 128, as said below
- timesteps: int32 [8], P('dp'), may hold values from 0 to 999
- time_weight: bfloat16 [256, 1536], P('dp'), may hold values from -0.5 to 0.5
- self_gain: float32 [1536], replicated, may hold values from 0.5 to 1.5
- self_bias: float32 [1536], replicated, may hold values from -1.75 to 1.75
- qkv_weight: bfloat16 [1536, 3, 1536], P('dp', None, 'mp'), may hold values from -0.15625 to 0.15625
- self_out_weight: bfloat16 [1536, 1536], P('mp', 'dp'), may hold values from -1.5 to 1.5
- cross_gain: float32 [1536], replicated, may hold values from 0.5 to 1.5
- cross_bias: float32 [1536], replicated, may hold values from -1.75 to 1.75
- cross_query_weight: bfloat16 [1536, 1536], P('dp', 'mp'), may hold values from -0.15625 to 0.15625
- context_weight: bfloat16 [768, 2, 1536], P('dp', None, 'mp'), may hold values from -0.21875 to 0.21875
- cross_out_weight: bfloat16 [1536, 1536], P('mp', 'dp'), may hold values from -0.75 to 0.75
- feed_gain: float32 [1536], replicated, may hold values from 0.5 to 1.5
- feed_bias: float32 [1536], replicated, may hold values from -1.75 to 1.75
- gate_up_weight: bfloat16 [1536, 2, 6144], P('dp', None, 'mp'), may hold values from -0.15625 to 0.15625
- down_weight: bfloat16 [6144, 1536], P('mp', 'dp'), may hold values from -0.109375 to 0.109375
- down_bias: float32 [1536], replicated, may hold values from -1.75 to 1.75
- cotangent: bfloat16 [8, 1024, 1536], P('dp', 'mp'), may hold values from -6 to 6
Outputs:
- output: bfloat16 [8, 1024, 1536], P('dp', 'mp')
- latents_grad: bfloat16 [8, 1023, 1536], P('dp')
- time_weight_grad: float32 [256, 1536], P('dp')
- self_gain_grad: float32 [1536], P('dp')
- self_bias_grad: float32 [1536], P('dp')
- qkv_weight_grad: float32 [1536, 3, 1536], P('dp', None, 'mp')
- self_out_grad: float32 [1536, 1536], P('mp', 'dp')
- cross_gain_grad: float32 [1536], P('dp')
- cross_bias_grad: float32 [1536], P('dp')
- cross_query_grad: float32 [1536, 1536], P('dp', 'mp')
- context_weight_grad: float32 [768, 2, 1536], P('dp', None, 'mp')
- cross_out_grad: float32 [1536, 1536], P('mp', 'dp')
- feed_gain_grad: float32 [1536], P('dp')
- feed_bias_grad: float32 [1536], P('dp')
- gate_up_grad: float32 [1536, 2, 6144], P('dp', None, 'mp')
- down_weight_grad: float32 [6144, 1536], P('mp', 'dp')
- down_bias_grad: float32 [1536], P('dp')
Inputs may be any that keep to these rules, and one draw needn't show every extreme that they name: `prompt_lengths`: short prompts are far commoner than long ones; some item of every draw has all 128 tokens.
All inputs are finite; a program needn't handle non-finite values.
Results may differ from a plain program's by a relative error of at most 0.025.
Values may be sent and summed in bfloat16 or wider, within the bound.
A program may use at most 192 MiB of HBM per device.

v0:
```python
import math

import jax
import jax.numpy as jnp
from jax import lax
from jax.sharding import PartitionSpec as P

HD = 64


EPS = 1e-05
NEG = -1e30


def time_features(steps_in, feature_width):
    half_width = feature_width // 2
    freqs = jnp.exp(-math.log(10000.0) * jnp.arange(half_width, dtype=jnp.float32) / half_width)
    angles = steps_in.astype(jnp.float32)[:, None] * freqs[None, :]
    return jnp.concatenate([jnp.cos(angles), jnp.sin(angles)], axis=-1)


def rope_tables(length, head_size):
    rotated_width = head_size // 2
    half_width = rotated_width // 2
    inverse = jnp.exp(
        -math.log(10000.0) * jnp.arange(half_width, dtype=jnp.float32) * 2.0 / rotated_width
    )
    angles = jnp.arange(length, dtype=jnp.float32)[:, None] * inverse[None, :]
    cosine = jnp.concatenate([jnp.cos(angles), jnp.cos(angles)], axis=-1)
    sine = jnp.concatenate([jnp.sin(angles), jnp.sin(angles)], axis=-1)
    return (cosine[:, None, :], sine[:, None, :])


def rotate(values, cosine, sine):
    rotated_width = cosine.shape[-1]
    half_width = rotated_width // 2
    first = values[..., :rotated_width]
    turned = jnp.concatenate([-first[..., half_width:], first[..., :half_width]], axis=-1)
    return jnp.concatenate([first * cosine + turned * sine, values[..., rotated_width:]], axis=-1)


def unrotate(grads_in, cosine, sine):
    rotated_width = cosine.shape[-1]
    half_width = rotated_width // 2
    first = grads_in[..., :rotated_width]
    scaled_in = first * sine
    turned = jnp.concatenate([scaled_in[..., half_width:], -scaled_in[..., :half_width]], axis=-1)
    return jnp.concatenate([first * cosine + turned, grads_in[..., rotated_width:]], axis=-1)


def layer_norm(values, gain, bias):
    centered = values - jnp.mean(values, axis=-1, keepdims=True)
    inverse = lax.rsqrt(jnp.mean(centered * centered, axis=-1, keepdims=True) + EPS)
    scaled = centered * inverse
    return (scaled * gain + bias, scaled, inverse)


def norm_back(grad_normed, scaled, inverse, gain):
    grad_scaled = grad_normed * gain
    first_mean = jnp.mean(grad_scaled, axis=-1, keepdims=True)
    second_mean = jnp.mean(grad_scaled * scaled, axis=-1, keepdims=True)
    grad_values = inverse * (grad_scaled - first_mean - scaled * second_mean)
    return (
        grad_values,
        jnp.sum(grad_normed * scaled, axis=(0, 1)),
        jnp.sum(grad_normed, axis=(0, 1)),
    )


def attend_forward(queries, key_rows, value_rows, bias_rows, block_size):
    score_scale = queries.shape[-1] ** (-0.5)

    def one_item(operands):
        item_query, item_key, item_value, item_bias = operands
        query_blocks = item_query.reshape(-1, block_size, item_query.shape[1], item_query.shape[2])

        def one_block(block_query):
            scores = jnp.einsum(
                "qhe,khe->hqk", block_query, item_key, preferred_element_type=jnp.float32
            )
            scores = scores * score_scale + item_bias[None, None, :]
            row_max = jnp.max(scores, axis=-1, keepdims=True)
            expos = jnp.exp(scores - row_max)
            row_total = jnp.sum(expos, axis=-1, keepdims=True)
            weights_p = (expos / row_total).astype(jnp.bfloat16)
            mixed = jnp.einsum(
                "hqk,khe->qhe", weights_p, item_value, preferred_element_type=jnp.float32
            )
            return (mixed, (row_max + jnp.log(row_total))[..., 0])

        mixed, log_total = lax.map(one_block, query_blocks)
        return (mixed.reshape(item_query.shape), log_total)

    return lax.map(one_item, (queries, key_rows, value_rows, bias_rows))


def attend_backward(queries, key_rows, value_rows, bias_rows, log_totals, grad_out, block_size):
    score_scale = queries.shape[-1] ** (-0.5)

    def one_item(operands):
        item_query, item_key, item_value, item_bias, item_log, item_grad = operands
        block_shape = (-1, block_size, item_query.shape[1], item_query.shape[2])
        query_blocks = item_query.reshape(block_shape)
        grad_blocks = item_grad.reshape(block_shape)

        def one_block(carry, operands_block):
            block_query, block_log, block_grad = operands_block
            scores = jnp.einsum(
                "qhe,khe->hqk", block_query, item_key, preferred_element_type=jnp.float32
            )
            scores = scores * score_scale + item_bias[None, None, :]
            probs_full = jnp.exp(scores - block_log[..., None])
            grad_probs = jnp.einsum(
                "qhe,khe->hqk", block_grad, item_value, preferred_element_type=jnp.float32
            )
            delta_row = jnp.sum(probs_full * grad_probs, axis=-1, keepdims=True)
            grad_scores = (probs_full * (grad_probs - delta_row)).astype(jnp.bfloat16)
            grad_query = (
                jnp.einsum(
                    "hqk,khe->qhe", grad_scores, item_key, preferred_element_type=jnp.float32
                )
                * score_scale
            )
            grad_key = (
                carry[0]
                + jnp.einsum(
                    "hqk,qhe->khe", grad_scores, block_query, preferred_element_type=jnp.float32
                )
                * score_scale
            )
            grad_value = carry[1] + jnp.einsum(
                "hqk,qhe->khe",
                probs_full.astype(jnp.bfloat16),
                block_grad,
                preferred_element_type=jnp.float32,
            )
            return ((grad_key, grad_value), grad_query)

        start_carry = (
            jnp.zeros(item_key.shape, jnp.float32),
            jnp.zeros(item_value.shape, jnp.float32),
        )
        (grad_key, grad_value), grad_query = lax.scan(
            one_block, start_carry, (query_blocks, item_log, grad_blocks)
        )
        return (grad_query.reshape(item_query.shape), grad_key, grad_value)

    return lax.map(one_item, (queries, key_rows, value_rows, bias_rows, log_totals, grad_out))


def per_device(
    latents,
    prompt_tokens,
    prompt_lengths,
    timesteps,
    time_weight,
    self_gain,
    self_bias,
    qkv_weight,
    self_out_weight,
    cross_gain,
    cross_bias,
    cross_query_weight,
    context_weight,
    cross_out_weight,
    feed_gain,
    feed_bias,
    gate_up_weight,
    down_weight,
    down_bias,
    cotangent,
):
    gathered = (
        lax.all_gather(time_weight, "dp", axis=0, tiled=True),
        lax.all_gather(qkv_weight, "dp", axis=0, tiled=True),
        lax.all_gather(self_out_weight, "dp", axis=1, tiled=True),
        lax.all_gather(cross_query_weight, "dp", axis=0, tiled=True),
        lax.all_gather(context_weight, "dp", axis=0, tiled=True),
        lax.all_gather(cross_out_weight, "dp", axis=1, tiled=True),
        lax.all_gather(gate_up_weight, "dp", axis=0, tiled=True),
        lax.all_gather(down_weight, "dp", axis=1, tiled=True),
    )
    (
        time_full,
        qkv_full,
        self_out_full,
        cross_query_full,
        context_full,
        cross_out_full,
        gate_up_full,
        down_full,
    ) = gathered
    items_here = latents.shape[0]
    seq_len = latents.shape[1] + 1
    shard_rows = seq_len // lax.axis_size("mp")
    first_row = lax.axis_index("mp") * shard_rows
    head_size = HD
    block_size = min(512, seq_len)
    features = time_features(timesteps, time_full.shape[0]).astype(jnp.bfloat16)
    token_row = jnp.dot(features, time_full, preferred_element_type=jnp.float32)
    residual_in = jnp.concatenate([token_row[:, None, :], latents.astype(jnp.float32)], axis=1)
    normed_one, scaled_one, inverse_one = layer_norm(residual_in, self_gain, self_bias)
    normed_one = normed_one.astype(jnp.bfloat16)
    projected = jnp.einsum(
        "bsd,dkc->bskc", normed_one, qkv_full, preferred_element_type=jnp.float32
    )
    heads_here = projected.shape[-1] // head_size
    head_shape = (items_here, seq_len, heads_here, head_size)
    cosine, sine = rope_tables(seq_len, head_size)
    queries = rotate(projected[:, :, 0].reshape(head_shape), cosine, sine).astype(jnp.bfloat16)
    key_rows = rotate(projected[:, :, 1].reshape(head_shape), cosine, sine).astype(jnp.bfloat16)
    value_rows = projected[:, :, 2].reshape(head_shape).astype(jnp.bfloat16)
    open_rows = jnp.zeros((items_here, seq_len), jnp.float32)
    attended, self_logs = attend_forward(queries, key_rows, value_rows, open_rows, block_size)
    attended = attended.reshape(items_here, seq_len, heads_here * head_size).astype(jnp.bfloat16)
    segment = attended
    self_branch = jnp.swapaxes(
        lax.psum_scatter(
            jnp.swapaxes(jnp.dot(segment, self_out_full, preferred_element_type=jnp.float32), 0, 1),
            "mp",
            scatter_dimension=0,
            tiled=True,
        ),
        0,
        1,
    )
    residual_one = lax.dynamic_slice_in_dim(residual_in, first_row, shard_rows, 1) + self_branch
    normed_two, scaled_two, inverse_two = layer_norm(residual_one, cross_gain, cross_bias)
    normed_two_all = lax.all_gather(normed_two.astype(jnp.bfloat16), "mp", axis=1, tiled=True)
    cross_q = (
        jnp.dot(normed_two_all, cross_query_full, preferred_element_type=jnp.float32)
        .astype(jnp.bfloat16)
        .reshape(head_shape)
    )
    context = jnp.einsum(
        "bpc,ckh->bpkh", prompt_tokens, context_full, preferred_element_type=jnp.float32
    ).astype(jnp.bfloat16)
    prompt_slots = prompt_tokens.shape[1]
    context_shape = (items_here, prompt_slots, heads_here, head_size)
    context_keys = context[:, :, 0].reshape(context_shape)
    context_values = context[:, :, 1].reshape(context_shape)
    slot_index = jnp.arange(prompt_slots, dtype=jnp.int32)
    mask_rows = jnp.where(slot_index[None, :] < prompt_lengths[:, None], 0.0, NEG).astype(
        jnp.float32
    )
    crossed, cross_logs = attend_forward(
        cross_q, context_keys, context_values, mask_rows, block_size
    )
    crossed = crossed.reshape(items_here, seq_len, heads_here * head_size).astype(jnp.bfloat16)
    segment = crossed
    cross_branch = jnp.swapaxes(
        lax.psum_scatter(
            jnp.swapaxes(
                jnp.dot(segment, cross_out_full, preferred_element_type=jnp.float32), 0, 1
            ).astype(jnp.bfloat16),
            "mp",
            scatter_dimension=0,
            tiled=True,
        ).astype(jnp.float32),
        0,
        1,
    )
    residual_two = residual_one + cross_branch
    normed_three, scaled_three, inverse_three = layer_norm(residual_two, feed_gain, feed_bias)
    normed_three_all = lax.all_gather(normed_three.astype(jnp.bfloat16), "mp", axis=1, tiled=True)
    gate_up = jnp.einsum(
        "bsd,dkf->bskf", normed_three_all, gate_up_full, preferred_element_type=jnp.float32
    )
    gate_part = gate_up[:, :, 0]
    up_part = gate_up[:, :, 1]
    hidden = (jax.nn.silu(gate_part) * up_part).astype(jnp.bfloat16)
    segment = hidden
    feed_branch = jnp.swapaxes(
        lax.psum_scatter(
            jnp.swapaxes(
                jnp.dot(segment, down_full, preferred_element_type=jnp.float32), 0, 1
            ).astype(jnp.bfloat16),
            "mp",
            scatter_dimension=0,
            tiled=True,
        ).astype(jnp.float32),
        0,
        1,
    )
    output = (residual_two + feed_branch + down_bias).astype(jnp.bfloat16)
    regathered = (
        lax.all_gather(qkv_weight, "dp", axis=0, tiled=True),
        lax.all_gather(self_out_weight, "dp", axis=1, tiled=True),
        lax.all_gather(cross_query_weight, "dp", axis=0, tiled=True),
        lax.all_gather(context_weight, "dp", axis=0, tiled=True),
        lax.all_gather(cross_out_weight, "dp", axis=1, tiled=True),
        lax.all_gather(gate_up_weight, "dp", axis=0, tiled=True),
        lax.all_gather(down_weight, "dp", axis=1, tiled=True),
    )
    (
        qkv_back,
        self_out_back,
        cross_query_back,
        context_back,
        cross_out_back,
        gate_up_back,
        down_back,
    ) = regathered
    grad_rows = lax.all_gather(cotangent, "mp", axis=1, tiled=True)
    grad_hidden = jnp.einsum(
        "bsd,fd->bsf", grad_rows, down_back, preferred_element_type=jnp.float32
    )
    sigmoid_gate = jax.nn.sigmoid(gate_part)
    grad_up = grad_hidden * gate_part * sigmoid_gate
    grad_gate = grad_hidden * up_part * sigmoid_gate * (1.0 + gate_part * (1.0 - sigmoid_gate))
    grad_gate_up = jnp.stack([grad_gate, grad_up], axis=2).astype(jnp.bfloat16)
    down_weight_grad = jnp.einsum(
        "bsf,bsd->fd", hidden, grad_rows, preferred_element_type=jnp.float32
    )
    gate_up_grad = jnp.einsum(
        "bsd,bskf->dkf", normed_three_all, grad_gate_up, preferred_element_type=jnp.float32
    )
    segment = grad_gate_up
    grad_normed_three = jnp.swapaxes(
        lax.psum_scatter(
            jnp.swapaxes(
                jnp.einsum(
                    "bskf,dkf->bsd", segment, gate_up_back, preferred_element_type=jnp.float32
                ),
                0,
                1,
            ).astype(jnp.bfloat16),
            "mp",
            scatter_dimension=0,
            tiled=True,
        ).astype(jnp.float32),
        0,
        1,
    )
    grad_two_norm, feed_gain_part, feed_bias_part = norm_back(
        grad_normed_three, scaled_three, inverse_three, feed_gain
    )
    grad_out_shard = cotangent.astype(jnp.float32)
    down_bias_part = jnp.sum(grad_out_shard, axis=(0, 1))
    grad_residual_two = (grad_out_shard + grad_two_norm).astype(jnp.bfloat16)
    grad_rows_two = lax.all_gather(grad_residual_two, "mp", axis=1, tiled=True)
    grad_crossed = jnp.einsum(
        "bsd,hd->bsh", grad_rows_two, cross_out_back, preferred_element_type=jnp.float32
    ).astype(jnp.bfloat16)
    cross_out_grad = jnp.einsum(
        "bsh,bsd->hd", crossed, grad_rows_two, preferred_element_type=jnp.float32
    )
    grad_cross_q, grad_cross_k, grad_cross_v = attend_backward(
        cross_q,
        context_keys,
        context_values,
        mask_rows,
        cross_logs,
        grad_crossed.reshape(head_shape),
        block_size,
    )
    grad_cross_q = grad_cross_q.reshape(items_here, seq_len, heads_here * head_size).astype(
        jnp.bfloat16
    )
    grad_context = (
        jnp.stack([grad_cross_k, grad_cross_v], axis=2)
        .reshape(items_here, prompt_slots, 2, heads_here * head_size)
        .astype(jnp.bfloat16)
    )
    cross_query_grad = jnp.einsum(
        "bsd,bsh->dh", normed_two_all, grad_cross_q, preferred_element_type=jnp.float32
    )
    context_weight_grad = jnp.einsum(
        "bpc,bpkh->ckh", prompt_tokens, grad_context, preferred_element_type=jnp.float32
    )
    segment = grad_cross_q
    grad_normed_two = jnp.swapaxes(
        lax.psum_scatter(
            jnp.swapaxes(
                jnp.einsum(
                    "bsh,dh->bsd", segment, cross_query_back, preferred_element_type=jnp.float32
                ),
                0,
                1,
            ).astype(jnp.bfloat16),
            "mp",
            scatter_dimension=0,
            tiled=True,
        ).astype(jnp.float32),
        0,
        1,
    )
    grad_one_norm, cross_gain_part, cross_bias_part = norm_back(
        grad_normed_two, scaled_two, inverse_two, cross_gain
    )
    grad_residual_one = (grad_residual_two.astype(jnp.float32) + grad_one_norm).astype(jnp.bfloat16)
    grad_rows_one = lax.all_gather(grad_residual_one, "mp", axis=1, tiled=True)
    grad_attended = jnp.einsum(
        "bsd,hd->bsh", grad_rows_one, self_out_back, preferred_element_type=jnp.float32
    ).astype(jnp.bfloat16)
    self_out_grad = jnp.einsum(
        "bsh,bsd->hd", attended, grad_rows_one, preferred_element_type=jnp.float32
    )
    grad_query, grad_key, grad_value = attend_backward(
        queries,
        key_rows,
        value_rows,
        open_rows,
        self_logs,
        grad_attended.reshape(head_shape),
        block_size,
    )
    grad_query = unrotate(grad_query, cosine, sine)
    grad_key = unrotate(grad_key, cosine, sine)
    grad_projected = (
        jnp.stack([grad_query, grad_key, grad_value], axis=2)
        .reshape(items_here, seq_len, 3, heads_here * head_size)
        .astype(jnp.bfloat16)
    )
    qkv_weight_grad = jnp.einsum(
        "bsd,bskc->dkc", normed_one, grad_projected, preferred_element_type=jnp.float32
    )
    grad_normed_part = jnp.einsum(
        "bskc,dkc->bsd", grad_projected, qkv_back, preferred_element_type=jnp.float32
    )
    summed = (
        lax.psum(grad_normed_part.astype(jnp.bfloat16), "mp").astype(jnp.float32),
        lax.psum(cross_gain_part.astype(jnp.bfloat16), "mp").astype(jnp.float32),
        lax.psum(cross_bias_part.astype(jnp.bfloat16), "mp").astype(jnp.float32),
        lax.psum(feed_gain_part.astype(jnp.bfloat16), "mp").astype(jnp.float32),
        lax.psum(feed_bias_part.astype(jnp.bfloat16), "mp").astype(jnp.float32),
        lax.psum(down_bias_part.astype(jnp.bfloat16), "mp").astype(jnp.float32),
    )
    grad_in_norm, self_gain_part, self_bias_part = norm_back(
        summed[0], scaled_one, inverse_one, self_gain
    )
    grad_residual_in = grad_rows_one.astype(jnp.float32) + grad_in_norm
    latents_grad = grad_residual_in[:, 1:].astype(jnp.bfloat16)
    time_weight_grad = jnp.dot(
        features.astype(jnp.float32).T, grad_residual_in[:, 0], precision=lax.Precision.HIGHEST
    )
    cross_gain_sum, cross_bias_sum, feed_gain_sum, feed_bias_sum, down_bias_sum = (
        summed[1],
        summed[2],
        summed[3],
        summed[4],
        summed[5],
    )
    reduced = (
        lax.psum_scatter(
            time_weight_grad.astype(jnp.bfloat16), "dp", scatter_dimension=0, tiled=True
        ).astype(jnp.float32),
        lax.psum_scatter(
            qkv_weight_grad.astype(jnp.bfloat16), "dp", scatter_dimension=0, tiled=True
        ).astype(jnp.float32),
        lax.psum_scatter(
            self_out_grad.astype(jnp.bfloat16), "dp", scatter_dimension=1, tiled=True
        ).astype(jnp.float32),
        lax.psum_scatter(
            cross_query_grad.astype(jnp.bfloat16), "dp", scatter_dimension=0, tiled=True
        ).astype(jnp.float32),
        lax.psum_scatter(
            context_weight_grad.astype(jnp.bfloat16), "dp", scatter_dimension=0, tiled=True
        ).astype(jnp.float32),
        lax.psum_scatter(
            cross_out_grad.astype(jnp.bfloat16), "dp", scatter_dimension=1, tiled=True
        ).astype(jnp.float32),
        lax.psum_scatter(
            gate_up_grad.astype(jnp.bfloat16), "dp", scatter_dimension=0, tiled=True
        ).astype(jnp.float32),
        lax.psum_scatter(
            down_weight_grad.astype(jnp.bfloat16), "dp", scatter_dimension=1, tiled=True
        ).astype(jnp.float32),
        lax.psum_scatter(
            self_gain_part.astype(jnp.bfloat16), "dp", scatter_dimension=0, tiled=True
        ).astype(jnp.float32),
        lax.psum_scatter(
            self_bias_part.astype(jnp.bfloat16), "dp", scatter_dimension=0, tiled=True
        ).astype(jnp.float32),
        lax.psum_scatter(
            cross_gain_sum.astype(jnp.bfloat16), "dp", scatter_dimension=0, tiled=True
        ).astype(jnp.float32),
        lax.psum_scatter(
            cross_bias_sum.astype(jnp.bfloat16), "dp", scatter_dimension=0, tiled=True
        ).astype(jnp.float32),
        lax.psum_scatter(
            feed_gain_sum.astype(jnp.bfloat16), "dp", scatter_dimension=0, tiled=True
        ).astype(jnp.float32),
        lax.psum_scatter(
            feed_bias_sum.astype(jnp.bfloat16), "dp", scatter_dimension=0, tiled=True
        ).astype(jnp.float32),
        lax.psum_scatter(
            down_bias_sum.astype(jnp.bfloat16), "dp", scatter_dimension=0, tiled=True
        ).astype(jnp.float32),
    )
    return (
        output,
        latents_grad,
        reduced[0],
        reduced[8],
        reduced[9],
        reduced[1],
        reduced[2],
        reduced[10],
        reduced[11],
        reduced[3],
        reduced[4],
        reduced[5],
        reduced[12],
        reduced[13],
        reduced[6],
        reduced[7],
        reduced[14],
    )


def solution(mesh):
    placed = (
        P("dp", None, None),
        P("dp", None, None),
        P("dp"),
        P("dp"),
        P("dp", None),
        P(),
        P(),
        P("dp", None, "mp"),
        P("mp", "dp"),
        P(),
        P(),
        P("dp", "mp"),
        P("dp", None, "mp"),
        P("mp", "dp"),
        P(),
        P(),
        P("dp", None, "mp"),
        P("mp", "dp"),
        P(),
        P("dp", "mp", None),
    )
    return jax.shard_map(
        per_device,
        mesh=mesh,
        in_specs=placed,
        out_specs=(
            P("dp", "mp", None),
            P("dp", None, None),
            P("dp", None),
            P("dp"),
            P("dp"),
            P("dp", None, "mp"),
            P("mp", "dp"),
            P("dp"),
            P("dp"),
            P("dp", "mp"),
            P("dp", None, "mp"),
            P("mp", "dp"),
            P("dp"),
            P("dp"),
            P("dp", None, "mp"),
            P("mp", "dp"),
            P("dp"),
        ),
        check_vma=False,
    )
```

profile of v0, /device:TPU:1, one launch (start us, length us, event | category | flops | bytes accessed | tf_op | source)
XLA Modules:
  0.0 1677.5 jit_solution(2373560016104457918)
XLA Ops:
  10.4 12.1 all_gather.45
  22.5 6.2 fusion.183
  34.0 12.4 all-gather.13.cloned.1.call-done
  46.5 8.0 convolution_bitcast_fusion.4
  66.7 20.4 %while.97 = (s32[]{:T(128)}, bf16[2,512,6,64]{1,3,2,0:T(8,128)(2,1)S(1)}, f32[2,6,512]{2,1,0:T(8,128)S(1)}, bf16[2,512,6,64]{1,3,2,0:T(8,128)(2,1)}, bf16[1024,6...) while((s32[]{:T(128)}, bf16[2,512,6,64]{1,3,2,0:T(8,128)(2,1)S(1)}, ...), condition=%wide.region_5.6_spmd, body=%wide.region_2.5_spmd.sunk | while | flops 833614848 | bytes 40620128 | solution.py:91
  72.4 4.2 fusion.261
  82.4 4.2 fusion.261
  88.2 6.1 convolution_bitcast_fusion.3
  96.5 108.3 %reduce-scatter.13.cloned.1.call-done = f32[256,1,1536]{2,0,1:T(8,128)} async-done(((f32[1024,1,1536]{2,0,1:T(8,128)}), f32[256,1,1536]{2,0,1:T(8,128)}) %reduce-scatter.13.cloned.1.call-update) | async-done | bytes 1572880 | tf_op jit(solution)/shard_map/reduce_scatter | solution.py:218
  209.4 22.7 %all-gather.21.cloned.1.call-done = bf16[768,2,384]{2,0,1:T(8,128)(2,1)} async-done(((bf16[96,2,384]{2,0,1:T(8,128)(2,1)}), bf16[768,2,384]{2,0,1:T(8,128)(2,1)}) %all-gather.21.cloned.1.call-update) | async-done | bytes 1179664 | tf_op jit(solution)/shard_map/all_gather | solution.py:178
  234.0 23.9 %all-gather.19.cloned.1.call-done = bf16[1536,384]{1,0:T(8,128)(2,1)} async-done(((bf16[192,384]{1,0:T(8,128)(2,1)}), bf16[1536,384]{1,0:T(8,128)(2,1)}) %all-gather.19.cloned.1.call-update) | async-done | bytes 1179664 | tf_op jit(solution)/shard_map/all_gather | solution.py:177
  257.9 65.1 %all-gather.17.cloned.1.call-done = bf16[1,1024,1536]{2,1,0:T(8,128)(2,1)} async-done(((bf16[1,256,1536]{2,1,0:T(8,128)(2,1)}), bf16[1,1024,1536]{2,1,0:T(8,128)(2,1)}) %all-gather.17.cloned.1.call-update) | async-done | bytes 3145744 | tf_op jit(solution)/shard_map/all_gather | solution.py:229
  323.0 4.9 fusion.143
  333.5 7.4 while.98
  343.9 4.2 all-gather.23.cloned.1.call-done
  348.1 5.0 fusion.86
  355.7 57.3 %reduce-scatter.15.cloned.1.call-done = bf16[256,1,1536]{2,0,1:T(8,128)(2,1)} async-done(((bf16[1024,1,1536]{2,0,1:T(8,128)(2,1)}), bf16[256,1,1536]{2,0,1:T(8,128)(2,1)}) %reduce-scatter.15.cloned.1.call-update) | async-done | bytes 786448 | tf_op jit(solution)/shard_map/reduce_scatter | solution.py:252
  418.7 56.2 %all-gather.27.cloned.1.call-done = bf16[1536,2,1536]{2,0,1:T(8,128)(2,1)} async-done(((bf16[192,2,1536]{2,0,1:T(8,128)(2,1)}), bf16[1536,2,1536]{2,0,1:T(8,128)(2,1)}) %all-gather.27.cloned.1.call-update) | async-done | bytes 9437200 | tf_op jit(solution)/shard_map/all_gather | solution.py:180
  474.9 65.1 %all-gather.25.cloned.1.call-done = bf16[1,1024,1536]{2,1,0:T(8,128)(2,1)} async-done(((bf16[1,256,1536]{2,1,0:T(8,128)(2,1)}), bf16[1,1024,1536]{2,1,0:T(8,128)(2,1)}) %all-gather.25.cloned.1.call-update) | async-done | bytes 3145744 | tf_op jit(solution)/shard_map/all_gather | solution.py:265
  540.0 16.4 convolution_bitcast_fusion.2
  556.4 47.3 %all-gather.31.cloned.1.call-done = bf16[1,1024,1536]{2,1,0:T(8,128)(2,1)} async-done(((bf16[1,256,1536]{2,1,0:T(8,128)(2,1)}), bf16[1,1024,1536]{2,1,0:T(8,128)(2,1)}) %all-gather.31.cloned.1.call-update) | async-done | bytes 3145744 | tf_op jit(solution)/shard_map/all_gather | solution.py:304
  603.7 39.8 %all-gather.29.cloned.1.call-done = bf16[1536,1536]{0,1:T(8,128)(2,1)} async-done(((bf16[1536,192]{0,1:T(8,128)(2,1)}), bf16[1536,1536]{0,1:T(8,128)(2,1)}) %all-gather.29.cloned.1.call-update) | async-done | bytes 4718608 | tf_op jit(solution)/shard_map/all_gather | solution.py:181
  643.5 11.8 fusion.109
  658.0 13.6 fusion.84
  671.6 10.6 fusion.83
  682.6 48.8 %reduce-scatter.19.cloned.1.call-done = bf16[256,1,1536]{2,0,1:T(8,128)(2,1)} async-done(((bf16[1024,1,1536]{2,0,1:T(8,128)(2,1)}), bf16[256,1,1536]{2,0,1:T(8,128)(2,1)}) %reduce-scatter.19.cloned.1.call-update) | async-done | bytes 786448 | tf_op jit(solution)/shard_map/reduce_scatter | solution.py:320
  735.4 58.5 %reduce-scatter.17.cloned.1.call-done = bf16[256,1,1536]{2,0,1:T(8,128)(2,1)} async-done(((bf16[1024,1,1536]{2,0,1:T(8,128)(2,1)}), bf16[256,1,1536]{2,0,1:T(8,128)(2,1)}) %reduce-scatter.17.cloned.1.call-update) | async-done | bytes 786448 | tf_op jit(solution)/shard_map/reduce_scatter | solution.py:274
  793.9 4.2 fusion.135
  798.1 63.7 %all-gather.33.cloned.1.call-done = bf16[1,1024,1536]{2,1,0:T(8,128)(2,1)} async-done(((bf16[1,256,1536]{2,1,0:T(8,128)(2,1)}), bf16[1,1024,1536]{2,1,0:T(8,128)(2,1)}) %all-gather.33.cloned.1.call-update) | async-done | bytes 3145744 | tf_op jit(solution)/shard_map/all_gather | solution.py:341
  861.9 4.9 fusion.146
  875.4 12.9 while.99
  894.9 58.9 %reduce-scatter.21.cloned.1.call-done = bf16[256,1,1536]{2,0,1:T(8,128)(2,1)} async-done(((bf16[1024,1,1536]{2,0,1:T(8,128)(2,1)}), bf16[256,1,1536]{2,0,1:T(8,128)(2,1)}) %reduce-scatter.21.cloned.1.call-update) | async-done | bytes 786448 | tf_op jit(solution)/shard_map/reduce_scatter | solution.py:373
  959.0 63.7 %all-gather.35.cloned.1.call-done = bf16[1,1024,1536]{2,1,0:T(8,128)(2,1)} async-done(((bf16[1,256,1536]{2,1,0:T(8,128)(2,1)}), bf16[1,1024,1536]{2,1,0:T(8,128)(2,1)}) %all-gather.35.cloned.1.call-update) | async-done | bytes 3145744 | tf_op jit(solution)/shard_map/all_gather | solution.py:392
  1022.7 4.9 fusion.149
  1032.6 85.0 %while.100 = (s32[]{:T(128)}, f32[1024,6,64]{0,2,1:T(8,128)S(1)}, f32[1024,6,64]{0,2,1:T(8,128)}, f32[2,512,6,64]{1,0,3,2:T(2,128)}, bf16[2,512,6,64]{1,3,2,0:T(...) while((s32[]{:T(128)}, f32[1024,6,64]{0,2,1:T(8,128)S(1)}, ...), condition=%wide.region_28.29_spmd.clone, body=%wide.region_26.28_spmd.clone.sunk | while | flops 2053174272 | bytes 108613792 | solution.py:143
  1035.8 4.6 bitcast_add_fusion.5
  1040.5 7.8 multiply_reduce_fusion.11
  1048.3 6.5 multiply_convert_fusion.8
  1060.0 15.0 dynamic_update_slice.69
  1077.8 5.2 bitcast_add_fusion.5
  1083.0 7.8 multiply_reduce_fusion.11
  1090.8 6.5 multiply_convert_fusion.8
  1102.6 15.0 dynamic_update_slice.69
  1132.8 7.9 fusion.85
  1140.8 11.0 convolution_convert_fusion.1
  1156.2 4.9 fusion.113
  1161.1 4.8 fusion.110
  1166.0 15.8 convolution_convert_fusion
  1183.0 4.8 fusion.116
  1187.8 72.8 %all-reduce.13.cloned.1.call-done = bf16[1,1024,1536]{2,1,0:T(8,128)(2,1)} async-done(((bf16[1,1024,1536]{2,1,0:T(8,128)(2,1)}), bf16[1,1024,1536]{2,1,0:T(8,128)(2,1)}) %all-reduce.13.cloned.1.call-update) | async-done | bytes 3145744 | tf_op jit(solution)/shard_map/psum | solution.py:422
  1260.7 6.3 fusion.68
  1267.1 6.1 fusion.66
  1277.4 9.6 convolution_convert_fusion.2
  1289.8 27.2 %reduce-scatter.35.cloned.1.call-done = bf16[1536,192]{0,1:T(8,128)(2,1)} async-done(((bf16[1536,1536]{0,1:T(8,128)(2,1)}), bf16[1536,192]{0,1:T(8,128)(2,1)}) %reduce-scatter.35.cloned.1.call-update) | async-done | bytes 589840 | tf_op jit(solution)/shard_map/reduce_scatter | solution.py:466
  1319.3 57.3 %all-reduce.15.cloned.1.call-done = bf16[768,2,384]{2,1,0:T(2,128)(2,1)} async-done(((bf16[768,2,384]{2,1,0:T(2,128)(2,1)}), bf16[768,2,384]{2,1,0:T(2,128)(2,1)}) %all-reduce.15.cloned.1.call-update) | async-done | bytes 1179664
  1378.3 38.3 %reduce-scatter.31.cloned.1.call-done = bf16[384,192]{0,1:T(8,128)(2,1)} async-done(((bf16[384,1536]{0,1:T(8,128)(2,1)}), bf16[384,192]{0,1:T(8,128)(2,1)}) %reduce-scatter.31.cloned.1.call-update) | async-done | bytes 147472 | tf_op jit(solution)/shard_map/reduce_scatter | solution.py:460
  1418.2 39.3 %reduce-scatter.29.cloned.1.call-done = bf16[192,384]{1,0:T(8,128)(2,1)} async-done(((bf16[1536,384]{1,0:T(8,128)(2,1)}), bf16[192,384]{1,0:T(8,128)(2,1)}) %reduce-scatter.29.cloned.1.call-update) | async-done | bytes 147472 | tf_op jit(solution)/shard_map/reduce_scatter | solution.py:454
  1459.2 78.5 %reduce-scatter.33.cloned.1.call-done = bf16[192,2,1536]{2,0,1:T(8,128)(2,1)} async-done(((bf16[1536,2,1536]{2,0,1:T(8,128)(2,1)}), bf16[192,2,1536]{2,0,1:T(8,128)(2,1)}) %reduce-scatter.33.cloned.1.call-update) | async-done | bytes 1179664 | tf_op jit(solution)/shard_map/reduce_scatter | solution.py:463
  1537.6 3.9 copy.115
  1541.6 35.8 %reduce-scatter.27.cloned.1.call-done = bf16[384,192]{0,1:T(8,128)(2,1)} async-done(((bf16[384,1536]{0,1:T(8,128)(2,1)}), bf16[384,192]{0,1:T(8,128)(2,1)}) %reduce-scatter.27.cloned.1.call-update) | async-done | bytes 147472 | tf_op jit(solution)/shard_map/reduce_scatter | solution.py:451
  1579.1 5.3 slice.185
  1586.7 20.6 %all-reduce.8 = (bf16[1536]{0:T(1024)(128)(2,1)S(1)}, bf16[1536]{0:T(1024)(128)(2,1)S(1)}, bf16[1536]{0:T(1024)(128)(2,1)S(1)}, bf16[1536]{0:T(1024)(128)(2,1)S(...) all-reduce(bf16[1536]{0:T(1024)(128)(2,1)S(1)} %get-tuple-element.5, ...), channel_id=8, replica_groups=mesh['dp'=8,'mp'=4] {'dp'}, use_global_device_ids=true, to_apply=%region_34.35.clone | all-reduce | flops 10752 | bytes 43008
  1607.7 9.6 all-reduce.9
  1623.1 45.5 %reduce-scatter.25.cloned.1.call-done = bf16[192,3,384]{2,0,1:T(8,128)(2,1)} async-done(((bf16[1536,3,384]{2,0,1:T(8,128)(2,1)}), bf16[192,3,384]{2,0,1:T(8,128)(2,1)}) %reduce-scatter.25.cloned.1.call-update) | async-done | bytes 442384 | tf_op jit(solution)/shard_map/reduce_scatter | solution.py:448
  (373 shorter events, 172.3 us)
Async XLA Ops:
  7.2 224.9 %copy-start = (bf16[1,128,768]{2,1,0:T(8,128)(2,1)S(1)}, bf16[1,128,768]{2,1,0:T(8,128)(2,1)}, u32[]{:S(2)}) copy-start(bf16[1,128,768]{2,1,0:T(8,128)(2,1)} %param.29) | copy-start | bytes 589828
  7.2 39.2 %all-gather.13.cloned.1.call-start = ((), (), s32[]{:S(2)}) async-start(), calls=%async_computation.12 | async-start | bytes 3981312 | tf_op jit(solution)/shard_map/all_gather | solution.py:175
  7.9 80.2 %all-gather.15.cloned.1.call-start = ((), (), s32[]{:S(2)}) async-start(), calls=%async_computation.13 | async-start | bytes 1327104 | tf_op jit(solution)/shard_map/all_gather | solution.py:176
  8.7 196.1 %reduce-scatter.13.cloned.1.call-start = ((), (), s32[]{:S(2)}) async-start(), calls=%async_computation.14 | async-start | bytes 7864320 | tf_op jit(solution)/shard_map/reduce_scatter | solution.py:218
  28.9 175.9 %copy-start.41 = (f32[1,1536]{1,0:T(1,128)}, f32[1,1536]{1,0:T(1,128)S(1)}, u32[]{:S(2)}) copy-start(f32[1,1536]{1,0:T(1,128)S(1)} %fusion.189) | copy-start | bytes 18436
  31.4 15.0 copy-start.46
  31.4 15.0 copy-start.50
  31.4 15.0 copy-start.64
  33.3 21.1 %copy-start.48 = (f32[1024]{0:T(1024)}, f32[1024]{0:T(1024)S(1)}, u32[]{:S(2)}) copy-start(f32[1024]{0:T(1024)S(1)} %add_rsqrt_fusion) | copy-start | bytes 12292
  34.0 26.0 %copy-start.25 = (f32[1024,32]{0,1:T(8,128)}, f32[1024,32]{0,1:T(8,128)S(1)}, u32[]{:S(2)}) copy-start(f32[1024,32]{0,1:T(8,128)S(1)} %get-tuple-element.691) | copy-start | bytes 393220
  87.2 7.1 copy-start.37
  88.1 6.1 copy-start.17
  94.2 137.9 %all-gather.21.cloned.1.call-start = ((), (), s32[]{:S(2)}) async-start(), calls=%async_computation.17 | async-start | bytes 1327104 | tf_op jit(solution)/shard_map/all_gather | solution.py:178
  95.8 162.1 %all-gather.19.cloned.1.call-start = ((), (), s32[]{:S(2)}) async-start(), calls=%async_computation.16 | async-start | bytes 1327104 | tf_op jit(solution)/shard_map/all_gather | solution.py:177
  96.4 226.6 %all-gather.17.cloned.1.call-start = ((), (), s32[]{:S(2)}) async-start(), calls=%async_computation.15 | async-start | bytes 3932160 | tf_op jit(solution)/shard_map/all_gather | solution.py:229
  96.5 110.9 %copy-start.45 = (f32[1536]{0:T(1024)S(1)}, f32[1536]{0:T(1024)}, u32[]{:S(2)}) copy-start(f32[1536]{0:T(1024)} %param.37) | copy-start | bytes 18436
  96.5 110.9 %copy-start.60 = (f32[1536]{0:T(1024)S(1)}, f32[1536]{0:T(1024)}, u32[]{:S(2)}) copy-start(f32[1536]{0:T(1024)} %param.38) | copy-start | bytes 18436
  207.0 25.1 %copy-start.52 = (f32[256]{0:T(256)}, f32[256]{0:T(256)S(1)}, u32[]{:S(2)}) copy-start(f32[256]{0:T(256)S(1)} %broadcast_multiply_fusion.8) | copy-start | bytes 3076
  207.4 24.7 %copy-start.55 = (f32[256]{0:T(256)}, f32[256]{0:T(256)S(1)}, u32[]{:S(2)}) copy-start(f32[256]{0:T(256)S(1)} %add_rsqrt_fusion.2) | copy-start | bytes 3076
  208.6 139.5 %all-gather.23.cloned.1.call-start = ((), (), s32[]{:S(2)}) async-start(), calls=%async_computation.18 | async-start | bytes 1327104 | tf_op jit(solution)/shard_map/all_gather | solution.py:179
  209.4 203.6 %reduce-scatter.15.cloned.1.call-start = ((), (), s32[]{:S(2)}) async-start(), calls=%async_computation.19 | async-start | bytes 3932160 | tf_op jit(solution)/shard_map/reduce_scatter | solution.py:252
  353.1 121.8 %all-gather.27.cloned.1.call-start = ((), (), s32[]{:S(2)}) async-start(), calls=%async_computation.21 | async-start | bytes 10616832 | tf_op jit(solution)/shard_map/all_gather | solution.py:180
  355.6 60.5 %copy-start.44 = (f32[1536]{0:T(1024)S(1)}, f32[1536]{0:T(1024)}, u32[]{:S(2)}) copy-start(f32[1536]{0:T(1024)} %param.42) | copy-start | bytes 18436
  355.6 184.3 %all-gather.25.cloned.1.call-start = ((), (), s32[]{:S(2)}) async-start(), calls=%async_computation.20 | async-start | bytes 3932160 | tf_op jit(solution)/shard_map/all_gather | solution.py:265
  413.0 3.1 copy-start.61
  417.3 186.4 %all-gather.31.cloned.1.call-start = ((), (), s32[]{:S(2)}) async-start(), calls=%async_computation.24 | async-start | bytes 3932160 | tf_op jit(solution)/shard_map/all_gather | solution.py:304
  418.0 225.5 %all-gather.29.cloned.1.call-start = ((), (), s32[]{:S(2)}) async-start(), calls=%async_computation.22 | async-start | bytes 5308416 | tf_op jit(solution)/shard_map/all_gather | solution.py:181
  418.6 312.8 %reduce-scatter.19.cloned.1.call-start = ((), (), s32[]{:S(2)}) async-start(), calls=%async_computation.25 | async-start | bytes 3932160 | tf_op jit(solution)/shard_map/reduce_scatter | solution.py:320
  671.6 122.3 %reduce-scatter.17.cloned.1.call-start = ((), (), s32[]{:S(2)}) async-start(), calls=%async_computation.23 | async-start | bytes 3932160 | tf_op jit(solution)/shard_map/reduce_scatter | solution.py:274
  682.3 179.6 %all-gather.33.cloned.1.call-start = ((), (), s32[]{:S(2)}) async-start(), calls=%async_computation.26 | async-start | bytes 3932160 | tf_op jit(solution)/shard_map/all_gather | solution.py:341
  798.1 155.8 %reduce-scatter.21.cloned.1.call-start = ((), (), s32[]{:S(2)}) async-start(), calls=%async_computation.27 | async-start | bytes 3932160 | tf_op jit(solution)/shard_map/reduce_scatter | solution.py:373
  888.2 3.1 copy-start.63
  894.9 59.0 %copy-start.53 = (f32[256]{0:T(256)S(1)}, f32[256]{0:T(256)}, u32[]{:S(2)}) copy-start(f32[256]{0:T(256)} %copy-done.52) | copy-start | bytes 3076
  894.9 59.0 %copy-start.56 = (f32[256]{0:T(256)S(1)}, f32[256]{0:T(256)}, u32[]{:S(2)}) copy-start(f32[256]{0:T(256)} %copy-done.55) | copy-start | bytes 3076
  894.9 61.4 %copy-start.11 = (bf16[1,256,1536]{2,1,0:T(8,128)(2,1)S(1)}, bf16[1,256,1536]{2,1,0:T(8,128)(2,1)}, u32[]{:S(2)}) copy-start(bf16[1,256,1536]{2,1,0:T(8,128)(2,1)} %get-tuple-element.669) | copy-start | bytes 2359300
  894.9 127.8 %all-gather.35.cloned.1.call-start = ((), (), s32[]{:S(2)}) async-start(), calls=%async_computation.28 | async-start | bytes 3932160 | tf_op jit(solution)/shard_map/all_gather | solution.py:392
  958.9 301.7 %all-reduce.13.cloned.1.call-start = ((), (), s32[]{:S(2)}) async-start(), calls=%async_computation.29 | async-start | bytes 6291456 | tf_op jit(solution)/shard_map/psum | solution.py:422
  1027.6 5.0 copy-start.38
  1117.6 6.4 copy-start.27
  1125.2 4.9 copy-start.26
  1132.1 8.6 copy-start.33
  1132.8 7.9 copy-start.35
  1140.7 176.3 %reduce-scatter.35.cloned.1.call-start = ((), (), s32[]{:S(2)}) async-start(), calls=%async_computation.36 | async-start | bytes 5308416 | tf_op jit(solution)/shard_map/reduce_scatter | solution.py:466
  1151.8 4.4 copy-start.28
  1151.8 224.7 %all-reduce.15.cloned.1.call-start = ((), (), s32[]{:S(2)}) async-start(), calls=%async_computation.37 | async-start | bytes 2359296
  1156.1 5.0 copy-start.30
  1156.1 260.5 %reduce-scatter.31.cloned.1.call-start = ((), (), s32[]{:S(2)}) async-start(), calls=%async_computation.34 | async-start | bytes 1327104 | tf_op jit(solution)/shard_map/reduce_scatter | solution.py:460
  1161.1 296.4 %reduce-scatter.29.cloned.1.call-start = ((), (), s32[]{:S(2)}) async-start(), calls=%async_computation.33 | async-start | bytes 1327104 | tf_op jit(solution)/shard_map/reduce_scatter | solution.py:454
  1166.0 371.6 %reduce-scatter.33.cloned.1.call-start = ((), (), s32[]{:S(2)}) async-start(), calls=%async_computation.35 | async-start | bytes 10616832 | tf_op jit(solution)/shard_map/reduce_scatter | solution.py:463
  1181.9 78.8 %copy-start.42 = (f32[1,1536]{1,0:T(1,128)S(1)}, f32[1,1536]{1,0:T(1,128)}, u32[]{:S(2)}) copy-start(f32[1,1536]{1,0:T(1,128)} %copy-done.41) | copy-start | bytes 18436
  1181.9 78.8 %copy-start.47 = (f32[1024]{0:T(1024)S(1)}, f32[1024]{0:T(1024)}, u32[]{:S(2)}) copy-start(f32[1024]{0:T(1024)} %copy-done.46) | copy-start | bytes 12292
  1181.9 78.8 %copy-start.49 = (f32[1024]{0:T(1024)S(1)}, f32[1024]{0:T(1024)}, u32[]{:S(2)}) copy-start(f32[1024]{0:T(1024)} %copy-done.48) | copy-start | bytes 12292
  1181.9 78.7 %copy-start.51 = (f32[1536]{0:T(1024)S(1)}, f32[1536]{0:T(1024)}, u32[]{:S(2)}) copy-start(f32[1536]{0:T(1024)} %param.33) | copy-start | bytes 18436
  1181.9 395.5 %reduce-scatter.27.cloned.1.call-start = ((), (), s32[]{:S(2)}) async-start(), calls=%async_computation.32 | async-start | bytes 1327104 | tf_op jit(solution)/shard_map/reduce_scatter | solution.py:451
  1187.8 433.7 %reduce-scatter.23.cloned.1.call-start = ((), (), s32[]{:S(2)}) async-start(), calls=%async_computation.30 | async-start | bytes 884736 | tf_op jit(solution)/shard_map/reduce_scatter | solution.py:445
  1260.6 6.3 copy-start.4
  1267.0 9.0 copy-start.62
  1267.0 10.4 copy-start.32
  1267.0 10.4 copy-start.34
  1267.0 10.4 copy-start.36
  1267.0 10.4 copy-start.65
  1273.1 2.9 copy-start.5
  1277.1 391.4 %reduce-scatter.25.cloned.1.call-start = ((), (), s32[]{:S(2)}) async-start(), calls=%async_computation.31 | async-start | bytes 3981312 | tf_op jit(solution)/shard_map/reduce_scatter | solution.py:448
  1289.8 251.7 %copy-start.13 = (bf16[256,1,1536]{2,0,1:T(8,128)(2,1)S(1)}, bf16[256,1,1536]{2,0,1:T(8,128)(2,1)}, u32[]{:S(2)}) copy-start(bf16[256,1,1536]{2,0,1:T(8,128)(2,1)} %reduce-scatter.21.cloned.1.call-done) | copy-start | bytes 2359300
  (42 other events, 52.8 us)
Sparse Core Ops, SparseCore 0:
  9.9 36.4 all-gather.12
  48.3 24.0 all-gather.14
  94.4 110.3 reduce-scatter.12
  207.1 24.9 all-gather.20
  233.8 24.0 all-gather.18
  259.9 63.0 all-gather.16
  324.9 23.1 all-gather.22
  353.3 59.6 reduce-scatter.14
  415.4 59.4 all-gather.26
  476.9 63.0 all-gather.24
  541.5 62.1 all-gather.30
  605.5 38.0 all-gather.28
  671.7 59.6 reduce-scatter.18
  733.6 60.2 reduce-scatter.16
  798.2 63.6 all-gather.32
  895.0 58.7 reduce-scatter.20
  959.1 63.6 all-gather.34
  1140.9 119.7 all-reduce.12
  1264.1 52.9 reduce-scatter.34
  1320.4 56.0 all-reduce.14
  1379.8 36.7 reduce-scatter.30
  1420.7 36.7 reduce-scatter.28
  1461.0 76.5 reduce-scatter.32
  1540.7 36.6 reduce-scatter.26
  1581.5 34.8 reduce-scatter.22
  1620.1 48.3 reduce-scatter.24
where the time goes:
time: 1690 us; the launch traced here: 1680 us
  waiting for transfers between devices  1190 us (70%)
  matrix products  213 us (13%)
  local copies, waits for them, and re-layouts  112 us (7%)
  other arithmetic  95.8 us (6%)
  blocking collectives  42.4 us (3%)
  between operations  17.4 us (1%)
    reduce_scatter x1, waiting for transfers between devices, per_device(): lax.psum_scatter(jnp.swapaxes(jnp.dot(segment, self_out_full, preferred_e...  108 us
    reduce_scatter x1, waiting for transfers between devices, per_device(): lax.psum_scatter(gate_up_grad.astype(jnp.bfloat16), 'dp', scatter_dimensi...  78.5 us
    psum x1, waiting for transfers between devices, per_device(): lax.psum(grad_normed_part.astype(jnp.bfloat16), 'mp').astype(jnp.float32)  72.8 us
    all_gather x1, waiting for transfers between devices, per_device(): lax.all_gather(normed_three.astype(jnp.bfloat16), 'mp', axis=1, tiled=True)  65.1 us
    all_gather x1, waiting for transfers between devices, per_device(): lax.all_gather(normed_two.astype(jnp.bfloat16), 'mp', axis=1, tiled=True)  65.1 us
    all_gather x1, waiting for transfers between devices, per_device(): grad_rows_two = lax.all_gather(grad_residual_two, 'mp', axis=1, tiled=True)  63.7 us
    all_gather x1, waiting for transfers between devices, per_device(): grad_rows_one = lax.all_gather(grad_residual_one, 'mp', axis=1, tiled=True)  63.7 us
    unnamed x27, waiting for transfers between devices  61.4 us
  transfers between devices with their start and end apart: 26, of which 24 were waited for; matrix products, arithmetic and copies ran while one was open for 12% of the time, Pallas kernels for 0%

commit v1 on v0

--- a/solution.py
+++ b/solution.py
@@ -1,8 +1,11 @@
+import functools
 import math
 
 import jax
 import jax.numpy as jnp
 from jax import lax
+from jax.experimental import pallas as pl
+from jax.experimental.pallas import tpu as pltpu
 from jax.sharding import PartitionSpec as P
 
 HD = 64
@@ -148,7 +151,7 @@
     return lax.map(one_item, (queries, key_rows, value_rows, bias_rows, log_totals, grad_out))
 
 
-def per_device(
+def per_device_general(
     latents,
     prompt_tokens,
     prompt_lengths,
@@ -509,6 +512,608 @@
     )
 
 
+AXES = ("dp", "mp")
+BF = jnp.bfloat16
+F32 = jnp.float32
+
+
+def flat_permutation(places):
+    pairs = []
+    for d in range(8):
+        for z in range(4):
+            target = places(d >> 1, d & 1, z & 1, z >> 1)
+            if target is not None:
+                s, c, zz, p = target
+                pairs.append(((2 * s + c) * 4 + 2 * p + zz, (2 * (d >> 1) + (d & 1)) * 4 + z))
+    return [(source, target) for target, source in pairs]
+
+
+SWAP_CORE = flat_permutation(lambda s, c, zz, p: (s, 1 - c, zz, p))
+SWAP_Z = flat_permutation(lambda s, c, zz, p: (s, c, 1 - zz, p))
+SWAP_PAIR = flat_permutation(lambda s, c, zz, p: (s, c, zz, 1 - p))
+SWAP_X = flat_permutation(lambda s, c, zz, p: (s ^ 1, c, zz, p))
+SWAP_Y = flat_permutation(lambda s, c, zz, p: (s ^ 2, c, zz, p))
+ROUTE_A = flat_permutation(lambda s, c, zz, p: (s, p, zz, c))
+ROUTE_B = flat_permutation(lambda s, c, zz, p: (s, p, zz, 1 - c))
+RETURN_B = flat_permutation(lambda s, c, zz, p: (s, 1 - p, zz, c))
+OWNER_TO_PARTNER = flat_permutation(lambda s, c, zz, p: (s, 1 - c, zz, p) if c == p else None)
+PARTNER_TO_OWNER = flat_permutation(lambda s, c, zz, p: (s, 1 - c, zz, p) if c != p else None)
+OWNER_TO_PAIR = flat_permutation(lambda s, c, zz, p: (s, c, zz, 1 - p) if c == p else None)
+OWNER_Z = flat_permutation(lambda s, c, zz, p: (s, c, 1 - zz, p) if c == p else None)
+PARTNER_Z = flat_permutation(lambda s, c, zz, p: (s, c, 1 - zz, p) if c != p else None)
+
+
+def move(values, pairs):
+    return lax.ppermute(values, AXES, pairs)
+
+
+def xor_blocks(values, axis, count, index):
+    blocks = jnp.split(values, count, axis=axis)
+    bit = 1
+    while bit < count:
+        flip = (index & bit) != 0
+        blocks = [jnp.where(flip, blocks[j ^ bit], blocks[j]) for j in range(count)]
+        bit *= 2
+    return jnp.concatenate(blocks, axis=axis)
+
+
+def attention_forward_kernel(head_size, query_block, turned, *refs):
+    if turned:
+        q_in, k_in, v_in, cos_ref, low_ref, high_ref, q_ref, k_ref, v_ref, o_ref, log_ref = refs
+    else:
+        q_in, k_in, v_in, bias_ref, o_ref, log_ref = refs
+    scale = head_size ** (-0.5)
+    length = q_in.shape[0]
+    if turned:
+        half = head_size // 4
+        width = q_in.shape[1]
+
+        def turn(source, target):
+            @pl.loop(0, length // query_block)
+            def _(step):
+                rows = pl.ds(pl.multiple_of(step * query_block, query_block), query_block)
+                values = source[rows, :]
+                target[rows, :] = (
+                    values * cos_ref[rows, :]
+                    + pltpu.roll(values, width - half, 1) * low_ref[rows, :]
+                    + pltpu.roll(values, half, 1) * high_ref[rows, :]
+                ).astype(BF)
+
+        turn(q_in, q_ref)
+        turn(k_in, k_ref)
+        v_ref[...] = v_in[...].astype(BF)
+        queries, keys, values = q_ref, k_ref, v_ref
+    else:
+        queries, keys, values = q_in, k_in, v_in
+    key_rows = keys[...]
+    values_turned = values[...].astype(F32).T.astype(BF)
+    lane = lax.broadcasted_iota(jnp.int32, (query_block, q_in.shape[1]), 1)
+
+    @pl.loop(0, length // query_block)
+    def _(step):
+        rows = pl.ds(pl.multiple_of(step * query_block, query_block), query_block)
+        block = queries[rows, :]
+        parts, logs = [], []
+        for head in range(2):
+            mine = (lane >= head * head_size) & (lane < (head + 1) * head_size)
+            masked = jnp.where(mine, block, jnp.zeros_like(block))
+            scores = lax.dot_general(
+                key_rows, masked, (((1,), (1,)), ((), ())), preferred_element_type=F32
+            )
+            scores = scores * scale
+            if not turned:
+                scores = scores + bias_ref[...]
+            top = jnp.max(scores, axis=0, keepdims=True)
+            expos = jnp.exp(scores - top)
+            total = jnp.sum(expos, axis=0, keepdims=True)
+            mixed = lax.dot_general(
+                values_turned[head * head_size : (head + 1) * head_size, :],
+                expos.astype(BF),
+                (((1,), (0,)), ((), ())),
+                preferred_element_type=F32,
+            )
+            parts.append(mixed * (1.0 / total))
+            logs.append(top + jnp.log(total))
+        o_ref[rows, :] = jnp.concatenate(parts, axis=0).T.astype(BF)
+        log_ref[0, :, rows] = jnp.concatenate(logs, axis=0)
+
+
+def attention_backward_kernel(head_size, query_block, turned, *refs):
+    if turned:
+        q_ref, k_ref, v_ref, d_ref, log_ref, cos_ref, low_ref, high_ref, g_ref, dk_acc, dv_acc = refs
+    else:
+        q_ref, k_ref, v_ref, d_ref, log_ref, bias_ref, dq_ref, g_ref, dk_acc, dv_acc = refs
+    scale = head_size ** (-0.5)
+    length, width = q_ref.shape
+    key_count = k_ref.shape[0]
+    here = pl.program_id(0)
+    half = head_size // 4
+    key_rows = k_ref[...]
+    value_rows = v_ref[...]
+    keys_turned = key_rows.astype(F32).T.astype(BF)
+    lane = lax.broadcasted_iota(jnp.int32, (query_block, width), 1)
+    dk_acc[...] = jnp.zeros_like(dk_acc)
+    dv_acc[...] = jnp.zeros_like(dv_acc)
+
+    def back_turn(values, rows):
+        return (
+            values * cos_ref[rows, :]
+            - pltpu.roll(values, width - half, 1) * low_ref[rows, :]
+            - pltpu.roll(values, half, 1) * high_ref[rows, :]
+        )
+
+    @pl.loop(0, length // query_block)
+    def _(step):
+        rows = pl.ds(pl.multiple_of(step * query_block, query_block), query_block)
+        block = q_ref[rows, :]
+        grads = d_ref[rows, :]
+        parts = []
+        for head in range(2):
+            mine = (lane >= head * head_size) & (lane < (head + 1) * head_size)
+            q_mine = jnp.where(mine, block, jnp.zeros_like(block))
+            d_mine = jnp.where(mine, grads, jnp.zeros_like(grads))
+            scores = lax.dot_general(
+                key_rows, q_mine, (((1,), (1,)), ((), ())), preferred_element_type=F32
+            )
+            scores = scores * scale
+            if not turned:
+                scores = scores + bias_ref[...]
+            probs = jnp.exp(scores - log_ref[0, head : head + 1, rows])
+            grad_probs = lax.dot_general(
+                value_rows, d_mine, (((1,), (1,)), ((), ())), preferred_element_type=F32
+            )
+            delta = jnp.sum(probs * grad_probs, axis=0, keepdims=True)
+            grad_scores = (probs * (grad_probs - delta)).astype(BF)
+            dv_acc[...] += jnp.dot(probs.astype(BF), d_mine, preferred_element_type=F32)
+            dk_acc[...] += jnp.dot(grad_scores, q_mine, preferred_element_type=F32)
+            parts.append(
+                jnp.dot(
+                    keys_turned[head * head_size : (head + 1) * head_size, :],
+                    grad_scores,
+                    preferred_element_type=F32,
+                )
+            )
+        grad_query = jnp.concatenate(parts, axis=0).T * scale
+        if turned:
+            columns = pl.ds(pl.multiple_of(here * width, width), width)
+            g_ref[rows, columns] = back_turn(grad_query, rows).astype(BF)
+        else:
+            dq_ref[rows, :] = grad_query.astype(BF)
+
+    total_width = g_ref.shape[1] // (3 if turned else 2)
+    first = total_width if turned else 0
+    key_columns = pl.ds(pl.multiple_of(first + here * width, width), width)
+    value_columns = pl.ds(pl.multiple_of(first + total_width + here * width, width), width)
+    if turned:
+
+        @pl.loop(0, key_count // query_block)
+        def _(step):
+            rows = pl.ds(pl.multiple_of(step * query_block, query_block), query_block)
+            g_ref[rows, key_columns] = back_turn(dk_acc[rows, :] * scale, rows).astype(BF)
+            g_ref[rows, value_columns] = dv_acc[rows, :].astype(BF)
+    else:
+        g_ref[:, key_columns] = (dk_acc[...] * scale).astype(BF)
+        g_ref[:, value_columns] = dv_acc[...].astype(BF)
+
+
+def self_attention(projected, tables):
+    length, total = projected.shape
+    pairs = total // 3 // 128
+    block = lambda shift: pl.BlockSpec((length, 128), lambda i: (0, i + shift))
+    fixed = pl.BlockSpec((length, 128), lambda i: (0, 0))
+    wide = jax.ShapeDtypeStruct((length, total // 3), BF)
+    return pl.pallas_call(
+        functools.partial(attention_forward_kernel, HD, 256, True),
+        grid=(pairs,),
+        in_specs=[block(0), block(pairs), block(2 * pairs), fixed, fixed, fixed],
+        out_specs=[block(0)] * 4 + [pl.BlockSpec((1, 2, length), lambda i: (i, 0, 0))],
+        out_shape=[wide] * 4 + [jax.ShapeDtypeStruct((pairs, 2, length), F32)],
+        cost_estimate=pl.CostEstimate(
+            flops=4 * length * length * total // 3,
+            transcendentals=length * length * total // 192,
+            bytes_accessed=length * total * 8,
+        ),
+        name="self_attention",
+    )(projected, projected, projected, *tables)
+
+
+def self_attention_back(queries, keys, values, grads, logs, tables):
+    length, total = queries.shape
+    pairs = total // 128
+    block = pl.BlockSpec((length, 128), lambda i: (0, i))
+    fixed = pl.BlockSpec((length, 128), lambda i: (0, 0))
+    return pl.pallas_call(
+        functools.partial(attention_backward_kernel, HD, 256, True),
+        grid=(pairs,),
+        in_specs=[block] * 4 + [pl.BlockSpec((1, 2, length), lambda i: (i, 0, 0))] + [fixed] * 3,
+        out_specs=pl.BlockSpec((length, 3 * total), lambda i: (0, 0)),
+        out_shape=jax.ShapeDtypeStruct((length, 3 * total), BF),
+        scratch_shapes=[pltpu.VMEM((length, 128), F32)] * 2,
+        cost_estimate=pl.CostEstimate(
+            flops=10 * length * length * total,
+            transcendentals=length * length * total // 64,
+            bytes_accessed=length * total * 16,
+        ),
+        name="self_attention_back",
+    )(queries, keys, values, grads, logs, *tables)
+
+
+def cross_attention(queries, context, bias):
+    length, total = queries.shape
+    slots = context.shape[0]
+    pairs = total // 128
+    block = pl.BlockSpec((length, 128), lambda i: (0, i))
+    key_block = lambda shift: pl.BlockSpec((slots, 128), lambda i: (0, i + shift))
+    return pl.pallas_call(
+        functools.partial(attention_forward_kernel, HD, 512, False),
+        grid=(pairs,),
+        in_specs=[block, key_block(0), key_block(pairs), pl.BlockSpec((slots, 1), lambda i: (0, 0))],
+        out_specs=[block, pl.BlockSpec((1, 2, length), lambda i: (i, 0, 0))],
+        out_shape=[
+            jax.ShapeDtypeStruct((length, total), BF),
+            jax.ShapeDtypeStruct((pairs, 2, length), F32),
+        ],
+        cost_estimate=pl.CostEstimate(
+            flops=4 * length * slots * total,
+            transcendentals=length * slots * total // 64,
+            bytes_accessed=length * total * 4,
+        ),
+        name="cross_attention",
+    )(queries, context, context, bias)
+
+
+def cross_attention_back(queries, context, bias, grads, logs):
+    length, total = queries.shape
+    slots = context.shape[0]
+    pairs = total // 128
+    block = pl.BlockSpec((length, 128), lambda i: (0, i))
+    key_block = lambda shift: pl.BlockSpec((slots, 128), lambda i: (0, i + shift))
+    return pl.pallas_call(
+        functools.partial(attention_backward_kernel, HD, 512, False),
+        grid=(pairs,),
+        in_specs=[
+            block,
+            key_block(0),
+            key_block(pairs),
+            block,
+            pl.BlockSpec((1, 2, length), lambda i: (i, 0, 0)),
+            pl.BlockSpec((slots, 1), lambda i: (0, 0)),
+        ],
+        out_specs=[block, pl.BlockSpec((slots, 2 * total), lambda i: (0, 0))],
+        out_shape=[
+            jax.ShapeDtypeStruct((length, total), BF),
+            jax.ShapeDtypeStruct((slots, 2 * total), BF),
+        ],
+        scratch_shapes=[pltpu.VMEM((slots, 128), F32)] * 2,
+        cost_estimate=pl.CostEstimate(
+            flops=10 * length * slots * total,
+            transcendentals=length * slots * total // 64,
+            bytes_accessed=length * total * 8,
+        ),
+        name="cross_attention_back",
+    )(queries, context, context, grads, logs, bias)
+
+
+def dot_nn(left, right):
+    return lax.dot_general(left, right, (((1,), (0,)), ((), ())), preferred_element_type=F32)
+
+
+def dot_nt(left, right):
+    return lax.dot_general(left, right, (((1,), (1,)), ((), ())), preferred_element_type=F32)
+
+
+def dot_tn(left, right):
+    return lax.dot_general(left, right, (((0,), (0,)), ((), ())), preferred_element_type=F32)
+
+
+def group_scatter(partial):
+    rows = partial.shape[0] // 4
+    other = move(partial[2 * rows :], SWAP_CORE)
+    half = partial[: 2 * rows].astype(F32) + other.astype(F32)
+    far = move(half[rows:].astype(BF), SWAP_Z)
+    return half[:rows] + far.astype(F32)
+
+
+def group_gather(part):
+    far = move(part, SWAP_Z)
+    half = jnp.concatenate([part, far], axis=0)
+    return jnp.concatenate([half, move(half, SWAP_CORE)], axis=0)
+
+
+def weight_spread(part, pair):
+    one = move(part, ROUTE_A)
+    two = move(part, ROUTE_B)
+    first = jnp.where(pair == 0, one, two)
+    second = jnp.where(pair == 0, two, one)
+    return jnp.concatenate([first, second], axis=0)
+
+
+def plane_gather(mine):
+    rows = mine.shape[0] // 2
+    from_x = move(mine, SWAP_X)
+    from_y = move(mine, SWAP_Y)
+    diag_one = move(from_x[:rows], SWAP_Y)
+    diag_two = move(from_y[rows:], SWAP_X)
+    return jnp.concatenate([mine, from_x, from_y, diag_one, diag_two], axis=0)
+
+
+def plane_scatter(grad, pair):
+    rows = grad.shape[0] // 8
+    blocks = [grad[2 * rows * j : 2 * rows * (j + 1)] for j in range(4)]
+    got_x = move(blocks[3][:rows], SWAP_X)
+    got_y = move(blocks[3][rows:], SWAP_Y)
+    to_x = jnp.concatenate(
+        [
+            blocks[1][:rows],
+            (blocks[1][rows:].astype(F32) + got_y.astype(F32)).astype(BF),
+        ],
+        axis=0,
+    )
+    to_y = jnp.concatenate(
+        [
+            (blocks[2][:rows].astype(F32) + got_x.astype(F32)).astype(BF),
+            blocks[2][rows:],
+        ],
+        axis=0,
+    )
+    total = (
+        blocks[0].astype(F32)
+        + move(to_x, SWAP_X).astype(F32)
+        + move(to_y, SWAP_Y).astype(F32)
+    ).astype(BF)
+    first, second = total[:rows], total[rows:]
+    one = move(jnp.where(pair == 0, first, second), ROUTE_A)
+    two = move(jnp.where(pair == 0, second, first), RETURN_B)
+    return one.astype(F32) + two.astype(F32)
+
+
+def per_device_paired(
+    latents,
+    prompt_tokens,
+    prompt_lengths,
+    timesteps,
+    time_weight,
+    self_gain,
+    self_bias,
+    qkv_weight,
+    self_out_weight,
+    cross_gain,
+    cross_bias,
+    cross_query_weight,
+    context_weight,
+    cross_out_weight,
+    feed_gain,
+    feed_bias,
+    gate_up_weight,
+    down_weight,
+    down_bias,
+    cotangent,
+):
+    d = lax.axis_index("dp")
+    z = lax.axis_index("mp")
+    core, column, pair = d & 1, d >> 1, z >> 1
+    shard = (z & 1) + 2 * core
+    owner = core == pair
+    width = latents.shape[-1]
+    length = latents.shape[1] + 1
+    rows = length // 4
+    part_rows = qkv_weight.shape[0]
+
+    qkv_part = qkv_weight.reshape(part_rows, -1)
+    side_part = jnp.concatenate(
+        [
+            self_out_weight.T,
+            cross_query_weight,
+            cross_out_weight.T,
+            context_weight.reshape(part_rows, -1),
+        ],
+        axis=1,
+    )
+    gate_up_part = gate_up_weight.reshape(part_rows, -1)
+    down_part = down_weight.T
+    qkv_own = weight_spread(qkv_part, pair)
+    side_own = weight_spread(side_part, pair)
+    gate_up_own = weight_spread(gate_up_part, pair)
+    down_own = weight_spread(down_part, pair)
+    qkv_full = plane_gather(qkv_own)
+    side_full = plane_gather(side_own)
+    gate_up_full = plane_gather(gate_up_own)
+    down_full = plane_gather(down_own)
+    n = cross_query_weight.shape[1]
+    self_out_full = side_full[:, :n]
+    cross_query_full = side_full[:, n : 2 * n]
+    cross_out_full = side_full[:, 2 * n : 3 * n]
+    context_full = side_full[:, 3 * n :].reshape(context_weight.shape[0] * 8, -1)
+
+    def of_item(values):
+        return jnp.where(owner, values, move(values, OWNER_TO_PARTNER))
+
+    item_latents = of_item(latents[0])
+    item_prompt = xor_blocks(of_item(prompt_tokens[0]), 1, 4, column)
+    scalars = of_item(jnp.stack([prompt_lengths[0], timesteps[0]]))
+    item_length, item_step = scalars[0], scalars[1]
+    time_full = time_weight
+    for pairs in (SWAP_CORE, SWAP_X, SWAP_Y):
+        time_full = jnp.concatenate([time_full, move(time_full, pairs)], axis=0)
+    feature_width = time_full.shape[0]
+    item_features = time_features(item_step[None], feature_width).astype(BF)
+    token_row = dot_nn(xor_blocks(item_features, 1, 8, d), time_full)
+    residual_in = jnp.concatenate([token_row, item_latents.astype(F32)], axis=0)
+    residual_in = xor_blocks(xor_blocks(residual_in, 0, 4, shard), 1, 4, column)
+    residual_mine = residual_in[:rows]
+    vectors = xor_blocks(
+        jnp.stack([self_gain, self_bias, cross_gain, cross_bias, feed_gain, feed_bias, down_bias]),
+        1,
+        4,
+        column,
+    )
+    gain_one, bias_one, gain_two, bias_two, gain_three, bias_three, bias_down = [
+        vectors[j] for j in range(7)
+    ]
+    cot_mine = xor_blocks(move(cotangent[0], ROUTE_A), 1, 4, column)
+    cot_all = group_gather(cot_mine)
+
+    normed_one, _, _ = layer_norm(residual_in, gain_one, bias_one)
+    normed_one = normed_one.astype(BF)
+    projected = dot_nn(normed_one, qkv_full)
+    cosine, sine = rope_tables(length, HD)
+    quarter = HD // 4
+    straight = jnp.ones((length, HD // 2), F32)
+    blank = jnp.zeros((length, quarter), F32)
+    cosine, sine = cosine[:, 0], sine[:, 0]
+    tables = jnp.stack(
+        [
+            jnp.tile(jnp.concatenate([cosine, straight], axis=1), (1, 2)),
+            jnp.tile(
+                jnp.concatenate([-sine[:, :quarter], blank, blank, blank], axis=1), (1, 2)
+            ),
+            jnp.tile(
+                jnp.concatenate([blank, sine[:, quarter:], blank, blank], axis=1), (1, 2)
+            ),
+        ]
+    )
+    tables = xor_blocks(tables, 1, 4, shard)
+    tables = (tables[0], tables[1], tables[2])
+    queries, keys, values, attended, self_logs = self_attention(projected, tables)
+    residual_one = residual_mine + group_scatter(dot_nt(attended, self_out_full).astype(BF))
+    normed_two, scaled_two, inverse_two = layer_norm(residual_one, gain_two, bias_two)
+    normed_two_all = group_gather(normed_two.astype(BF))
+    cross_q = dot_nn(normed_two_all, cross_query_full).astype(BF)
+    context = dot_nn(item_prompt, context_full).astype(BF)
+    slots = prompt_tokens.shape[1]
+    mask = jnp.where(jnp.arange(slots, dtype=jnp.int32)[:, None] < item_length, 0.0, NEG)
+    mask = mask.astype(F32)
+    crossed, cross_logs = cross_attention(cross_q, context, mask)
+    residual_two = residual_one + group_scatter(dot_nt(crossed, cross_out_full).astype(BF))
+    normed_three, scaled_three, inverse_three = layer_norm(residual_two, gain_three, bias_three)
+    normed_three_all = group_gather(normed_three.astype(BF))
+    gate_up = dot_nn(normed_three_all, gate_up_full)
+    hidden_width = gate_up.shape[1] // 2
+    gate, up = gate_up[:, :hidden_width], gate_up[:, hidden_width:]
+    sigmoid_gate = jax.nn.sigmoid(gate)
+    hidden = (gate * sigmoid_gate * up).astype(BF)
+    feed = group_scatter(dot_nt(hidden, down_full).astype(BF))
+    output = xor_blocks((residual_two + feed + bias_down).astype(BF), 1, 4, column)
+    output = move(output, ROUTE_A)
+
+    grad_hidden = dot_nn(cot_all, down_full)
+    grad_up = grad_hidden * gate * sigmoid_gate
+    grad_gate = grad_hidden * up * sigmoid_gate * (1.0 + gate * (1.0 - sigmoid_gate))
+    grad_gate_up = jnp.concatenate([grad_gate.astype(BF), grad_up.astype(BF)], axis=1)
+    grad_normed_three = group_scatter(dot_nt(grad_gate_up, gate_up_full).astype(BF))
+    down_grad = plane_scatter(dot_tn(cot_all, hidden).astype(BF), pair)
+    gate_up_grad = plane_scatter(dot_tn(normed_three_all, grad_gate_up).astype(BF), pair)
+
+    def norm_back_rows(grad_normed, scaled, inverse, gain):
+        grads, gain_part, bias_part = norm_back(grad_normed[None], scaled[None], inverse[None], gain)
+        return grads[0], gain_part, bias_part
+
+    grad_norm, feed_gain_part, feed_bias_part = norm_back_rows(
+        grad_normed_three, scaled_three, inverse_three, gain_three
+    )
+    cot_rows = cot_mine.astype(F32)
+    down_bias_part = jnp.sum(cot_rows, axis=0)
+    grad_two = (cot_rows + grad_norm).astype(BF)
+    grad_two_all = group_gather(grad_two)
+    grad_crossed = dot_nn(grad_two_all, cross_out_full).astype(BF)
+    grad_cross_q, grad_context = cross_attention_back(
+        cross_q, context, mask, grad_crossed, cross_logs
+    )
+    grad_normed_two = group_scatter(dot_nt(grad_cross_q, cross_query_full).astype(BF))
+    context_grad = dot_tn(item_prompt, grad_context).astype(BF).reshape(side_full.shape[0], -1)
+    cross_out_grad = dot_tn(grad_two_all, crossed).astype(BF)
+    cross_query_grad = dot_tn(normed_two_all, grad_cross_q).astype(BF)
+    cross_grads = plane_scatter(
+        jnp.concatenate([cross_query_grad, cross_out_grad, context_grad], axis=1), pair
+    )
+    grad_norm, cross_gain_part, cross_bias_part = norm_back_rows(
+        grad_normed_two, scaled_two, inverse_two, gain_two
+    )
+    grad_one = (grad_two.astype(F32) + grad_norm).astype(BF)
+    grad_one_all = group_gather(grad_one)
+    grad_attended = dot_nn(grad_one_all, self_out_full).astype(BF)
+    grad_projected = self_attention_back(
+        queries, keys, values, grad_attended, self_logs, tables
+    )
+    grad_normed_one = group_scatter(dot_nt(grad_projected, qkv_full).astype(BF))
+    self_out_grad = plane_scatter(dot_tn(grad_one_all, attended).astype(BF), pair)
+    qkv_grad = plane_scatter(dot_tn(normed_one, grad_projected).astype(BF), pair)
+    _, scaled_one, inverse_one = layer_norm(residual_mine, gain_one, bias_one)
+    grad_norm, self_gain_part, self_bias_part = norm_back_rows(
+        grad_normed_one, scaled_one, inverse_one, gain_one
+    )
+    grad_in = (grad_one.astype(F32) + grad_norm).astype(BF)
+    grad_in = xor_blocks(grad_in, 1, 4, column)
+
+    from_partner = move(grad_in, PARTNER_TO_OWNER)
+    first = jnp.where(core == 0, grad_in, from_partner)
+    second = jnp.where(core == 0, from_partner, grad_in)
+    half = jnp.concatenate([first, second], axis=0)
+    far_half = move(half, OWNER_TO_PAIR)
+    own_z = move(half, OWNER_Z)
+    here = jnp.where(owner, half, far_half)
+    there = jnp.where(owner, own_z, move(far_half, PARTNER_Z))
+    even = jnp.where((z & 1) == 0, here, there)
+    odd = jnp.where((z & 1) == 0, there, here)
+    whole = jnp.concatenate([even[:rows], odd[:rows], even[rows:], odd[rows:]], axis=0)
+    latents_grad = whole[1:]
+
+    token_rows = whole[:1]
+    steps = timesteps
+    for pairs in (SWAP_CORE, SWAP_X, SWAP_Y):
+        token_rows = jnp.concatenate([token_rows, move(token_rows, pairs)], axis=0)
+        steps = jnp.concatenate([steps, move(steps, pairs)], axis=0)
+    all_features = time_features(steps, feature_width).astype(BF)
+    my_features = jnp.zeros((8, feature_width // 8), F32)
+    for j in range(8):
+        piece = all_features[:, j * (feature_width // 8) : (j + 1) * (feature_width // 8)]
+        my_features = my_features + jnp.where(d == j, piece.astype(F32), 0.0)
+    time_grad = lax.dot_general(
+        my_features.astype(BF), token_rows, (((0,), (0,)), ((), ())), preferred_element_type=F32
+    )
+
+    parts = jnp.stack(
+        [
+            self_gain_part,
+            self_bias_part,
+            cross_gain_part,
+            cross_bias_part,
+            feed_gain_part,
+            feed_bias_part,
+            down_bias_part,
+        ]
+    )
+    block = width // 4
+    got = move(jnp.concatenate([parts[:, block : 2 * block], parts[:, 3 * block :]], axis=1), SWAP_X)
+    keep = jnp.concatenate([parts[:, :block], parts[:, 2 * block : 3 * block]], axis=1) + got
+    mine = keep[:, :block] + move(keep[:, block:], SWAP_Y)
+    low_half, high_half = mine[:, : block // 2], mine[:, block // 2 :]
+    other = move(jnp.where(core == 0, high_half, low_half), SWAP_CORE)
+    mine = jnp.where(core == 0, low_half, high_half) + other
+    mine = mine + move(mine, SWAP_Z)
+    mine = mine + move(mine, SWAP_PAIR)
+
+    return (
+        output[None],
+        latents_grad[None],
+        time_grad,
+        mine[0],
+        mine[1],
+        qkv_grad.reshape(qkv_weight.shape),
+        self_out_grad.T,
+        mine[2],
+        mine[3],
+        cross_grads[:, :n],
+        cross_grads[:, 2 * n :].reshape(context_weight.shape),
+        cross_grads[:, n : 2 * n].T,
+        mine[4],
+        mine[5],
+        gate_up_grad.reshape(gate_up_weight.shape),
+        down_grad.T,
+        mine[6],
+    )
+
+
 def solution(mesh):
     placed = (
         P("dp", None, None),
@@ -532,8 +1137,9 @@
         P(),
         P("dp", "mp", None),
     )
+    paired = mesh.shape["dp"] == 8 and mesh.shape["mp"] == 4
     return jax.shard_map(
-        per_device,
+        per_device_paired if paired else per_device_general,
         mesh=mesh,
         in_specs=placed,
         out_specs=(

time: 1690 us -> 938 us (0.56)
  waiting for transfers between devices: 1190 us -> 371 us
  starting transfers between devices: 1.53 us -> 188 us
  matrix products: 213 us -> 142 us
  Pallas kernels: 0 us -> 70.5 us
  local copies, waits for them, and re-layouts: 112 us -> 60.5 us
  blocking collectives: 42.4 us -> 0 us
    reduce_scatter x12 -> x0, waiting for transfers between devices: 596 us -> none  [the longest x1 108 us: per_device(): lax.psum_scatter(jnp.swapaxes(jnp.dot(segment, self_out_full, preferred_e...]
    all_gather x12 -> x0, waiting for transfers between devices: 464 us -> none  [the longest x1 65.1 us: per_device(): lax.all_gather(normed_three.astype(jnp.bfloat16), 'mp', axis=1, tiled=True)]
    ppermute x0 -> x99, waiting for transfers between devices: none -> 371 us  [move(): return lax.ppermute(values, AXES, pairs)]
    ppermute x0 -> x99, starting transfers between devices: none -> 188 us  [move(): return lax.ppermute(values, AXES, pairs)]
    psum x1 -> x0, waiting for transfers between devices: 72.8 us -> none  [per_device(): lax.psum(grad_normed_part.astype(jnp.bfloat16), 'mp').astype(jnp.float32)]
    pallas_call x0 -> x4, Pallas kernels: none -> 70.5 us  [the longest x1 30.5 us: self_attention_back(): pl.pallas_call(functools.partial(attention_backward_kernel, HD, 256, True...]
    dot_general x49 -> x22, matrix products: 213 us -> 142 us  [the longest x8 57.3 us: dot_nn(): lax.dot_general(left, right, (((1,), (0,)), ((), ())), preferred_element_...]
    unnamed x27 -> x0, waiting for transfers between devices: 61.4 us -> none
  transfers between devices with their start and end apart: 26 -> 99, of which waited for: 24 -> 40; matrix products, arithmetic and copies ran while one was open for 12% -> 24% of each run, Pallas kernels for 0% -> 5%
where the time goes in v1:
time: 938 us; the launch traced here: 926 us
  waiting for transfers between devices  371 us (40%)
  starting transfers between devices  188 us (20%)
  matrix products  142 us (15%)
  other arithmetic  89 us (9%)
  Pallas kernels  70.5 us (8%)
  local copies, waits for them, and re-layouts  60.5 us (6%)
    ppermute x99, waiting for transfers between devices, move(): return lax.ppermute(values, AXES, pairs)  371 us
    ppermute x99, starting transfers between devices, move(): return lax.ppermute(values, AXES, pairs)  188 us
    dot_general x8, matrix products, dot_nn(): lax.dot_general(left, right, (((1,), (0,)), ((), ())), preferred_element_...  57.3 us
    dot_general x7, matrix products, dot_tn(): lax.dot_general(left, right, (((0,), (0,)), ((), ())), preferred_element_...  44.5 us
    dot_general x6, matrix products, dot_nt(): lax.dot_general(left, right, (((1,), (1,)), ((), ())), preferred_element_...  39.6 us
    pallas_call x1, Pallas kernels, self_attention_back(): pl.pallas_call(functools.partial(attention_backward_kernel, HD, 256, True...  30.5 us
    unnamed x216, local copies, waits for them, and re-layouts  26.6 us
    pallas_call x1, Pallas kernels, self_attention(): pl.pallas_call(functools.partial(attention_forward_kernel, HD, 256, True)...  25.9 us
  transfers between devices with their start and end apart: 99, of which 40 were waited for; matrix products, arithmetic and copies ran while one was open for 24% of the time, Pallas kernels for 5%

profile of v1, /device:TPU:1, one launch (start us, length us, event | category | flops | bytes accessed | tf_op | source)
XLA Modules:
  0.0 926.3 jit_solution(3807937863500885726)
XLA Ops:
  2.6 5.6 collective-permute-start.5
  11.2 4.8 collective-permute-start.11
  28.6 5.1 collective-permute-done.3
  33.7 4.4 collective-permute-start.32
  40.2 8.7 collective-permute-done.6
  54.9 10.5 %collective-permute-done.11 = bf16[192,1536]{1,0:T(8,128)(2,1)} collective-permute-done((bf16[192,1536]{1,0:T(8,128)(2,1)}, bf16[192,1536]{1,0:T(8,128)(2,1)}, u32[]{:S(2)}, u32[]{:S(2)}) %collective-permute-start.11) | collective-permute-done | bytes 589856 | tf_op jit(solution)/shard_map/ppermute | solution.py:547
  71.0 7.0 collective-permute-done.32
  92.2 7.8 collective-permute-done.8
  104.9 9.4 %collective-permute-done.13 = bf16[384,1536]{1,0:T(8,128)(2,1)} collective-permute-done((bf16[384,1536]{1,0:T(8,128)(2,1)}, bf16[384,1536]{1,0:T(8,128)(2,1)}, u32[]{:S(2)}, u32[]{:S(2)}) %collective-permute-start.13) | collective-permute-done | bytes 1179680 | tf_op jit(solution)/shard_map/ppermute | solution.py:547
  116.7 8.5 collective-permute-done.14
  144.3 3.7 pad_maximum_fusion.1
  148.8 6.5 fusion.87.refs_0_.refs_1_.refs_2_
  155.2 25.9 %self_attention.1 = (bf16[1024,384]{1,0:T(8,128)(2,1)}, bf16[1024,384]{1,0:T(8,128)(2,1)}, bf16[1024,384]{1,0:T(8,128)(2,1)}, bf16[1024,384]{1,0:T(8,128)(2,1)}, f32[3,2,1024]{2,1,0:T(2,128)}) custom-call(f32[1024,1152]{1,0:T(8,128)} %fusion.87.refs_0_.refs_1_.refs_2_, f32[1024,1152]{1,0:T(8,128)} %fusion.87.refs_0_.refs_1_.refs_2_, ...), custom_call_target="tpu_custom_call" | custom-call | flops 1610612736 | bytes 9437184 | tf_op jit(solution)/shard_map/self_attention/pallas_call | solution.py:705
  181.1 3.5 convolution_convert_fusion.6
  184.8 3.4 collective-permute-done.17
  188.8 7.2 collective-permute-start.18
  196.8 16.9 %collective-permute-done.18 = bf16[256,1536]{1,0:T(8,128)(2,1)S(1)} collective-permute-done((bf16[256,1536]{1,0:T(8,128)(2,1)S(1)}, bf16[256,1536]{1,0:T(8,128)(2,1)S(1)}, u32[]{:S(2)}, u32[]{:S(2)}) %collective-permute-start.18) | collective-permute-done | bytes 786464 | tf_op jit(solution)/shard_map/ppermute | solution.py:547
  217.0 17.1 %collective-permute-done.19 = bf16[256,1536]{1,0:T(8,128)(2,1)S(1)} collective-permute-done((bf16[256,1536]{1,0:T(8,128)(2,1)S(1)}, bf16[256,1536]{1,0:T(8,128)(2,1)S(1)}, u32[]{:S(2)}, u32[]{:S(2)}) %collective-permute-start.19) | collective-permute-done | bytes 786464 | tf_op jit(solution)/shard_map/ppermute | solution.py:547
  251.3 4.7 collective-permute-start.41
  260.9 3.4 reshape.341
  266.7 4.6 convolution_convert_fusion.14.refs_0_
  271.4 6.5 cross_attention.1
  277.8 3.3 convolution_convert_fusion.5
  281.3 6.7 collective-permute-start.22
  290.1 21.7 %collective-permute-done.41 = bf16[256,1536]{1,0:T(8,128)(2,1)} collective-permute-done((bf16[256,1536]{1,0:T(8,128)(2,1)}, bf16[256,1536]{1,0:T(8,128)(2,1)}, u32[]{:S(2)}, u32[]{:S(2)}) %collective-permute-start.41) | collective-permute-done | bytes 786464 | tf_op jit(solution)/shard_map/ppermute | solution.py:547
  322.7 11.8 %collective-permute-done.42 = bf16[256,1536]{1,0:T(8,128)(2,1)S(1)} collective-permute-done((bf16[256,1536]{1,0:T(8,128)(2,1)S(1)}, bf16[256,1536]{1,0:T(8,128)(2,1)S(1)}, u32[]{:S(2)}, u32[]{:S(2)}) %collective-permute-start.42) | collective-permute-done | bytes 786464 | tf_op jit(solution)/shard_map/ppermute | solution.py:547
  337.6 9.1 collective-permute-done.23
  350.0 40.1 %collective-permute-done.36 = bf16[192,1536]{1,0:T(8,128)(2,1)S(1)} collective-permute-done((bf16[192,1536]{1,0:T(8,128)(2,1)S(1)}, bf16[192,1536]{1,0:T(8,128)(2,1)S(1)}, u32[]{:S(2)}, u32[]{:S(2)}) %collective-permute-start.36) | collective-permute-done | bytes 589856 | tf_op jit(solution)/shard_map/ppermute | solution.py:547
  398.6 19.4 %collective-permute-done.30 = bf16[192,3072]{1,0:T(8,128)(2,1)S(1)} collective-permute-done((bf16[192,3072]{1,0:T(8,128)(2,1)S(1)}, bf16[192,3072]{1,0:T(8,128)(2,1)S(1)}, u32[]{:S(2)}, u32[]{:S(2)}) %collective-permute-start.30) | collective-permute-done | bytes 1179680 | tf_op jit(solution)/shard_map/ppermute | solution.py:547
  421.4 15.8 %fusion.15 = f32[1024,3072]{1,0:T(8,128)} fusion(bf16[1536,3072]{1,0:T(8,128)(2,1)} %constant_dynamic-update-slice_fusion.12, bf16[512,1536]{1,0:T(8,128)(2,1)S(1)} %collective-permute-done.25, bf16[256,1536]{1,0:T(8,128)(2,1)S(1)} %collective-permute-done.24, bf16[256,1536]{1,0:T(8,128)(2,1)S(1)} %add_convert_fusion.9), kind=kOutput, calls=%fused_computation.122 | convolution fusion | flops 9673113600 | bytes 25165824 | tf_op jit(solution)/shard_map/dot_general | solution.py:798
  437.2 17.7 %multiply_convert_fusion.1 = (bf16[1024,1536]{1,0:T(8,128)(2,1)S(1)}, bf16[1024,1536]{1,0:T(8,128)(2,1)}, bf16[1024,1536]{1,0:T(8,128)(2,1)}) fusion(f32[1024,3072]{1,0:T(8,128)} %fusion.15, bf16[1536,1536]{1,0:T(8,128)(2,1)} %constant_dynamic-update-slice_fusion.18, bf16[512,1536]{1,0:T(8,128)(2,1)} %collective-permute-done.43, ...), kind=kOutput, calls=%fused_computation.7 | convolution fusion | flops 4875878400 | bytes 29884416 | tf_op jit(solution)/shard_map/dot_general | solution.py:798
  454.9 12.6 %convolution_convert_fusion.1 = bf16[1536,1536]{1,0:T(8,128)(2,1)S(1)} fusion(bf16[1024,1536]{1,0:T(8,128)(2,1)} %get-tuple-element.132, bf16[512,1536]{1,0:T(8,128)(2,1)} %collective-permute-done.43, bf16[256,1536]{1,0:T(8,128)(2,1)S(1)} %copy-done.36, bf16[256,384]{1,0:T(8,128)(2,1)S(1)} %copy-done.29, bf16[256,384]{1,0:T(8,128)(2,1)S(1)} %copy-done.27, ...), kind=kOutput, calls=%fused_computation.1 | convolution fusion | flops 4853071872 | bytes 11010048 | tf_op jit(solution)/shard_map/dot_general | solution.py:806
  472.1 13.9 %fusion.1 = bf16[1024,1536]{1,0:T(8,128)(2,1)} fusion(bf16[1536,3072]{1,0:T(8,128)(2,1)} %constant_dynamic-update-slice_fusion.12, bf16[1024,1536]{1,0:T(8,128)(2,1)S(1)} %copy-done.93, bf16[1024,1536]{1,0:T(8,128)(2,1)S(1)} %get-tuple-element.130), kind=kOutput, calls=%fused_computation.19 | convolution fusion | flops 9677832192 | bytes 18874368 | tf_op jit(solution)/shard_map/dot_general | solution.py:802
  486.1 13.5 %convolution_convert_fusion = bf16[1536,3072]{1,0:T(8,128)(2,1)S(1)} fusion(bf16[1024,1536]{1,0:T(8,128)(2,1)} %get-tuple-element.131, bf16[1024,1536]{1,0:T(8,128)(2,1)} %copy-done.92, bf16[512,1536]{1,0:T(8,128)(2,1)} %copy-done.89, bf16[256,1536]{1,0:T(8,128)(2,1)} %copy-done.37, bf16[256,1536]{1,0:T(8,128)(2,1)S(1)} %add_convert_fusion.9), kind=kOutput, calls=%fused_computation | convolution fusion | flops 9690415104 | bytes 18874368 | tf_op jit(solution)/shard_map/dot_general | solution.py:806
  501.4 8.4 convolution_convert_fusion.4
  518.2 7.3 collective-permute-done.87
  534.6 16.8 %collective-permute-done.94 = bf16[384,1536]{1,0:T(8,128)(2,1)} collective-permute-done((bf16[384,1536]{1,0:T(8,128)(2,1)}, bf16[384,1536]{1,0:T(8,128)(2,1)}, u32[]{:S(2)}, u32[]{:S(2)}) %collective-permute-start.94) | collective-permute-done | bytes 1179680 | tf_op jit(solution)/shard_map/ppermute | solution.py:547
  553.6 11.4 %collective-permute-start.97 = (bf16[192,1536]{1,0:T(8,128)(2,1)S(1)}, bf16[192,1536]{1,0:T(8,128)(2,1)S(1)}, u32[]{:S(2)}, u32[]{:S(2)}) collective-permute-start(bf16[192,1536]{1,0:T(8,128)(2,1)S(1)} %get-tuple-element.188), channel_id=1, source_target_pairs={{0,0},{1,1},{2,4},{3,5},{4,2},{5,3},{6,6},{7,7},{8,8},{9,9},{10,12... | collective-permute-start | bytes 1769480 | tf_op jit(solution)/shard_map/ppermute | solution.py:547
  575.1 12.0 %collective-permute-start.40 = (bf16[256,1536]{1,0:T(8,128)(2,1)S(1)}, bf16[256,1536]{1,0:T(8,128)(2,1)S(1)}, u32[]{:S(2)}, u32[]{:S(2)}) collective-permute-start(bf16[256,1536]{1,0:T(8,128)(2,1)S(1)} %pad_maximum_fusion.43), channel_id=1, source_target_pairs={{0,0},{1,1},{2,4},{3,5},{4,2},{5,3},{6,6},{7,7},{8,8},{9,9},{10,12... | collective-permute-start | bytes 2359304 | tf_op jit(solution)/shard_map/ppermute | solution.py:547
  588.4 8.1 collective-permute-done.46
  596.6 12.9 %collective-permute-start.47 = (bf16[512,1536]{1,0:T(8,128)(2,1)S(1)}, bf16[512,1536]{1,0:T(8,128)(2,1)S(1)}, u32[]{:S(2)}, u32[]{:S(2)}) collective-permute-start(bf16[512,1536]{1,0:T(8,128)(2,1)S(1)} %pad_maximum_fusion.25), channel_id=1, source_target_pairs={{0,4},{1,5},{2,6},{3,7},{4,0},{5,1},{6,2},{7,3},{8,12},{9,13},{10,... | collective-permute-start | bytes 4718600 | tf_op jit(solution)/shard_map/ppermute | solution.py:547
  610.4 3.6 add_convert_fusion.1
  615.6 8.7 collective-permute-start.91
  624.3 8.5 collective-permute-start.92
  632.8 4.5 convolution_convert_fusion.13.refs_3_
  637.3 7.7 cross_attention_back.1
  645.0 3.3 convolution_convert_fusion.3
  658.8 3.7 convolution_convert_fusion.8
  669.2 4.7 collective-permute-done.81
  676.4 17.0 %collective-permute-done.49 = bf16[256,1536]{1,0:T(8,128)(2,1)S(1)} collective-permute-done((bf16[256,1536]{1,0:T(8,128)(2,1)S(1)}, bf16[256,1536]{1,0:T(8,128)(2,1)S(1)}, u32[]{:S(2)}, u32[]{:S(2)}) %collective-permute-start.49) | collective-permute-done | bytes 786464 | tf_op jit(solution)/shard_map/ppermute | solution.py:547
  698.7 3.5 collective-permute-start.85
  704.7 18.7 %collective-permute-done.50 = bf16[256,1536]{1,0:T(8,128)(2,1)S(1)} collective-permute-done((bf16[256,1536]{1,0:T(8,128)(2,1)S(1)}, bf16[256,1536]{1,0:T(8,128)(2,1)S(1)}, u32[]{:S(2)}, u32[]{:S(2)}) %collective-permute-start.50) | collective-permute-done | bytes 786464 | tf_op jit(solution)/shard_map/ppermute | solution.py:547
  734.2 3.4 convolution_convert_fusion.10
  739.1 4.4 convolution_convert_fusion.12.refs_3_
  743.5 30.5 %self_attention_back.1 = bf16[1024,1152]{1,0:T(8,128)(2,1)} custom-call(bf16[1024,384]{1,0:T(8,128)(2,1)} %get-tuple-element.30.refs_0_, bf16[1024,384]{1,0:T(8,128)(2,1)} %get-tuple-element.31.refs_1_, bf16[1024,384]{1,0:T(8,128)(2,1)} %get-tuple-element.32.refs_2_, bf16[1024,384]{1,0:T(8,128)(2,1)} %convolution_convert_fusion.12.refs_3_, ...), custom_call_target="tpu_custom_call" | custom-call | flops 4026531840 | bytes 6291456 | tf_op jit(solution)/shard_map/self_attention_back/pallas_call | solution.py:725
  774.0 7.1 convolution_convert_fusion.7
  783.0 6.5 convolution_convert_fusion.2
  794.6 6.1 collective-permute-done.69
  801.6 9.4 %collective-permute-done.53 = bf16[256,1536]{1,0:T(8,128)(2,1)S(1)} collective-permute-done((bf16[256,1536]{1,0:T(8,128)(2,1)S(1)}, bf16[256,1536]{1,0:T(8,128)(2,1)S(1)}, u32[]{:S(2)}, u32[]{:S(2)}) %collective-permute-start.53) | collective-permute-done | bytes 786464 | tf_op jit(solution)/shard_map/ppermute | solution.py:547
  813.7 4.9 collective-permute-start.54
  829.6 11.5 %collective-permute-done.64 = f32[7,768]{1,0:T(8,128)S(1)} collective-permute-done((f32[7,768]{1,0:T(8,128)S(1)}, f32[7,768]{1,0:T(8,128)S(1)}, u32[]{:S(2)}, u32[]{:S(2)}) %collective-permute-start.64) | collective-permute-done | bytes 21536 | tf_op jit(solution)/shard_map/ppermute | solution.py:547
  846.5 22.2 %collective-permute-done.55 = bf16[512,1536]{1,0:T(8,128)(2,1)S(1)} collective-permute-done((bf16[512,1536]{1,0:T(8,128)(2,1)S(1)}, bf16[512,1536]{1,0:T(8,128)(2,1)S(1)}, u32[]{:S(2)}, u32[]{:S(2)}) %collective-permute-start.55) | collective-permute-done | bytes 1572896 | tf_op jit(solution)/shard_map/ppermute | solution.py:547
  870.7 6.4 collective-permute-start.73
  878.1 33.9 %collective-permute-done.67 = f32[7,192]{1,0:T(8,128)S(1)} collective-permute-done((f32[7,192]{1,0:T(8,128)S(1)}, f32[7,192]{1,0:T(8,128)S(1)}, u32[]{:S(2)}, u32[]{:S(2)}) %collective-permute-start.67) | collective-permute-done | bytes 5408 | tf_op jit(solution)/shard_map/ppermute | solution.py:547
  (585 shorter events, 253.1 us)
Async XLA Ops:
  2.6 37.6 %collective-permute-start.5 = (bf16[192,1152]{1,0:T(8,128)(2,1)}, bf16[192,1152]{1,0:T(8,128)(2,1)}, u32[]{:S(2)}, u32[]{:S(2)}) collective-permute-start(bf16[192,1152]{1,0:T(8,128)(2,1)} %bitcast.32), channel_id=1, source_target_pairs={{0,0},{1,1},{2,4},{3,5},{4,2},{5,3},{6,6},{7,7},{8,8},{9,9},{10,12... | collective-permute-start | bytes 1327112 | tf_op jit(solution)/shard_map/ppermute | solution.py:547
  8.2 40.6 %collective-permute-start.6 = (bf16[192,1152]{1,0:T(8,128)(2,1)}, bf16[192,1152]{1,0:T(8,128)(2,1)}, u32[]{:S(2)}, u32[]{:S(2)}) collective-permute-start(bf16[192,1152]{1,0:T(8,128)(2,1)} %bitcast.32), channel_id=1, source_target_pairs={{0,2},{1,3},{2,6},{3,7},{4,0},{5,1},{6,4},{7,5},{8,10},{9,11},{10,... | collective-permute-start | bytes 1327112 | tf_op jit(solution)/shard_map/ppermute | solution.py:547
  11.2 54.3 %collective-permute-start.11 = (bf16[192,1536]{1,0:T(8,128)(2,1)}, bf16[192,1536]{1,0:T(8,128)(2,1)}, u32[]{:S(2)}, u32[]{:S(2)}) collective-permute-start(bf16[192,1536]{1,0:T(8,128)(2,1)} %pad_maximum_fusion.46), channel_id=1, source_target_pairs={{0,0},{1,1},{2,4},{3,5},{4,2},{5,3},{6,6},{7,7},{8,8},{9,9},{10,12... | collective-permute-start | bytes 1769480 | tf_op jit(solution)/shard_map/ppermute | solution.py:547
  15.9 51.9 %collective-permute-start.12 = (bf16[192,1536]{1,0:T(8,128)(2,1)}, bf16[192,1536]{1,0:T(8,128)(2,1)}, u32[]{:S(2)}, u32[]{:S(2)}) collective-permute-start(bf16[192,1536]{1,0:T(8,128)(2,1)} %pad_maximum_fusion.46), channel_id=1, source_target_pairs={{0,2},{1,3},{2,6},{3,7},{4,0},{5,1},{6,4},{7,5},{8,10},{9,11},{10,... | collective-permute-start | bytes 1769480 | tf_op jit(solution)/shard_map/ppermute | solution.py:547
  33.7 44.3 %collective-permute-start.32 = (bf16[192,1536]{1,0:T(8,128)(2,1)}, bf16[192,1536]{1,0:T(8,128)(2,1)S(1)}, u32[]{:S(2)}, u32[]{:S(2)}) collective-permute-start(bf16[192,1536]{1,0:T(8,128)(2,1)} %bitcast.93), channel_id=1, source_target_pairs={{0,0},{1,1},{2,4},{3,5},{4,2},{5,3},{6,6},{7,7},{8,8},{9,9},{10,12... | collective-permute-start | bytes 1769480 | tf_op jit(solution)/shard_map/ppermute | solution.py:547
  40.2 39.1 %collective-permute-start.33 = (bf16[192,1536]{1,0:T(8,128)(2,1)}, bf16[192,1536]{1,0:T(8,128)(2,1)S(1)}, u32[]{:S(2)}, u32[]{:S(2)}) collective-permute-start(bf16[192,1536]{1,0:T(8,128)(2,1)} %bitcast.94), channel_id=1, source_target_pairs={{0,2},{1,3},{2,6},{3,7},{4,0},{5,1},{6,4},{7,5},{8,10},{9,11},{10,... | collective-permute-start | bytes 1769480 | tf_op jit(solution)/shard_map/ppermute | solution.py:547
  48.8 89.3 %collective-permute-start = (bf16[1023,1536]{1,0:T(8,128)(2,1)S(1)}, bf16[1023,1536]{1,0:T(8,128)(2,1)}, u32[]{:S(2)}, u32[]{:S(2)}) collective-permute-start(bf16[1023,1536]{1,0:T(8,128)(2,1)S(1)} %bitcast.75), channel_id=1, source_target_pairs={{0,4},{1,5},{6,2},{7,3},{8,12},{9,13},{14,10},{15,11},{16,20},{17,... | collective-permute-start | bytes 9427976 | tf_op jit(solution)/shard_map/ppermute | solution.py:547
  67.8 22.4 %collective-permute-start.7 = (bf16[384,1152]{1,0:T(8,128)(2,1)}, bf16[384,1152]{1,0:T(8,128)(2,1)}, u32[]{:S(2)}, u32[]{:S(2)}) collective-permute-start(bf16[384,1152]{1,0:T(8,128)(2,1)} %pad_maximum_fusion.40), channel_id=1, source_target_pairs={{0,8},{1,9},{2,10},{3,11},{4,12},{5,13},{6,14},{7,15},{8,0},{9,1},... | collective-permute-start | bytes 2654216 | tf_op jit(solution)/shard_map/ppermute | solution.py:547
  78.0 22.0 %collective-permute-start.8 = (bf16[384,1152]{1,0:T(8,128)(2,1)}, bf16[384,1152]{1,0:T(8,128)(2,1)}, u32[]{:S(2)}, u32[]{:S(2)}) collective-permute-start(bf16[384,1152]{1,0:T(8,128)(2,1)} %pad_maximum_fusion.40), channel_id=1, source_target_pairs={{0,16},{1,17},{2,18},{3,19},{4,20},{5,21},{6,22},{7,23},{8,24},{9,... | collective-permute-start | bytes 2654216 | tf_op jit(solution)/shard_map/ppermute | solution.py:547
  83.9 30.5 %collective-permute-start.13 = (bf16[384,1536]{1,0:T(8,128)(2,1)}, bf16[384,1536]{1,0:T(8,128)(2,1)}, u32[]{:S(2)}, u32[]{:S(2)}) collective-permute-start(bf16[384,1536]{1,0:T(8,128)(2,1)} %pad_maximum_fusion.36), channel_id=1, source_target_pairs={{0,8},{1,9},{2,10},{3,11},{4,12},{5,13},{6,14},{7,15},{8,0},{9,1},... | collective-permute-start | bytes 3538952 | tf_op jit(solution)/shard_map/ppermute | solution.py:547
  85.1 40.1 %collective-permute-start.14 = (bf16[384,1536]{1,0:T(8,128)(2,1)}, bf16[384,1536]{1,0:T(8,128)(2,1)}, u32[]{:S(2)}, u32[]{:S(2)}) collective-permute-start(bf16[384,1536]{1,0:T(8,128)(2,1)} %pad_maximum_fusion.36), channel_id=1, source_target_pairs={{0,16},{1,17},{2,18},{3,19},{4,20},{5,21},{6,22},{7,23},{8,24},{9,... | collective-permute-start | bytes 3538952 | tf_op jit(solution)/shard_map/ppermute | solution.py:547
  91.2 38.8 %collective-permute-start.9 = (bf16[192,1152]{1,0:T(8,128)(2,1)S(1)}, bf16[192,1152]{1,0:T(8,128)(2,1)S(1)}, u32[]{:S(2)}, u32[]{:S(2)}) collective-permute-start(bf16[192,1152]{1,0:T(8,128)(2,1)S(1)} %slice.581), channel_id=1, source_target_pairs={{0,16},{1,17},{2,18},{3,19},{4,20},{5,21},{6,22},{7,23},{8,24},{9,... | collective-permute-start | bytes 1327112 | tf_op jit(solution)/shard_map/ppermute | solution.py:547
  101.1 29.0 %collective-permute-start.10 = (bf16[192,1152]{1,0:T(8,128)(2,1)S(1)}, bf16[192,1152]{1,0:T(8,128)(2,1)S(1)}, u32[]{:S(2)}, u32[]{:S(2)}) collective-permute-start(bf16[192,1152]{1,0:T(8,128)(2,1)S(1)} %slice.582), channel_id=1, source_target_pairs={{0,8},{1,9},{2,10},{3,11},{4,12},{5,13},{6,14},{7,15},{8,0},{9,1},... | collective-permute-start | bytes 1327112 | tf_op jit(solution)/shard_map/ppermute | solution.py:547
  188.8 25.0 %collective-permute-start.18 = (bf16[256,1536]{1,0:T(8,128)(2,1)S(1)}, bf16[256,1536]{1,0:T(8,128)(2,1)S(1)}, u32[]{:S(2)}, u32[]{:S(2)}) collective-permute-start(bf16[256,1536]{1,0:T(8,128)(2,1)S(1)} %slice.848), channel_id=1, source_target_pairs={{0,1},{1,0},{2,3},{3,2},{4,5},{5,4},{6,7},{7,6},{8,9},{9,8},{10,11... | collective-permute-start | bytes 2359304 | tf_op jit(solution)/shard_map/ppermute | solution.py:547
  235.5 31.2 %collective-permute-start.20 = (bf16[512,1536]{1,0:T(8,128)(2,1)}, bf16[512,1536]{1,0:T(8,128)(2,1)}, u32[]{:S(2)}, u32[]{:S(2)}) collective-permute-start(bf16[512,1536]{1,0:T(8,128)(2,1)} %pad_maximum_fusion.22), channel_id=1, source_target_pairs={{0,4},{1,5},{2,6},{3,7},{4,0},{5,1},{6,2},{7,3},{8,12},{9,13},{10,... | collective-permute-start | bytes 4718600 | tf_op jit(solution)/shard_map/ppermute | solution.py:547
  238.2 76.6 %collective-permute-start.26 = (bf16[192,3072]{1,0:T(8,128)(2,1)}, bf16[192,3072]{1,0:T(8,128)(2,1)S(1)}, u32[]{:S(2)}, u32[]{:S(2)}) collective-permute-start(bf16[192,3072]{1,0:T(8,128)(2,1)} %bitcast.34), channel_id=1, source_target_pairs={{0,0},{1,1},{2,4},{3,5},{4,2},{5,3},{6,6},{7,7},{8,8},{9,9},{10,12... | collective-permute-start | bytes 3538952 | tf_op jit(solution)/shard_map/ppermute | solution.py:547
  240.6 74.3 %collective-permute-start.27 = (bf16[192,3072]{1,0:T(8,128)(2,1)}, bf16[192,3072]{1,0:T(8,128)(2,1)}, u32[]{:S(2)}, u32[]{:S(2)}) collective-permute-start(bf16[192,3072]{1,0:T(8,128)(2,1)} %bitcast.34), channel_id=1, source_target_pairs={{0,2},{1,3},{2,6},{3,7},{4,0},{5,1},{6,4},{7,5},{8,10},{9,11},{10,... | collective-permute-start | bytes 3538952 | tf_op jit(solution)/shard_map/ppermute | solution.py:547
  251.3 60.5 %collective-permute-start.41 = (bf16[256,1536]{1,0:T(8,128)(2,1)}, bf16[256,1536]{1,0:T(8,128)(2,1)}, u32[]{:S(2)}, u32[]{:S(2)}) collective-permute-start(bf16[256,1536]{1,0:T(8,128)(2,1)} %bitcast.92), channel_id=1, source_target_pairs={{0,0},{1,1},{2,4},{3,5},{4,2},{5,3},{6,6},{7,7},{8,8},{9,9},{10,12... | collective-permute-start | bytes 2359304 | tf_op jit(solution)/shard_map/ppermute | solution.py:547
  281.3 35.1 %collective-permute-start.22 = (bf16[512,1536]{1,0:T(8,128)(2,1)S(1)}, bf16[512,1536]{1,0:T(8,128)(2,1)S(1)}, u32[]{:S(2)}, u32[]{:S(2)}) collective-permute-start(bf16[512,1536]{1,0:T(8,128)(2,1)S(1)} %slice.597), channel_id=1, source_target_pairs={{0,4},{1,5},{2,6},{3,7},{4,0},{5,1},{6,2},{7,3},{8,12},{9,13},{10,... | collective-permute-start | bytes 4718600 | tf_op jit(solution)/shard_map/ppermute | solution.py:547
  288.8 46.4 %collective-permute-start.34 = (bf16[384,1536]{1,0:T(8,128)(2,1)S(1)}, bf16[384,1536]{1,0:T(8,128)(2,1)S(1)}, u32[]{:S(2)}, u32[]{:S(2)}) collective-permute-start(bf16[384,1536]{1,0:T(8,128)(2,1)S(1)} %pad_maximum_fusion.37), channel_id=1, source_target_pairs={{0,8},{1,9},{2,10},{3,11},{4,12},{5,13},{6,14},{7,15},{8,0},{9,1},... | collective-permute-start | bytes 3538952 | tf_op jit(solution)/shard_map/ppermute | solution.py:547
  311.8 24.4 %collective-permute-start.35 = (bf16[384,1536]{1,0:T(8,128)(2,1)S(1)}, bf16[384,1536]{1,0:T(8,128)(2,1)S(1)}, u32[]{:S(2)}, u32[]{:S(2)}) collective-permute-start(bf16[384,1536]{1,0:T(8,128)(2,1)S(1)} %pad_maximum_fusion.37), channel_id=1, source_target_pairs={{0,16},{1,17},{2,18},{3,19},{4,20},{5,21},{6,22},{7,23},{8,24},{9,... | collective-permute-start | bytes 3538952 | tf_op jit(solution)/shard_map/ppermute | solution.py:547
  317.0 29.7 %collective-permute-start.23 = (bf16[256,1536]{1,0:T(8,128)(2,1)S(1)}, bf16[256,1536]{1,0:T(8,128)(2,1)S(1)}, u32[]{:S(2)}, u32[]{:S(2)}) collective-permute-start(bf16[256,1536]{1,0:T(8,128)(2,1)S(1)} %slice.847), channel_id=1, source_target_pairs={{0,1},{1,0},{2,3},{3,2},{4,5},{5,4},{6,7},{7,6},{8,9},{9,8},{10,11... | collective-permute-start | bytes 2359304 | tf_op jit(solution)/shard_map/ppermute | solution.py:547
  321.5 69.4 %collective-permute-start.28 = (bf16[384,3072]{1,0:T(8,128)(2,1)S(1)}, bf16[384,3072]{1,0:T(8,128)(2,1)S(1)}, u32[]{:S(2)}, u32[]{:S(2)}) collective-permute-start(bf16[384,3072]{1,0:T(8,128)(2,1)S(1)} %pad_maximum_fusion.16), channel_id=1, source_target_pairs={{0,8},{1,9},{2,10},{3,11},{4,12},{5,13},{6,14},{7,15},{8,0},{9,1},... | collective-permute-start | bytes 7077896 | tf_op jit(solution)/shard_map/ppermute | solution.py:547
  334.5 58.3 %collective-permute-start.29 = (bf16[384,3072]{1,0:T(8,128)(2,1)S(1)}, bf16[384,3072]{1,0:T(8,128)(2,1)S(1)}, u32[]{:S(2)}, u32[]{:S(2)}) collective-permute-start(bf16[384,3072]{1,0:T(8,128)(2,1)S(1)} %pad_maximum_fusion.16), channel_id=1, source_target_pairs={{0,16},{1,17},{2,18},{3,19},{4,20},{5,21},{6,22},{7,23},{8,24},{9,... | collective-permute-start | bytes 7077896 | tf_op jit(solution)/shard_map/ppermute | solution.py:547
  335.3 54.8 %collective-permute-start.36 = (bf16[192,1536]{1,0:T(8,128)(2,1)S(1)}, bf16[192,1536]{1,0:T(8,128)(2,1)S(1)}, u32[]{:S(2)}, u32[]{:S(2)}) collective-permute-start(bf16[192,1536]{1,0:T(8,128)(2,1)S(1)} %slice.604), channel_id=1, source_target_pairs={{0,16},{1,17},{2,18},{3,19},{4,20},{5,21},{6,22},{7,23},{8,24},{9,... | collective-permute-start | bytes 1769480 | tf_op jit(solution)/shard_map/ppermute | solution.py:547
  336.3 55.6 %collective-permute-start.37 = (bf16[192,1536]{1,0:T(8,128)(2,1)S(1)}, bf16[192,1536]{1,0:T(8,128)(2,1)S(1)}, u32[]{:S(2)}, u32[]{:S(2)}) collective-permute-start(bf16[192,1536]{1,0:T(8,128)(2,1)S(1)} %slice.605), channel_id=1, source_target_pairs={{0,8},{1,9},{2,10},{3,11},{4,12},{5,13},{6,14},{7,15},{8,0},{9,1},... | collective-permute-start | bytes 1769480 | tf_op jit(solution)/shard_map/ppermute | solution.py:547
  347.7 46.6 %collective-permute-start.24 = (bf16[256,1536]{1,0:T(8,128)(2,1)S(1)}, bf16[256,1536]{1,0:T(8,128)(2,1)S(1)}, u32[]{:S(2)}, u32[]{:S(2)}) collective-permute-start(bf16[256,1536]{1,0:T(8,128)(2,1)S(1)} %add_convert_fusion.9), channel_id=1, source_target_pairs={{0,1},{1,0},{2,3},{3,2},{4,5},{5,4},{6,7},{7,6},{8,9},{9,8},{10,11... | collective-permute-start | bytes 2359304 | tf_op jit(solution)/shard_map/ppermute | solution.py:547
  390.0 47.2 %collective-permute-start.43 = (bf16[512,1536]{1,0:T(8,128)(2,1)S(1)}, bf16[512,1536]{1,0:T(8,128)(2,1)}, u32[]{:S(2)}, u32[]{:S(2)}) collective-permute-start(bf16[512,1536]{1,0:T(8,128)(2,1)S(1)} %pad_maximum_fusion.24), channel_id=1, source_target_pairs={{0,4},{1,5},{2,6},{3,7},{4,0},{5,1},{6,2},{7,3},{8,12},{9,13},{10,... | collective-permute-start | bytes 4718600 | tf_op jit(solution)/shard_map/ppermute | solution.py:547
  391.0 27.1 %collective-permute-start.30 = (bf16[192,3072]{1,0:T(8,128)(2,1)S(1)}, bf16[192,3072]{1,0:T(8,128)(2,1)S(1)}, u32[]{:S(2)}, u32[]{:S(2)}) collective-permute-start(bf16[192,3072]{1,0:T(8,128)(2,1)S(1)} %slice.600), channel_id=1, source_target_pairs={{0,16},{1,17},{2,18},{3,19},{4,20},{5,21},{6,22},{7,23},{8,24},{9,... | collective-permute-start | bytes 3538952 | tf_op jit(solution)/shard_map/ppermute | solution.py:547
  392.9 26.8 %collective-permute-start.31 = (bf16[192,3072]{1,0:T(8,128)(2,1)S(1)}, bf16[192,3072]{1,0:T(8,128)(2,1)S(1)}, u32[]{:S(2)}, u32[]{:S(2)}) collective-permute-start(bf16[192,3072]{1,0:T(8,128)(2,1)S(1)} %slice.601), channel_id=1, source_target_pairs={{0,8},{1,9},{2,10},{3,11},{4,12},{5,13},{6,14},{7,15},{8,0},{9,1},... | collective-permute-start | bytes 3538952 | tf_op jit(solution)/shard_map/ppermute | solution.py:547
  394.3 27.1 %collective-permute-start.25 = (bf16[512,1536]{1,0:T(8,128)(2,1)S(1)}, bf16[512,1536]{1,0:T(8,128)(2,1)S(1)}, u32[]{:S(2)}, u32[]{:S(2)}) collective-permute-start(bf16[512,1536]{1,0:T(8,128)(2,1)S(1)} %pad_maximum_fusion.23), channel_id=1, source_target_pairs={{0,4},{1,5},{2,6},{3,7},{4,0},{5,1},{6,2},{7,3},{8,12},{9,13},{10,... | collective-permute-start | bytes 4718600 | tf_op jit(solution)/shard_map/ppermute | solution.py:547
  470.5 41.9 %collective-permute-start.93 = (bf16[192,1536]{1,0:T(8,128)(2,1)}, bf16[192,1536]{1,0:T(8,128)(2,1)}, u32[]{:S(2)}, u32[]{:S(2)}) collective-permute-start(bf16[192,1536]{1,0:T(8,128)(2,1)} %get-tuple-element.156), channel_id=1, source_target_pairs={{0,16},{1,17},{2,18},{3,19},{4,20},{5,21},{6,22},{7,23},{8,24},{9,... | collective-permute-start | bytes 1769480 | tf_op jit(solution)/shard_map/ppermute | solution.py:547
  471.1 43.1 %collective-permute-start.95 = (bf16[192,1536]{1,0:T(8,128)(2,1)}, bf16[192,1536]{1,0:T(8,128)(2,1)}, u32[]{:S(2)}, u32[]{:S(2)}) collective-permute-start(bf16[192,1536]{1,0:T(8,128)(2,1)} %get-tuple-element.155), channel_id=1, source_target_pairs={{0,8},{1,9},{2,10},{3,11},{4,12},{5,13},{6,14},{7,15},{8,0},{9,1},... | collective-permute-start | bytes 1769480 | tf_op jit(solution)/shard_map/ppermute | solution.py:547
  499.9 25.6 %collective-permute-start.87 = (bf16[192,3072]{1,0:T(8,128)(2,1)S(1)}, bf16[192,3072]{1,0:T(8,128)(2,1)}, u32[]{:S(2)}, u32[]{:S(2)}) collective-permute-start(bf16[192,3072]{1,0:T(8,128)(2,1)S(1)} %get-tuple-element.136), channel_id=1, source_target_pairs={{0,16},{1,17},{2,18},{3,19},{4,20},{5,21},{6,22},{7,23},{8,24},{9,... | collective-permute-start | bytes 3538952 | tf_op jit(solution)/shard_map/ppermute | solution.py:547
  501.1 25.3 %collective-permute-start.89 = (bf16[192,3072]{1,0:T(8,128)(2,1)S(1)}, bf16[192,3072]{1,0:T(8,128)(2,1)}, u32[]{:S(2)}, u32[]{:S(2)}) collective-permute-start(bf16[192,3072]{1,0:T(8,128)(2,1)S(1)} %get-tuple-element.135), channel_id=1, source_target_pairs={{0,8},{1,9},{2,10},{3,11},{4,12},{5,13},{6,14},{7,15},{8,0},{9,1},... | collective-permute-start | bytes 3538952 | tf_op jit(solution)/shard_map/ppermute | solution.py:547
  516.9 34.5 %collective-permute-start.94 = (bf16[384,1536]{1,0:T(8,128)(2,1)}, bf16[384,1536]{1,0:T(8,128)(2,1)}, u32[]{:S(2)}, u32[]{:S(2)}) collective-permute-start(bf16[384,1536]{1,0:T(8,128)(2,1)} %pad_maximum_fusion.38), channel_id=1, source_target_pairs={{0,8},{1,9},{2,10},{3,11},{4,12},{5,13},{6,14},{7,15},{8,0},{9,1},... | collective-permute-start | bytes 3538952 | tf_op jit(solution)/shard_map/ppermute | solution.py:547
  525.5 25.9 %collective-permute-start.96 = (bf16[384,1536]{1,0:T(8,128)(2,1)S(1)}, bf16[384,1536]{1,0:T(8,128)(2,1)}, u32[]{:S(2)}, u32[]{:S(2)}) collective-permute-start(bf16[384,1536]{1,0:T(8,128)(2,1)S(1)} %pad_maximum_fusion.39), channel_id=1, source_target_pairs={{0,16},{1,17},{2,18},{3,19},{4,20},{5,21},{6,22},{7,23},{8,24},{9,... | collective-permute-start | bytes 3538952 | tf_op jit(solution)/shard_map/ppermute | solution.py:547
  529.1 80.4 %collective-permute-start.88 = (bf16[384,3072]{1,0:T(8,128)(2,1)S(1)}, bf16[384,3072]{1,0:T(8,128)(2,1)}, u32[]{:S(2)}, u32[]{:S(2)}) collective-permute-start(bf16[384,3072]{1,0:T(8,128)(2,1)S(1)} %pad_maximum_fusion.17), channel_id=1, source_target_pairs={{0,8},{1,9},{2,10},{3,11},{4,12},{5,13},{6,14},{7,15},{8,0},{9,1},... | collective-permute-start | bytes 7077896 | tf_op jit(solution)/shard_map/ppermute | solution.py:547
  529.5 80.8 %collective-permute-start.90 = (bf16[384,3072]{1,0:T(8,128)(2,1)S(1)}, bf16[384,3072]{1,0:T(8,128)(2,1)}, u32[]{:S(2)}, u32[]{:S(2)}) collective-permute-start(bf16[384,3072]{1,0:T(8,128)(2,1)S(1)} %pad_maximum_fusion.18), channel_id=1, source_target_pairs={{0,16},{1,17},{2,18},{3,19},{4,20},{5,21},{6,22},{7,23},{8,24},{9,... | collective-permute-start | bytes 7077896 | tf_op jit(solution)/shard_map/ppermute | solution.py:547
  532.6 36.5 %collective-permute-start.39 = (bf16[256,1536]{1,0:T(8,128)(2,1)S(1)}, bf16[256,1536]{1,0:T(8,128)(2,1)S(1)}, u32[]{:S(2)}, u32[]{:S(2)}) collective-permute-start(bf16[256,1536]{1,0:T(8,128)(2,1)S(1)} %slice.846), channel_id=1, source_target_pairs={{0,1},{1,0},{2,3},{3,2},{4,5},{5,4},{6,7},{7,6},{8,9},{9,8},{10,11... | collective-permute-start | bytes 2359304 | tf_op jit(solution)/shard_map/ppermute | solution.py:547
  565.0 22.2 %collective-permute-start.98 = (bf16[192,1536]{1,0:T(8,128)(2,1)S(1)}, bf16[192,1536]{1,0:T(8,128)(2,1)S(1)}, u32[]{:S(2)}, u32[]{:S(2)}) collective-permute-start(bf16[192,1536]{1,0:T(8,128)(2,1)S(1)} %get-tuple-element.189), channel_id=1, source_target_pairs={{0,4},{1,5},{2,0},{3,1},{4,6},{5,7},{6,2},{7,3},{8,12},{9,13},{10,... | collective-permute-start | bytes 1769480 | tf_op jit(solution)/shard_map/ppermute | solution.py:547
  570.2 26.3 %collective-permute-start.46 = (bf16[256,1536]{1,0:T(8,128)(2,1)S(1)}, bf16[256,1536]{1,0:T(8,128)(2,1)S(1)}, u32[]{:S(2)}, u32[]{:S(2)}) collective-permute-start(bf16[256,1536]{1,0:T(8,128)(2,1)S(1)} %get-tuple-element.179), channel_id=1, source_target_pairs={{0,1},{1,0},{2,3},{3,2},{4,5},{5,4},{6,7},{7,6},{8,9},{9,8},{10,11... | collective-permute-start | bytes 2359304 | tf_op jit(solution)/shard_map/ppermute | solution.py:547
  575.1 34.3 %collective-permute-start.40 = (bf16[256,1536]{1,0:T(8,128)(2,1)S(1)}, bf16[256,1536]{1,0:T(8,128)(2,1)S(1)}, u32[]{:S(2)}, u32[]{:S(2)}) collective-permute-start(bf16[256,1536]{1,0:T(8,128)(2,1)S(1)} %pad_maximum_fusion.43), channel_id=1, source_target_pairs={{0,0},{1,1},{2,4},{3,5},{4,2},{5,3},{6,6},{7,7},{8,8},{9,9},{10,12... | collective-permute-start | bytes 2359304 | tf_op jit(solution)/shard_map/ppermute | solution.py:547
  596.6 36.2 %collective-permute-start.47 = (bf16[512,1536]{1,0:T(8,128)(2,1)S(1)}, bf16[512,1536]{1,0:T(8,128)(2,1)S(1)}, u32[]{:S(2)}, u32[]{:S(2)}) collective-permute-start(bf16[512,1536]{1,0:T(8,128)(2,1)S(1)} %pad_maximum_fusion.25), channel_id=1, source_target_pairs={{0,4},{1,5},{2,6},{3,7},{4,0},{5,1},{6,2},{7,3},{8,12},{9,13},{10,... | collective-permute-start | bytes 4718600 | tf_op jit(solution)/shard_map/ppermute | solution.py:547
  615.6 110.3 %collective-permute-start.91 = (bf16[192,3072]{1,0:T(8,128)(2,1)}, bf16[192,3072]{1,0:T(8,128)(2,1)}, u32[]{:S(2)}, u32[]{:S(2)}) collective-permute-start(bf16[192,3072]{1,0:T(8,128)(2,1)} %get-tuple-element.171), channel_id=1, source_target_pairs={{0,0},{1,1},{2,4},{3,5},{4,2},{5,3},{6,6},{7,7},{8,8},{9,9},{10,12... | collective-permute-start | bytes 3538952 | tf_op jit(solution)/shard_map/ppermute | solution.py:547
  624.3 101.6 %collective-permute-start.92 = (bf16[192,3072]{1,0:T(8,128)(2,1)}, bf16[192,3072]{1,0:T(8,128)(2,1)}, u32[]{:S(2)}, u32[]{:S(2)}) collective-permute-start(bf16[192,3072]{1,0:T(8,128)(2,1)} %get-tuple-element.172), channel_id=1, source_target_pairs={{0,4},{1,5},{2,0},{3,1},{4,6},{5,7},{6,2},{7,3},{8,12},{9,13},{10,... | collective-permute-start | bytes 3538952 | tf_op jit(solution)/shard_map/ppermute | solution.py:547
  666.9 26.5 %collective-permute-start.49 = (bf16[256,1536]{1,0:T(8,128)(2,1)S(1)}, bf16[256,1536]{1,0:T(8,128)(2,1)S(1)}, u32[]{:S(2)}, u32[]{:S(2)}) collective-permute-start(bf16[256,1536]{1,0:T(8,128)(2,1)S(1)} %slice.844), channel_id=1, source_target_pairs={{0,1},{1,0},{2,3},{3,2},{4,5},{5,4},{6,7},{7,6},{8,9},{9,8},{10,11... | collective-permute-start | bytes 2359304 | tf_op jit(solution)/shard_map/ppermute | solution.py:547
  695.1 28.4 %collective-permute-start.50 = (bf16[256,1536]{1,0:T(8,128)(2,1)S(1)}, bf16[256,1536]{1,0:T(8,128)(2,1)S(1)}, u32[]{:S(2)}, u32[]{:S(2)}) collective-permute-start(bf16[256,1536]{1,0:T(8,128)(2,1)S(1)} %add_convert_fusion.8), channel_id=1, source_target_pairs={{0,1},{1,0},{2,3},{3,2},{4,5},{5,4},{6,7},{7,6},{8,9},{9,8},{10,11... | collective-permute-start | bytes 2359304 | tf_op jit(solution)/shard_map/ppermute | solution.py:547
  698.7 32.5 %collective-permute-start.85 = (bf16[192,1152]{1,0:T(8,128)(2,1)}, bf16[192,1152]{1,0:T(8,128)(2,1)}, u32[]{:S(2)}, u32[]{:S(2)}) collective-permute-start(bf16[192,1152]{1,0:T(8,128)(2,1)} %get-tuple-element.199), channel_id=1, source_target_pairs={{0,0},{1,1},{2,4},{3,5},{4,2},{5,3},{6,6},{7,7},{8,8},{9,9},{10,12... | collective-permute-start | bytes 1327112 | tf_op jit(solution)/shard_map/ppermute | solution.py:547
  702.1 29.0 %collective-permute-start.86 = (bf16[192,1152]{1,0:T(8,128)(2,1)}, bf16[192,1152]{1,0:T(8,128)(2,1)}, u32[]{:S(2)}, u32[]{:S(2)}) collective-permute-start(bf16[192,1152]{1,0:T(8,128)(2,1)} %get-tuple-element.200), channel_id=1, source_target_pairs={{0,4},{1,5},{2,0},{3,1},{4,6},{5,7},{6,2},{7,3},{8,12},{9,13},{10,... | collective-permute-start | bytes 1327112 | tf_op jit(solution)/shard_map/ppermute | solution.py:547
  737.7 53.6 %collective-permute-start.75 = (bf16[192,384]{1,0:T(8,128)(2,1)S(1)}, bf16[192,384]{1,0:T(8,128)(2,1)S(1)}, u32[]{:S(2)}, u32[]{:S(2)}) collective-permute-start(bf16[192,384]{1,0:T(8,128)(2,1)S(1)} %get-tuple-element.193), channel_id=1, source_target_pairs={{0,16},{1,17},{2,18},{3,19},{4,20},{5,21},{6,22},{7,23},{8,24},{9,... | collective-permute-start | bytes 442376 | tf_op jit(solution)/shard_map/ppermute | solution.py:547
  739.0 52.4 %collective-permute-start.77 = (bf16[192,384]{1,0:T(8,128)(2,1)S(1)}, bf16[192,384]{1,0:T(8,128)(2,1)}, u32[]{:S(2)}, u32[]{:S(2)}) collective-permute-start(bf16[192,384]{1,0:T(8,128)(2,1)S(1)} %get-tuple-element.192), channel_id=1, source_target_pairs={{0,8},{1,9},{2,10},{3,11},{4,12},{5,13},{6,14},{7,15},{8,0},{9,1},... | collective-permute-start | bytes 442376 | tf_op jit(solution)/shard_map/ppermute | solution.py:547
  793.2 28.6 %collective-permute-start.76 = (bf16[384,384]{1,0:T(8,128)(2,1)S(1)}, bf16[384,384]{1,0:T(8,128)(2,1)S(1)}, u32[]{:S(2)}, u32[]{:S(2)}) collective-permute-start(bf16[384,384]{1,0:T(8,128)(2,1)S(1)} %pad_maximum_fusion.50), channel_id=1, source_target_pairs={{0,8},{1,9},{2,10},{3,11},{4,12},{5,13},{6,14},{7,15},{8,0},{9,1},... | collective-permute-start | bytes 884744 | tf_op jit(solution)/shard_map/ppermute | solution.py:547
  794.1 27.8 %collective-permute-start.78 = (bf16[384,384]{1,0:T(8,128)(2,1)S(1)}, bf16[384,384]{1,0:T(8,128)(2,1)S(1)}, u32[]{:S(2)}, u32[]{:S(2)}) collective-permute-start(bf16[384,384]{1,0:T(8,128)(2,1)S(1)} %pad_maximum_fusion.51), channel_id=1, source_target_pairs={{0,16},{1,17},{2,18},{3,19},{4,20},{5,21},{6,22},{7,23},{8,24},{9,... | collective-permute-start | bytes 884744 | tf_op jit(solution)/shard_map/ppermute | solution.py:547
  819.6 21.8 %collective-permute-start.70 = (bf16[384,1152]{1,0:T(8,128)(2,1)}, bf16[384,1152]{1,0:T(8,128)(2,1)S(1)}, u32[]{:S(2)}, u32[]{:S(2)}) collective-permute-start(bf16[384,1152]{1,0:T(8,128)(2,1)} %pad_maximum_fusion.41), channel_id=1, source_target_pairs={{0,8},{1,9},{2,10},{3,11},{4,12},{5,13},{6,14},{7,15},{8,0},{9,1},... | collective-permute-start | bytes 2654216 | tf_op jit(solution)/shard_map/ppermute | solution.py:547
  823.6 45.1 %collective-permute-start.55 = (bf16[512,1536]{1,0:T(8,128)(2,1)S(1)}, bf16[512,1536]{1,0:T(8,128)(2,1)S(1)}, u32[]{:S(2)}, u32[]{:S(2)}) collective-permute-start(bf16[512,1536]{1,0:T(8,128)(2,1)S(1)} %pad_maximum_fusion.27), channel_id=1, source_target_pairs={{0,2},{1,3},{6,4},{7,5},{8,10},{9,11},{14,12},{15,13},{16,18},{17,... | collective-permute-start | bytes 4718600 | tf_op jit(solution)/shard_map/ppermute | solution.py:547
  826.4 44.3 %collective-permute-start.79 = (bf16[192,384]{1,0:T(8,128)(2,1)S(1)}, bf16[192,384]{1,0:T(8,128)(2,1)S(1)}, u32[]{:S(2)}, u32[]{:S(2)}) collective-permute-start(bf16[192,384]{1,0:T(8,128)(2,1)S(1)} %get-tuple-element.215), channel_id=1, source_target_pairs={{0,0},{1,1},{2,4},{3,5},{4,2},{5,3},{6,6},{7,7},{8,8},{9,9},{10,12... | collective-permute-start | bytes 442376 | tf_op jit(solution)/shard_map/ppermute | solution.py:547
  841.1 36.2 %collective-permute-start.80 = (bf16[192,384]{1,0:T(8,128)(2,1)S(1)}, bf16[192,384]{1,0:T(8,128)(2,1)S(1)}, u32[]{:S(2)}, u32[]{:S(2)}) collective-permute-start(bf16[192,384]{1,0:T(8,128)(2,1)S(1)} %get-tuple-element.216), channel_id=1, source_target_pairs={{0,4},{1,5},{2,0},{3,1},{4,6},{5,7},{6,2},{7,3},{8,12},{9,13},{10,... | collective-permute-start | bytes 442376 | tf_op jit(solution)/shard_map/ppermute | solution.py:547
  844.5 32.7 %collective-permute-start.66 = (f32[7,192]{1,0:T(8,128)S(1)}, f32[7,192]{1,0:T(8,128)S(1)}, u32[]{:S(2)}, u32[]{:S(2)}) collective-permute-start(f32[7,192]{1,0:T(8,128)S(1)} %slice_select_fusion.16), channel_id=1, source_target_pairs={{0,4},{1,5},{2,6},{3,7},{4,0},{5,1},{6,2},{7,3},{8,12},{9,13},{10,... | collective-permute-start | bytes 16136 | tf_op jit(solution)/shard_map/ppermute | solution.py:547
  845.7 70.2 %collective-permute-start.56 = (bf16[512,1536]{1,0:T(8,128)(2,1)S(1)}, bf16[512,1536]{1,0:T(8,128)(2,1)S(1)}, u32[]{:S(2)}, u32[]{:S(2)}) collective-permute-start(bf16[512,1536]{1,0:T(8,128)(2,1)S(1)} %pad_maximum_fusion.27), channel_id=1, source_target_pairs={{0,1},{1,0},{6,7},{7,6},{8,9},{9,8},{14,15},{15,14},{16,17},{17,16... | collective-permute-start | bytes 4718600 | tf_op jit(solution)/shard_map/ppermute | solution.py:547
  868.7 47.3 %collective-permute-start.57 = (bf16[512,1536]{1,0:T(8,128)(2,1)S(1)}, bf16[512,1536]{1,0:T(8,128)(2,1)S(1)}, u32[]{:S(2)}, u32[]{:S(2)}) collective-permute-start(bf16[512,1536]{1,0:T(8,128)(2,1)S(1)} %collective-permute-done.55), channel_id=1, source_target_pairs={{2,3},{3,2},{4,5},{5,4},{10,11},{11,10},{12,13},{13,12},{18,19},{1... | collective-permute-start | bytes 4718600 | tf_op jit(solution)/shard_map/ppermute | solution.py:547
  870.7 41.2 %collective-permute-start.73 = (bf16[192,1152]{1,0:T(8,128)(2,1)S(1)}, bf16[192,1152]{1,0:T(8,128)(2,1)S(1)}, u32[]{:S(2)}, u32[]{:S(2)}) collective-permute-start(bf16[192,1152]{1,0:T(8,128)(2,1)S(1)} %get-tuple-element.201), channel_id=1, source_target_pairs={{0,0},{1,1},{2,4},{3,5},{4,2},{5,3},{6,6},{7,7},{8,8},{9,9},{10,12... | collective-permute-start | bytes 1327112 | tf_op jit(solution)/shard_map/ppermute | solution.py:547
  877.1 34.8 %collective-permute-start.74 = (bf16[192,1152]{1,0:T(8,128)(2,1)S(1)}, bf16[192,1152]{1,0:T(8,128)(2,1)S(1)}, u32[]{:S(2)}, u32[]{:S(2)}) collective-permute-start(bf16[192,1152]{1,0:T(8,128)(2,1)S(1)} %get-tuple-element.202), channel_id=1, source_target_pairs={{0,4},{1,5},{2,0},{3,1},{4,6},{5,7},{6,2},{7,3},{8,12},{9,13},{10,... | collective-permute-start | bytes 1327112 | tf_op jit(solution)/shard_map/ppermute | solution.py:547
  877.3 34.7 %collective-permute-start.67 = (f32[7,192]{1,0:T(8,128)S(1)}, f32[7,192]{1,0:T(8,128)S(1)}, u32[]{:S(2)}, u32[]{:S(2)}) collective-permute-start(f32[7,192]{1,0:T(8,128)S(1)} %select_add_fusion), channel_id=1, source_target_pairs={{0,1},{1,0},{2,3},{3,2},{4,5},{5,4},{6,7},{7,6},{8,9},{9,8},{10,11... | collective-permute-start | bytes 16136 | tf_op jit(solution)/shard_map/ppermute | solution.py:547
  (136 other events, 2012.8 us)

commit v2 on v1

--- a/solution.py
+++ b/solution.py
@@ -557,37 +557,12 @@
     return jnp.concatenate(blocks, axis=axis)
 
 
-def attention_forward_kernel(head_size, query_block, turned, *refs):
-    if turned:
-        q_in, k_in, v_in, cos_ref, low_ref, high_ref, q_ref, k_ref, v_ref, o_ref, log_ref = refs
-    else:
-        q_in, k_in, v_in, bias_ref, o_ref, log_ref = refs
+def attend_pair(head_size, query_block, queries, keys, values, bias, o_ref, log_ref):
     scale = head_size ** (-0.5)
-    length = q_in.shape[0]
-    if turned:
-        half = head_size // 4
-        width = q_in.shape[1]
-
-        def turn(source, target):
-            @pl.loop(0, length // query_block)
-            def _(step):
-                rows = pl.ds(pl.multiple_of(step * query_block, query_block), query_block)
-                values = source[rows, :]
-                target[rows, :] = (
-                    values * cos_ref[rows, :]
-                    + pltpu.roll(values, width - half, 1) * low_ref[rows, :]
-                    + pltpu.roll(values, half, 1) * high_ref[rows, :]
-                ).astype(BF)
-
-        turn(q_in, q_ref)
-        turn(k_in, k_ref)
-        v_ref[...] = v_in[...].astype(BF)
-        queries, keys, values = q_ref, k_ref, v_ref
-    else:
-        queries, keys, values = q_in, k_in, v_in
+    length, width = queries.shape
     key_rows = keys[...]
     values_turned = values[...].astype(F32).T.astype(BF)
-    lane = lax.broadcasted_iota(jnp.int32, (query_block, q_in.shape[1]), 1)
+    lane = lax.broadcasted_iota(jnp.int32, (query_block, width), 1)
 
     @pl.loop(0, length // query_block)
     def _(step):
@@ -601,8 +576,8 @@
                 key_rows, masked, (((1,), (1,)), ((), ())), preferred_element_type=F32
             )
             scores = scores * scale
-            if not turned:
-                scores = scores + bias_ref[...]
+            if bias is not None:
+                scores = scores + bias[...]
             top = jnp.max(scores, axis=0, keepdims=True)
             expos = jnp.exp(scores - top)
             total = jnp.sum(expos, axis=0, keepdims=True)
@@ -618,9 +593,90 @@
         log_ref[0, :, rows] = jnp.concatenate(logs, axis=0)
 
 
-def attention_backward_kernel(head_size, query_block, turned, *refs):
+def cross_attention_kernel(q_ref, k_ref, v_ref, bias_ref, o_ref, log_ref):
+    attend_pair(HD, 512, q_ref, k_ref, v_ref, bias_ref, o_ref, log_ref)
+
+
+def self_attention_kernel(load, *refs):
+    res_ref, gain_ref, bias_ref, w_ref, cos_ref, low_ref, high_ref, part_ref = refs[:8]
+    n_ref, q_ref, k_ref, v_ref, o_ref, log_ref, own_ref = refs[8:15]
+    projected = refs[15]
+    here = pl.program_id(0)
+    place = Place()
+    carried = load.begin(place, [part_ref], [own_ref], refs[16:])
+    length, width = res_ref.shape
+    total = w_ref.shape[1]
+    block = 256
+
+    @pl.when(here == 0)
+    def _():
+        greet(load.peers(place, [place.core_peer]))
+        for each in carried:
+            each.start()
+
+        @pl.loop(0, length // 16)
+        def _(step):
+            rows = pl.ds(pl.multiple_of(step * 16, 16), 16)
+            values = res_ref[rows, :]
+            centered = values - jnp.mean(values, axis=-1, keepdims=True)
+            inverse = lax.rsqrt(jnp.mean(centered * centered, axis=-1, keepdims=True) + EPS)
+            n_ref[rows, :] = (centered * inverse * gain_ref[...] + bias_ref[...]).astype(BF)
+
+        for part in range(3):
+            columns = pl.ds(part * (total // 3), total // 3)
+
+            @pl.loop(0, length // block)
+            def _(step):
+                rows = pl.ds(pl.multiple_of(step * block, block), block)
+                projected[rows, columns] = jnp.dot(
+                    n_ref[rows, :], w_ref[:, columns], preferred_element_type=F32
+                )
+
+    half = HD // 4
+
+    def turn(first, target):
+        columns = pl.ds(pl.multiple_of(first + here * 128, 128), 128)
+
+        @pl.loop(0, length // block)
+        def _(step):
+            rows = pl.ds(pl.multiple_of(step * block, block), block)
+            values = projected[rows, columns]
+            target[rows, :] = (
+                values * cos_ref[rows, :]
+                + pltpu.roll(values, 128 - half, 1) * low_ref[rows, :]
+                + pltpu.roll(values, half, 1) * high_ref[rows, :]
+            ).astype(BF)
+
+    turn(0, q_ref)
+    turn(total // 3, k_ref)
+    v_ref[...] = projected[
+        :, pl.ds(pl.multiple_of(2 * (total // 3) + here * 128, 128), 128)
+    ].astype(BF)
+    attend_pair(HD, block, q_ref, k_ref, v_ref, None, o_ref, log_ref)
+
+    @pl.when(here == pl.num_programs(0) - 1)
+    def _():
+        for each in carried:
+            each.finish()
+
+
+def attention_backward_kernel(head_size, query_block, turned, load, *refs):
     if turned:
-        q_ref, k_ref, v_ref, d_ref, log_ref, cos_ref, low_ref, high_ref, g_ref, dk_acc, dv_acc = refs
+        refs = list(refs)
+        q_ref, k_ref, v_ref, d_ref, log_ref, cos_ref, low_ref, high_ref = refs[:8]
+        more = (len(load.operands), len(load.outs_like))
+        refs = refs[8:]
+        load_ins, g_ref, refs = refs[: more[0]], refs[more[0]], refs[more[0] + 1 :]
+        load_outs, refs = refs[: more[1]], refs[more[1] :]
+        dk_acc, dv_acc = refs[:2]
+        place = Place()
+        carried = load.begin(place, load_ins, load_outs, refs[2:])
+
+        @pl.when(pl.program_id(0) == 0)
+        def _():
+            greet(load.peers(place, [place.core_peer]))
+            for each in carried:
+                each.start()
     else:
         q_ref, k_ref, v_ref, d_ref, log_ref, bias_ref, dq_ref, g_ref, dk_acc, dv_acc = refs
     scale = head_size ** (-0.5)
@@ -691,51 +747,73 @@
             rows = pl.ds(pl.multiple_of(step * query_block, query_block), query_block)
             g_ref[rows, key_columns] = back_turn(dk_acc[rows, :] * scale, rows).astype(BF)
             g_ref[rows, value_columns] = dv_acc[rows, :].astype(BF)
+
+        @pl.when(here == pl.num_programs(0) - 1)
+        def _():
+            for each in carried:
+                each.finish()
     else:
         g_ref[:, key_columns] = (dk_acc[...] * scale).astype(BF)
         g_ref[:, value_columns] = dv_acc[...].astype(BF)
 
 
-def self_attention(projected, tables):
-    length, total = projected.shape
+def self_attention(place, residual, gain, bias, weight, tables, part):
+    length, width = residual.shape
+    total = weight.shape[1]
     pairs = total // 3 // 128
-    block = lambda shift: pl.BlockSpec((length, 128), lambda i: (0, i + shift))
+    load = Loads((Spread, part))
+    block = pl.BlockSpec((length, 128), lambda i: (0, i))
     fixed = pl.BlockSpec((length, 128), lambda i: (0, 0))
+    whole = pl.BlockSpec(memory_space=pltpu.VMEM)
     wide = jax.ShapeDtypeStruct((length, total // 3), BF)
     return pl.pallas_call(
-        functools.partial(attention_forward_kernel, HD, 256, True),
+        functools.partial(self_attention_kernel, load),
         grid=(pairs,),
-        in_specs=[block(0), block(pairs), block(2 * pairs), fixed, fixed, fixed],
-        out_specs=[block(0)] * 4 + [pl.BlockSpec((1, 2, length), lambda i: (i, 0, 0))],
-        out_shape=[wide] * 4 + [jax.ShapeDtypeStruct((pairs, 2, length), F32)],
+        in_specs=[whole] * 4 + [fixed] * 3 + [ANYWHERE],
+        out_specs=[pl.BlockSpec((length, width), lambda i: (0, 0))]
+        + [block] * 4
+        + [pl.BlockSpec((1, 2, length), lambda i: (i, 0, 0)), ANYWHERE],
+        out_shape=[jax.ShapeDtypeStruct((length, width), BF)]
+        + [wide] * 4
+        + [jax.ShapeDtypeStruct((pairs, 2, length), F32)]
+        + load.outs_like,
+        scratch_shapes=[pltpu.VMEM((length, total), F32)] + load.scratch,
+        compiler_params=pltpu.CompilerParams(
+            collective_id=place, has_side_effects=True, vmem_limit_bytes=60 * 2**20
+        ),
         cost_estimate=pl.CostEstimate(
-            flops=4 * length * length * total // 3,
+            flops=4 * length * length * total // 3 + 2 * length * width * total,
             transcendentals=length * length * total // 192,
-            bytes_accessed=length * total * 8,
+            bytes_accessed=100_000_000,
         ),
         name="self_attention",
-    )(projected, projected, projected, *tables)
-
-
-def self_attention_back(queries, keys, values, grads, logs, tables):
+    )(residual, gain[None], bias[None], weight, *tables, part)
+
+
+def self_attention_back(place, queries, keys, values, grads, logs, tables, load):
     length, total = queries.shape
     pairs = total // 128
     block = pl.BlockSpec((length, 128), lambda i: (0, i))
     fixed = pl.BlockSpec((length, 128), lambda i: (0, 0))
     return pl.pallas_call(
-        functools.partial(attention_backward_kernel, HD, 256, True),
+        functools.partial(attention_backward_kernel, HD, 256, True, load),
         grid=(pairs,),
-        in_specs=[block] * 4 + [pl.BlockSpec((1, 2, length), lambda i: (i, 0, 0))] + [fixed] * 3,
-        out_specs=pl.BlockSpec((length, 3 * total), lambda i: (0, 0)),
-        out_shape=jax.ShapeDtypeStruct((length, 3 * total), BF),
-        scratch_shapes=[pltpu.VMEM((length, 128), F32)] * 2,
+        in_specs=[block] * 4
+        + [pl.BlockSpec((1, 2, length), lambda i: (i, 0, 0))]
+        + [fixed] * 3
+        + [ANYWHERE] * len(load.operands),
+        out_specs=[pl.BlockSpec((length, 3 * total), lambda i: (0, 0))]
+        + [ANYWHERE] * len(load.outs_like),
+        out_shape=[jax.ShapeDtypeStruct((length, 3 * total), BF)] + load.outs_like,
+        scratch_shapes=[pltpu.VMEM((length, 128), F32)] * 2 + load.scratch,
+        compiler_params=pltpu.CompilerParams(collective_id=place, has_side_effects=True),
         cost_estimate=pl.CostEstimate(
             flops=10 * length * length * total,
             transcendentals=length * length * total // 64,
-            bytes_accessed=length * total * 16,
+            bytes_accessed=100_000_000,
         ),
         name="self_attention_back",
-    )(queries, keys, values, grads, logs, *tables)
+    )(queries, keys, values, grads, logs, *tables, *load.operands)
 
 
 def cross_attention(queries, context, bias):
@@ -745,7 +823,7 @@
     block = pl.BlockSpec((length, 128), lambda i: (0, i))
     key_block = lambda shift: pl.BlockSpec((slots, 128), lambda i: (0, i + shift))
     return pl.pallas_call(
-        functools.partial(attention_forward_kernel, HD, 512, False),
+        cross_attention_kernel,
         grid=(pairs,),
         in_specs=[block, key_block(0), key_block(pairs), pl.BlockSpec((slots, 1), lambda i: (0, 0))],
         out_specs=[block, pl.BlockSpec((1, 2, length), lambda i: (i, 0, 0))],
@@ -769,7 +847,7 @@
     block = pl.BlockSpec((length, 128), lambda i: (0, i))
     key_block = lambda shift: pl.BlockSpec((slots, 128), lambda i: (0, i + shift))
     return pl.pallas_call(
-        functools.partial(attention_backward_kernel, HD, 512, False),
+        functools.partial(attention_backward_kernel, HD, 512, False, None),
         grid=(pairs,),
         in_specs=[
             block,
@@ -806,65 +884,970 @@
     return lax.dot_general(left, right, (((0,), (0,)), ((), ())), preferred_element_type=F32)
 
 
-def group_scatter(partial):
-    rows = partial.shape[0] // 4
-    other = move(partial[2 * rows :], SWAP_CORE)
-    half = partial[: 2 * rows].astype(F32) + other.astype(F32)
-    far = move(half[rows:].astype(BF), SWAP_Z)
-    return half[:rows] + far.astype(F32)
-
-
-def group_gather(part):
-    far = move(part, SWAP_Z)
-    half = jnp.concatenate([part, far], axis=0)
+PLANE = [[0, 2, 4, 6], [1, 3, 5, 7]]
+
+
+def group_sum(partial):
+    rows = partial.shape[0] // 2
+    half = partial[:rows].astype(F32) + move(partial[rows:], SWAP_CORE).astype(F32)
+    half = half.astype(BF)
+    return half.astype(F32) + move(half, SWAP_Z).astype(F32)
+
+
+def both_halves(half):
     return jnp.concatenate([half, move(half, SWAP_CORE)], axis=0)
 
 
-def weight_spread(part, pair):
-    one = move(part, ROUTE_A)
-    two = move(part, ROUTE_B)
+def weight_order(one, two, pair):
     first = jnp.where(pair == 0, one, two)
     second = jnp.where(pair == 0, two, one)
     return jnp.concatenate([first, second], axis=0)
 
 
 def plane_gather(mine):
-    rows = mine.shape[0] // 2
-    from_x = move(mine, SWAP_X)
-    from_y = move(mine, SWAP_Y)
-    diag_one = move(from_x[:rows], SWAP_Y)
-    diag_two = move(from_y[rows:], SWAP_X)
-    return jnp.concatenate([mine, from_x, from_y, diag_one, diag_two], axis=0)
-
-
-def plane_scatter(grad, pair):
-    rows = grad.shape[0] // 8
-    blocks = [grad[2 * rows * j : 2 * rows * (j + 1)] for j in range(4)]
-    got_x = move(blocks[3][:rows], SWAP_X)
-    got_y = move(blocks[3][rows:], SWAP_Y)
-    to_x = jnp.concatenate(
-        [
-            blocks[1][:rows],
-            (blocks[1][rows:].astype(F32) + got_y.astype(F32)).astype(BF),
-        ],
-        axis=0,
-    )
-    to_y = jnp.concatenate(
-        [
-            (blocks[2][:rows].astype(F32) + got_x.astype(F32)).astype(BF),
-            blocks[2][rows:],
-        ],
-        axis=0,
-    )
-    total = (
-        blocks[0].astype(F32)
-        + move(to_x, SWAP_X).astype(F32)
-        + move(to_y, SWAP_Y).astype(F32)
-    ).astype(BF)
+    return lax.all_gather(mine, "dp", axis=0, tiled=True, axis_index_groups=PLANE)
+
+
+def plane_sum(grad):
+    return lax.psum_scatter(
+        grad, "dp", scatter_dimension=0, tiled=True, axis_index_groups=PLANE
+    )
+
+
+def to_owners(total, pair):
+    rows = total.shape[0] // 2
     first, second = total[:rows], total[rows:]
     one = move(jnp.where(pair == 0, first, second), ROUTE_A)
     two = move(jnp.where(pair == 0, second, first), RETURN_B)
     return one.astype(F32) + two.astype(F32)
+
+
+def after(values, *others):
+    return lax.optimization_barrier((values, *others))[0]
+
+
+class Place:
+    def __init__(self):
+        d = lax.axis_index("dp")
+        z = lax.axis_index("mp")
+        self.d, self.z = d, z
+        self.core = lax.rem(d, 2)
+        self.column = d // 2
+        self.pair = z // 2
+        self.owner = self.core == self.pair
+        self.core_peer = (d + 1 - 2 * self.core, z)
+        self.near_z = (d, z + 1 - 2 * lax.rem(z, 2))
+        self.far_z = z + 2 - 4 * self.pair
+        self.far_same = (d, self.far_z)
+        self.far_other = (self.core_peer[0], self.far_z)
+        self.user = (2 * self.column + self.pair, self.far_z)
+        self.x_peer = (d + 2 - 4 * lax.rem(self.column, 2), z)
+        self.y_peer = (d + 4 - 8 * (self.column // 2), z)
+        self.x_column = self.column + 1 - 2 * lax.rem(self.column, 2)
+        self.y_column = self.column + 2 - 4 * (self.column // 2)
+
+
+def greet(peers):
+    barrier = pltpu.get_barrier_semaphore()
+    for peer in peers:
+        pl.semaphore_signal(
+            barrier, inc=1, device_id=peer, device_id_type=pl.DeviceIdType.MESH
+        )
+    pl.semaphore_wait(barrier, len(peers))
+
+
+def send(source, target, sent, got, peer):
+    return pltpu.make_async_remote_copy(
+        src_ref=source,
+        dst_ref=target,
+        send_sem=sent,
+        recv_sem=got,
+        device_id=peer,
+        device_id_type=pl.DeviceIdType.MESH,
+    )
+
+
+class Spread:
+    scratch = [pltpu.SemaphoreType.DMA((2,)), pltpu.SemaphoreType.DMA((3,)), pltpu.SemaphoreType.DMA]
+    late = True
+
+    @staticmethod
+    def outs(part):
+        return [jax.ShapeDtypeStruct((2 * part.shape[0], part.shape[1]), BF)]
+
+    @staticmethod
+    def peers(place):
+        return [place.far_same, place.far_other]
+
+    def __init__(self, place, ins, outs, sems):
+        self.place = place
+        (self.part,), (self.own,), (self.sent, self.got, self.here) = ins, outs, sems
+
+    def target(self, sender):
+        rows = self.part.shape[0]
+        return self.own.at[pl.ds(pl.multiple_of(sender * rows, rows), rows)]
+
+    def far(self, sender):
+        return send(
+            self.part, self.target(sender), self.sent.at[0], self.got.at[sender], self.place.user
+        )
+
+    def near(self, sender):
+        return send(
+            self.part, self.target(sender), self.sent.at[1], self.got.at[2], self.place.core_peer
+        )
+
+    def local(self):
+        return pltpu.make_async_copy(self.part, self.target(self.place.core), self.here)
+
+    def start(self):
+        place = self.place
+        self.far(place.core).start()
+
+        @pl.when(place.owner)
+        def _():
+            self.local().start()
+
+        @pl.when(jnp.logical_not(place.owner))
+        def _():
+            self.near(place.core).start()
+
+    def middle(self):
+        pass
+
+    def finish(self):
+        place = self.place
+
+        @pl.when(place.owner)
+        def _():
+            self.local().wait()
+            self.near(1 - place.core).wait_recv()
+
+        @pl.when(jnp.logical_not(place.owner))
+        def _():
+            self.near(place.core).wait_send()
+            self.far(0).wait_recv()
+            self.far(1).wait_recv()
+
+        self.far(place.core).wait_send()
+
+
+class Plane:
+    scratch = [
+        pltpu.SemaphoreType.DMA((2, 3)),
+        pltpu.SemaphoreType.DMA((2, 3)),
+        pltpu.SemaphoreType.DMA,
+    ]
+    late = False
+
+    @staticmethod
+    def outs(own):
+        return [jax.ShapeDtypeStruct((4 * own.shape[0], own.shape[1]), BF)]
+
+    @staticmethod
+    def peers(place):
+        return [place.x_peer, place.y_peer]
+
+    def __init__(self, place, ins, outs, sems):
+        self.place = place
+        (self.own,), (self.full,), (self.sent, self.got, self.here) = ins, outs, sems
+        self.rows = self.own.shape[0] // 2
+
+    def target(self, column, part):
+        rows = self.rows
+        return self.full.at[pl.ds(pl.multiple_of((2 * column + part) * rows, rows), rows)]
+
+    def one(self, way, part):
+        place = self.place
+        peer = place.x_peer if way == 0 else place.y_peer
+        return send(
+            self.own.at[pl.ds(part * self.rows, self.rows)],
+            self.target(place.column, part),
+            self.sent.at[way, part],
+            self.got.at[way, part],
+            peer,
+        )
+
+    def two(self, way):
+        place = self.place
+        if way == 0:
+            spot = self.target(place.y_column, 1)
+            return send(spot, spot, self.sent.at[0, 2], self.got.at[0, 2], place.x_peer)
+        spot = self.target(place.x_column, 0)
+        return send(spot, spot, self.sent.at[1, 2], self.got.at[1, 2], place.y_peer)
+
+    def local(self):
+        rows = self.own.shape[0]
+        place = self.full.at[pl.ds(pl.multiple_of(self.place.column * rows, rows), rows)]
+        return pltpu.make_async_copy(self.own, place, self.here)
+
+    def start(self):
+        for way in range(2):
+            self.one(way, way).start()
+        for way in range(2):
+            self.one(way, 1 - way).start()
+        self.local().start()
+
+    def middle(self):
+        self.one(0, 0).wait_recv()
+        self.two(1).start()
+        self.one(1, 1).wait_recv()
+        self.two(0).start()
+
+    def finish(self):
+        self.local().wait()
+        for way in range(2):
+            self.one(way, 1 - way).wait_recv()
+            self.two(way).wait_recv()
+            self.two(way).wait_send()
+            for part in range(2):
+                self.one(way, part).wait_send()
+
+
+class Return:
+    scratch = [pltpu.SemaphoreType.DMA((2,)), pltpu.SemaphoreType.DMA((2,))]
+    late = True
+
+    @staticmethod
+    def outs(total):
+        shape = jax.ShapeDtypeStruct((total.shape[0] // 2, total.shape[1]), BF)
+        return [shape, shape]
+
+    @staticmethod
+    def peers(place):
+        return [place.far_same, place.far_other]
+
+    def __init__(self, place, ins, outs, sems):
+        self.place = place
+        (self.total,), (self.near, self.far), (self.sent, self.got) = ins, outs, sems
+
+    def part(self, which):
+        rows = self.near.shape[0]
+        return self.total.at[pl.ds(pl.multiple_of(which * rows, rows), rows)]
+
+    def to_near(self):
+        place = self.place
+        return send(
+            self.part(1 - place.core), self.near, self.sent.at[0], self.got.at[0], place.core_peer
+        )
+
+    def to_far(self, same):
+        place = self.place
+        which = place.core if same else 1 - place.core
+        peer = place.far_same if same else place.far_other
+        return send(
+            self.part(which), self.far, self.sent.at[0 if same else 1], self.got.at[1], peer
+        )
+
+    def start(self):
+        place = self.place
+
+        @pl.when(place.owner)
+        def _():
+            self.to_near().start()
+
+        @pl.when(jnp.logical_not(place.owner))
+        def _():
+            self.to_far(True).start()
+            self.to_far(False).start()
+
+    def middle(self):
+        pass
+
+    def finish(self):
+        place = self.place
+
+        @pl.when(place.owner)
+        def _():
+            self.to_near().wait_send()
+            self.to_far(True).wait_recv()
+
+        @pl.when(jnp.logical_not(place.owner))
+        def _():
+            self.to_far(True).wait_send()
+            self.to_far(False).wait_send()
+            self.to_near().wait_recv()
+            self.to_far(False).wait_recv()
+
+
+class Swap:
+    scratch = [pltpu.SemaphoreType.DMA, pltpu.SemaphoreType.DMA]
+    late = True
+    way = None
+
+    @staticmethod
+    def outs(values):
+        return [jax.ShapeDtypeStruct(values.shape, values.dtype)]
+
+    @classmethod
+    def peers(cls, place):
+        return {
+            "core": [place.core_peer],
+            "z": [place.near_z],
+            "route": [place.far_same, place.far_other],
+        }[cls.way]
+
+    def __init__(self, place, ins, outs, sems):
+        self.place = place
+        peer = {"core": place.core_peer, "z": place.near_z, "route": place.far_other}[self.way]
+        self.copy = send(ins[0], outs[0], sems[0], sems[1], peer)
+
+    def each(self, act):
+        if self.way != "route":
+            act()
+            return
+
+        @pl.when(jnp.logical_not(self.place.owner))
+        def _():
+            act()
+
+    def start(self):
+        self.each(lambda: self.copy.start())
+
+    def middle(self):
+        pass
+
+    def finish(self):
+        self.each(lambda: self.copy.wait())
+
+
+class SwapCore(Swap):
+    way = "core"
+
+
+class SwapNear(Swap):
+    way = "z"
+
+
+class SwapRoute(Swap):
+    way = "route"
+
+
+class Loads:
+    def __init__(self, *loads):
+        self.loads = loads
+        self.operands = [operand for _, operand in loads]
+        self.outs_like = [out for kind, operand in loads for out in kind.outs(operand)]
+        self.scratch = [sem for kind, _ in loads for sem in kind.scratch]
+
+    def peers(self, place, base):
+        found = {id(peer): peer for peer in base}
+        for kind, _ in self.loads:
+            for peer in kind.peers(place):
+                found[id(peer)] = peer
+        return list(found.values())
+
+    def begin(self, place, ins, outs, sems):
+        result, at, sem_at = [], 0, 0
+        for (kind, operand), source in zip(self.loads, ins):
+            count, sem_count = len(kind.outs(operand)), len(kind.scratch)
+            result.append(
+                kind(
+                    place,
+                    [source],
+                    outs[at : at + count],
+                    sems[sem_at : sem_at + sem_count],
+                )
+            )
+            at, sem_at = at + count, sem_at + sem_count
+        return result
+
+
+ANYWHERE = pl.BlockSpec(memory_space=pl.ANY)
+
+
+def returned(total, near, far, core, owner):
+    rows = near.shape[0]
+    mine = jnp.where(core == 0, total[:rows], total[rows:])
+    return jnp.where(owner, mine, near).astype(F32) + far.astype(F32)
+
+
+def exchange_kernel(kind, chunks, load, *refs):
+    refs = list(refs)
+    place = Place()
+    more = (len(load.operands), len(load.outs_like))
+    ins, refs = refs[:5], refs[5:]
+    load_ins, refs = refs[: more[0]], refs[more[0] :]
+    outs, refs = refs[:2], refs[2:]
+    load_outs, refs = refs[: more[1]], refs[more[1] :]
+    rest, refs = refs[:11], refs[11:]
+    if kind == "norm":
+        a_ref, w_ref, res_ref, gain_ref, bias_ref = ins
+        res_out, all_ref = outs
+    else:
+        a_ref, w_ref, res_ref, up_ref, gain_ref = ins
+        all_ref, sum_ref = outs
+    carried = load.begin(place, load_ins, load_outs, refs)
+    mine, given, near, half, far, send_near, got_near, send_far, got_far, send_all, got_all = rest
+    rows = mine.shape[0]
+    width = mine.shape[1]
+    chunk = rows // chunks
+    core_peer, far_peer = place.core_peer, place.near_z
+    copy = send
+    greet(load.peers(place, [core_peer, far_peer]))
+    for each in carried:
+        if not each.late:
+            each.start()
+
+    def near_copy(k):
+        part = pl.ds(k * chunk, chunk)
+        return copy(given.at[part], near.at[part], send_near.at[k], got_near.at[k], core_peer)
+
+    def far_copy(k):
+        part = pl.ds(k * chunk, chunk)
+        return copy(half.at[part], far.at[part], send_far.at[k], got_far.at[k], far_peer)
+
+    def all_copy(k):
+        return copy(
+            all_ref.at[pl.ds(k * chunk, chunk)],
+            all_ref.at[pl.ds(rows + k * chunk, chunk)],
+            send_all.at[k],
+            got_all.at[k],
+            core_peer,
+        )
+
+    block = 2 * chunk
+    tile = 256
+
+    def product(first, target, start):
+        @pl.loop(0, width // tile)
+        def _(step):
+            columns = pl.ds(pl.multiple_of(step * tile, tile), tile)
+            target[pl.ds(start, block), columns] = lax.dot_general(
+                a_ref[pl.ds(first, block), :],
+                w_ref[columns, :],
+                (((1,), (1,)), ((), ())),
+                preferred_element_type=F32,
+            ).astype(target.dtype)
+
+    step_rows = 16
+    for m in range(chunks // 2):
+        product(rows + m * block, given, m * block)
+        for k in (2 * m, 2 * m + 1):
+            near_copy(k).start()
+        product(m * block, mine, m * block)
+        for k in (2 * m, 2 * m + 1):
+            near_copy(k).wait_recv()
+
+            @pl.loop(0, chunk // step_rows)
+            def _(step):
+                part = pl.ds(pl.multiple_of(k * chunk + step * step_rows, step_rows), step_rows)
+                half[part, :] = (mine[part, :] + near[part, :].astype(F32)).astype(BF)
+
+            far_copy(k).start()
+    for each in carried:
+        if each.late:
+            each.start()
+    if kind != "norm":
+        sum_ref[...] = jnp.zeros_like(sum_ref)
+    for k in range(chunks):
+        far_copy(k).wait_recv()
+
+        @pl.loop(0, chunk // step_rows)
+        def _(step):
+            part = pl.ds(pl.multiple_of(k * chunk + step * step_rows, step_rows), step_rows)
+            total = half[part, :].astype(F32) + far[part, :].astype(F32)
+            if kind == "norm":
+                values = res_ref[part, :] + total
+                res_out[part, :] = values
+            else:
+                values = res_ref[part, :]
+            centered = values - jnp.mean(values, axis=-1, keepdims=True)
+            inverse = lax.rsqrt(jnp.mean(centered * centered, axis=-1, keepdims=True) + EPS)
+            scaled = centered * inverse
+            if kind == "norm":
+                all_ref[part, :] = (scaled * gain_ref[...] + bias_ref[...]).astype(BF)
+            else:
+                grad_scaled = total * gain_ref[...]
+                first_mean = jnp.mean(grad_scaled, axis=-1, keepdims=True)
+                second_mean = jnp.mean(grad_scaled * scaled, axis=-1, keepdims=True)
+                grads = inverse * (grad_scaled - first_mean - scaled * second_mean)
+                all_ref[part, :] = (up_ref[part, :].astype(F32) + grads).astype(BF)
+                product_rows = total * scaled
+                sum_ref[0] += product_rows[:8] + product_rows[8:]
+                sum_ref[1] += total[:8] + total[8:]
+
+        if k == 1:
+            for each in carried:
+                each.middle()
+        if kind != "half":
+            all_copy(k).start()
+    for k in range(chunks):
+        near_copy(k).wait_send()
+        far_copy(k).wait_send()
+        if kind != "half":
+            all_copy(k).wait_send()
+            all_copy(k).wait_recv()
+    for each in carried:
+        each.finish()
+
+
+def exchange(kind, place, a, w, residual, *others, load=Loads()):
+    length, depth = a.shape
+    width = w.shape[0]
+    rows = length // 2
+    chunks = 4
+    whole = pl.BlockSpec(memory_space=pltpu.VMEM)
+    if kind == "norm":
+        gain, bias = others
+        operands = (a, w, residual, gain[None], bias[None])
+        outs = [
+            jax.ShapeDtypeStruct((rows, width), F32),
+            jax.ShapeDtypeStruct((length, width), BF),
+        ]
+    else:
+        up, gain = others
+        operands = (a, w, residual, up, gain[None])
+        outs = [
+            jax.ShapeDtypeStruct((rows if kind == "half" else length, width), BF),
+            jax.ShapeDtypeStruct((2, 8, width), F32),
+        ]
+    specs = [whole] * 5 + [ANYWHERE] * len(load.operands)
+    out_specs = [whole] * 2 + [ANYWHERE] * len(load.outs_like)
+    operands += tuple(load.operands)
+    outs = outs + load.outs_like
+    return pl.pallas_call(
+        functools.partial(exchange_kernel, kind, chunks, load),
+        in_specs=specs,
+        out_specs=out_specs,
+        out_shape=outs,
+        scratch_shapes=[
+            pltpu.VMEM((rows, width), F32),
+            pltpu.VMEM((rows, width), BF),
+            pltpu.VMEM((rows, width), BF),
+            pltpu.VMEM((rows, width), BF),
+            pltpu.VMEM((rows, width), BF),
+        ]
+        + [pltpu.SemaphoreType.DMA((chunks,))] * 6
+        + load.scratch,
+        compiler_params=pltpu.CompilerParams(
+            collective_id=place, has_side_effects=True, vmem_limit_bytes=60 * 2**20
+        ),
+        cost_estimate=pl.CostEstimate(
+            flops=2 * length * depth * width,
+            transcendentals=0,
+            bytes_accessed=100_000_000,
+        ),
+        name="exchange_" + kind,
+    )(*operands)
+
+
+def spread_kernel(load, chunks, *refs):
+    refs = list(refs)
+    more = (len(load.operands), len(load.outs_like))
+    half_ref, refs = refs[0], refs[1:]
+    load_ins, refs = refs[: more[0]], refs[more[0] :]
+    (out_ref, token_ref), refs = refs[:2], refs[2:]
+    load_outs, refs = refs[: more[1]], refs[more[1] :]
+    (sent, got, send_token, got_token), refs = refs[:4], refs[4:]
+    place = Place()
+    carried = load.begin(place, load_ins, load_outs, refs)
+    d, core, pair = place.d, place.core, place.pair
+    inner_z = lax.rem(place.z, 2)
+    plane_peers = [(lax.rem(d + j, 8), place.z) for j in range(1, 8)]
+    greet([place.near_z, place.far_same, place.far_other] + plane_peers)
+    rows = half_ref.shape[0]
+    chunk = rows // chunks
+
+    def spot(which, k):
+        return out_ref.at[pl.ds(pl.multiple_of(which * rows + k * chunk, chunk), chunk)]
+
+    def owner_copy(k, which):
+        source = half_ref.at[pl.ds(k * chunk, chunk)]
+        return send(source, spot(which, k), sent.at[0, k], got.at[0, k], place.core_peer)
+
+    def pair_copy(k, which):
+        source = half_ref.at[pl.ds(k * chunk, chunk)]
+        return send(source, spot(which, k), sent.at[1, k], got.at[1, k], place.user)
+
+    def pass_copy(k, which):
+        return send(spot(which, k), spot(which, k), sent.at[2, k], got.at[2, k], place.near_z)
+
+    @pl.when(core == inner_z)
+    def _():
+        for k in range(chunks):
+            pair_copy(k, core).start()
+
+    for each in carried:
+        each.start()
+
+    @pl.when(core != pair)
+    def _():
+        for k in range(chunks):
+            owner_copy(k, core).start()
+
+    @pl.when(core == pair)
+    def _():
+        @pl.loop(0, rows // 16)
+        def _(step):
+            first = pl.multiple_of(step * 16, 16)
+            out_ref[pl.ds(pl.multiple_of(core * rows + first, 16), 16), :] = half_ref[
+                pl.ds(first, 16), :
+            ]
+
+        for k in range(chunks):
+            owner_copy(k, 1 - core).wait_recv()
+
+    @pl.when(core != pair)
+    def _():
+        for k in range(chunks):
+            pair_copy(k, inner_z).wait_recv()
+            pass_copy(k, inner_z).start()
+        for k in range(chunks):
+            pass_copy(k, 1 - inner_z).wait_recv()
+
+    head = 16
+    token_ref[pl.ds(pl.multiple_of(d * head, head), head), :] = out_ref[pl.ds(0, head), :]
+
+    def token_copy(j, sender):
+        return send(
+            out_ref.at[pl.ds(0, head)],
+            token_ref.at[pl.ds(pl.multiple_of(sender * head, head), head)],
+            send_token.at[j - 1],
+            got_token.at[j - 1],
+            plane_peers[j - 1],
+        )
+
+    for j in range(1, 8):
+        token_copy(j, d).start()
+
+    @pl.when(core != pair)
+    def _():
+        for k in range(chunks):
+            pass_copy(k, inner_z).wait_send()
+            owner_copy(k, core).wait_send()
+
+    @pl.when(core == inner_z)
+    def _():
+        for k in range(chunks):
+            pair_copy(k, core).wait_send()
+
+    for j in range(1, 8):
+        token_copy(j, d).wait_send()
+        token_copy(j, lax.rem(d + 8 - j, 8)).wait_recv()
+    for each in carried:
+        each.finish()
+
+
+def spread_gradient(place, half, load):
+    rows, width = half.shape
+    chunks = 4
+    whole = pl.BlockSpec(memory_space=pltpu.VMEM)
+    return pl.pallas_call(
+        functools.partial(spread_kernel, load, chunks),
+        in_specs=[whole] + [ANYWHERE] * len(load.operands),
+        out_specs=[whole] * 2 + [ANYWHERE] * len(load.outs_like),
+        out_shape=[
+            jax.ShapeDtypeStruct((2 * rows, width), BF),
+            jax.ShapeDtypeStruct((8 * 16, width), BF),
+        ]
+        + load.outs_like,
+        scratch_shapes=[
+            pltpu.SemaphoreType.DMA((3, chunks)),
+            pltpu.SemaphoreType.DMA((3, chunks)),
+            pltpu.SemaphoreType.DMA((7,)),
+            pltpu.SemaphoreType.DMA((7,)),
+        ]
+        + load.scratch,
+        compiler_params=pltpu.CompilerParams(
+            collective_id=place, has_side_effects=True, vmem_limit_bytes=60 * 2**20
+        ),
+        cost_estimate=pl.CostEstimate(flops=0, transcendentals=0, bytes_accessed=100_000_000),
+        name="spread_gradient",
+    )(half, *load.operands)
+
+
+def feed_kernel(n_ref, cot_ref, gate_ref, up_ref, down_ref, hidden_ref, grad_ref):
+    here = pl.program_id(0)
+    length = n_ref.shape[0]
+    tile = gate_ref.shape[1]
+    half = grad_ref.shape[1] // 2
+    block = 256
+    gate_columns = pl.ds(pl.multiple_of(here * tile, tile), tile)
+    up_columns = pl.ds(pl.multiple_of(half + here * tile, tile), tile)
+
+    @pl.loop(0, length // block)
+    def _(step):
+        rows = pl.ds(pl.multiple_of(step * block, block), block)
+        gate = jnp.dot(n_ref[rows, :], gate_ref[...], preferred_element_type=F32)
+        up = jnp.dot(n_ref[rows, :], up_ref[...], preferred_element_type=F32)
+        grad = jnp.dot(cot_ref[rows, :], down_ref[...], preferred_element_type=F32)
+        sigmoid = jax.nn.sigmoid(gate)
+        silu = gate * sigmoid
+        hidden_ref[rows, :] = (silu * up).astype(BF)
+        grad_ref[rows, gate_columns] = (
+            grad * up * sigmoid * (1.0 + gate * (1.0 - sigmoid))
+        ).astype(BF)
+        grad_ref[rows, up_columns] = (grad * silu).astype(BF)
+
+
+def feed_forward(normed, cot, gate_up, down):
+    length, width = normed.shape
+    hidden_width = down.shape[1]
+    tile = 256
+    steps = hidden_width // tile
+    fixed = pl.BlockSpec((length, width), lambda j: (0, 0))
+    return pl.pallas_call(
+        feed_kernel,
+        grid=(steps,),
+        in_specs=[
+            fixed,
+            fixed,
+            pl.BlockSpec((width, tile), lambda j: (0, j)),
+            pl.BlockSpec((width, tile), lambda j: (0, j + steps)),
+            pl.BlockSpec((width, tile), lambda j: (0, j)),
+        ],
+        out_specs=[
+            pl.BlockSpec((length, tile), lambda j: (0, j)),
+            pl.BlockSpec((length, 2 * hidden_width), lambda j: (0, 0)),
+        ],
+        out_shape=[
+            jax.ShapeDtypeStruct((length, hidden_width), BF),
+            jax.ShapeDtypeStruct((length, 2 * hidden_width), BF),
+        ],
+        compiler_params=pltpu.CompilerParams(vmem_limit_bytes=60 * 2**20),
+        cost_estimate=pl.CostEstimate(
+            flops=6 * length * width * hidden_width,
+            transcendentals=length * hidden_width,
+            bytes_accessed=30_000_000,
+        ),
+        name="feed_forward",
+    )(normed, cot, gate_up, gate_up, down)
+
+
+def front_kernel(
+    qkv_part,
+    side_part,
+    latents,
+    prompt,
+    time_part,
+    facts,
+    qkv_full,
+    side_own,
+    latents_too,
+    prompt_too,
+    time_full,
+    facts_full,
+    send_far,
+    got_far,
+    send_near,
+    got_near,
+    here,
+    send_plane,
+    got_plane,
+    send_swap,
+    got_swap,
+    send_small,
+    got_small,
+):
+    d = lax.axis_index("dp")
+    z = lax.axis_index("mp")
+    core = lax.rem(d, 2)
+    column = d // 2
+    pair = z // 2
+    far_z = z + 2 - 4 * pair
+    core_peer = (d + 1 - 2 * core, z)
+    x_peer = (d + 2 - 4 * lax.rem(column, 2), z)
+    y_peer = (d + 4 - 8 * (column // 2), z)
+    x_column = column + 1 - 2 * lax.rem(column, 2)
+    y_column = column + 2 - 4 * (column // 2)
+    owner = core == pair
+    barrier = pltpu.get_barrier_semaphore()
+    plane_peers = [(lax.rem(d + j, 8), z) for j in range(1, 8)]
+    peers = [(d, far_z), (core_peer[0], far_z)] + plane_peers
+    for peer in peers:
+        pl.semaphore_signal(
+            barrier, inc=1, device_id=peer, device_id_type=pl.DeviceIdType.MESH
+        )
+    pl.semaphore_wait(barrier, len(peers))
+    rows = qkv_part.shape[0]
+    piece = rows // 2
+
+    def copy(source, target, send, got, peer):
+        return pltpu.make_async_remote_copy(
+            src_ref=source,
+            dst_ref=target,
+            send_sem=send,
+            recv_sem=got,
+            device_id=peer,
+            device_id_type=pl.DeviceIdType.MESH,
+        )
+
+    def part_copy(k, sender, send, got, peer):
+        if k < 2:
+            return copy(
+                qkv_part.at[pl.ds(k * piece, piece)],
+                qkv_full.at[pl.ds((2 * column + sender) * rows + k * piece, piece)],
+                send,
+                got,
+                peer,
+            )
+        return copy(side_part, side_own.at[pl.ds(sender * rows, rows)], send, got, peer)
+
+    user = 2 * column + pair
+    swaps = [
+        copy(latents, latents_too, send_swap.at[0], got_swap.at[0], core_peer),
+        copy(prompt, prompt_too, send_swap.at[1], got_swap.at[1], core_peer),
+    ]
+    swaps[0].start()
+    far_parts = [
+        part_copy(k, core, send_far.at[k], got_far.at[core, k], (user, far_z)) for k in range(3)
+    ]
+    for part in far_parts:
+        part.start()
+    near_parts = [
+        part_copy(k, core, send_near.at[k], got_near.at[k], core_peer) for k in range(3)
+    ]
+    own_parts = [
+        pltpu.make_async_copy(
+            qkv_part, qkv_full.at[pl.ds((2 * column + core) * rows, rows)], here.at[0]
+        ),
+        pltpu.make_async_copy(side_part, side_own.at[pl.ds(core * rows, rows)], here.at[1]),
+    ]
+
+    @pl.when(owner)
+    def _():
+        for part in own_parts:
+            part.start()
+
+    @pl.when(jnp.logical_not(owner))
+    def _():
+        for part in near_parts:
+            part.start()
+
+    swaps[1].start()
+
+    def small_copies(sender, j, peer):
+        result = []
+        for which, (part, whole) in enumerate(((time_part, time_full), (facts, facts_full))):
+            count = part.shape[0]
+            place = whole.at[pl.ds(sender * count, count)]
+            result.append(
+                copy(part, place, send_small.at[which, j - 1], got_small.at[which, j - 1], peer)
+            )
+        return result
+
+    small_own = [
+        pltpu.make_async_copy(
+            part, whole.at[pl.ds(d * part.shape[0], part.shape[0])], here.at[2 + which]
+        )
+        for which, (part, whole) in enumerate(((time_part, time_full), (facts, facts_full)))
+    ]
+    for part in small_own:
+        part.start()
+    for j in range(1, 8):
+        for part in small_copies(d, j, plane_peers[j - 1]):
+            part.start()
+
+    def await_part(k, sender):
+        @pl.when(owner)
+        def _():
+            @pl.when(core == sender)
+            def _():
+                if k == 0:
+                    own_parts[0].wait()
+                if k == 2:
+                    own_parts[1].wait()
+
+            @pl.when(core != sender)
+            def _():
+                part_copy(k, sender, send_near.at[k], got_near.at[k], core_peer).wait_recv()
+
+        @pl.when(jnp.logical_not(owner))
+        def _():
+            part_copy(k, sender, send_far.at[k], got_far.at[sender, k], core_peer).wait_recv()
+
+    def plane_copy(stage, way, k, sender):
+        peer = x_peer if way == 0 else y_peer
+        if stage == 0:
+            source = column
+        else:
+            source = y_column if way == 0 else x_column
+        place = pl.ds((2 * source + sender) * rows + k * piece, piece)
+        slot = 4 * stage + 2 * sender + k
+        return copy(
+            qkv_full.at[place],
+            qkv_full.at[place],
+            send_plane.at[way, slot],
+            got_plane.at[way, slot],
+            peer,
+        )
+
+    for k in range(2):
+        for sender in range(2):
+            await_part(k, sender)
+            plane_copy(0, 0, k, sender).start()
+            plane_copy(0, 1, k, sender).start()
+    for k in range(2):
+        plane_copy(0, 0, k, 0).wait_recv()
+        plane_copy(1, 1, k, 0).start()
+        plane_copy(0, 1, k, 1).wait_recv()
+        plane_copy(1, 0, k, 1).start()
+        plane_copy(0, 0, k, 1).wait_recv()
+        plane_copy(0, 1, k, 0).wait_recv()
+    for k in range(2):
+        plane_copy(1, 1, k, 0).wait_recv()
+        plane_copy(1, 0, k, 1).wait_recv()
+    for sender in range(2):
+        await_part(2, sender)
+    for part in swaps:
+        part.wait()
+    for part in small_own:
+        part.wait()
+    for j in range(1, 8):
+        sender = lax.rem(d + 8 - j, 8)
+        for part in small_copies(sender, j, plane_peers[j - 1]):
+            part.wait_recv()
+        for part in small_copies(d, j, plane_peers[j - 1]):
+            part.wait_send()
+    for part in far_parts:
+        part.wait_send()
+
+    @pl.when(jnp.logical_not(owner))
+    def _():
+        for part in near_parts:
+            part.wait_send()
+
+    for k in range(2):
+        for sender in range(2):
+            plane_copy(0, 0, k, sender).wait_send()
+            plane_copy(0, 1, k, sender).wait_send()
+        plane_copy(1, 1, k, 0).wait_send()
+        plane_copy(1, 0, k, 1).wait_send()
+
+
+def front(qkv_part, side_part, latents, prompt, time_part, facts):
+    place = pl.BlockSpec(memory_space=pl.ANY)
+    rows = qkv_part.shape[0]
+    return pl.pallas_call(
+        front_kernel,
+        in_specs=[place] * 6,
+        out_specs=[place] * 6,
+        out_shape=(
+            jax.ShapeDtypeStruct((8 * rows, qkv_part.shape[1]), BF),
+            jax.ShapeDtypeStruct((2 * rows, side_part.shape[1]), BF),
+            jax.ShapeDtypeStruct(latents.shape, BF),
+            jax.ShapeDtypeStruct(prompt.shape, BF),
+            jax.ShapeDtypeStruct((8 * time_part.shape[0], time_part.shape[1]), BF),
+            jax.ShapeDtypeStruct((8 * facts.shape[0], facts.shape[1]), facts.dtype),
+        ),
+        scratch_shapes=[
+            pltpu.SemaphoreType.DMA((3,)),
+            pltpu.SemaphoreType.DMA((2, 3)),
+            pltpu.SemaphoreType.DMA((3,)),
+            pltpu.SemaphoreType.DMA((3,)),
+            pltpu.SemaphoreType.DMA((4,)),
+            pltpu.SemaphoreType.DMA((2, 8)),
+            pltpu.SemaphoreType.DMA((2, 8)),
+            pltpu.SemaphoreType.DMA((2,)),
+            pltpu.SemaphoreType.DMA((2,)),
+            pltpu.SemaphoreType.DMA((2, 7)),
+            pltpu.SemaphoreType.DMA((2, 7)),
+        ],
+        compiler_params=pltpu.CompilerParams(collective_id=5, has_side_effects=True),
+        cost_estimate=pl.CostEstimate(flops=0, transcendentals=0, bytes_accessed=100_000_000),
+        name="front",
+    )(qkv_part, side_part, latents, prompt, time_part, facts)
 
 
 def per_device_paired(
@@ -891,15 +1874,14 @@
 ):
     d = lax.axis_index("dp")
     z = lax.axis_index("mp")
-    core, column, pair = d & 1, d >> 1, z >> 1
-    shard = (z & 1) + 2 * core
+    core, pair = d & 1, z >> 1
     owner = core == pair
-    width = latents.shape[-1]
     length = latents.shape[1] + 1
     rows = length // 4
+    half_rows = length // 2
     part_rows = qkv_weight.shape[0]
-
-    qkv_part = qkv_weight.reshape(part_rows, -1)
+    n = cross_query_weight.shape[1]
+
     side_part = jnp.concatenate(
         [
             self_out_weight.T,
@@ -909,53 +1891,33 @@
         ],
         axis=1,
     )
-    gate_up_part = gate_up_weight.reshape(part_rows, -1)
-    down_part = down_weight.T
-    qkv_own = weight_spread(qkv_part, pair)
-    side_own = weight_spread(side_part, pair)
-    gate_up_own = weight_spread(gate_up_part, pair)
-    down_own = weight_spread(down_part, pair)
-    qkv_full = plane_gather(qkv_own)
+    facts = jnp.zeros((8, 128), jnp.int32)
+    facts = facts.at[0].set(prompt_lengths[0]).at[1].set(timesteps[0])
+    qkv_full, side_own, latents_too, prompt_too, time_full, facts_full = front(
+        qkv_weight.reshape(part_rows, -1),
+        side_part,
+        latents[0],
+        prompt_tokens[0],
+        time_weight,
+        facts,
+    )
     side_full = plane_gather(side_own)
-    gate_up_full = plane_gather(gate_up_own)
-    down_full = plane_gather(down_own)
-    n = cross_query_weight.shape[1]
     self_out_full = side_full[:, :n]
     cross_query_full = side_full[:, n : 2 * n]
     cross_out_full = side_full[:, 2 * n : 3 * n]
     context_full = side_full[:, 3 * n :].reshape(context_weight.shape[0] * 8, -1)
 
-    def of_item(values):
-        return jnp.where(owner, values, move(values, OWNER_TO_PARTNER))
-
-    item_latents = of_item(latents[0])
-    item_prompt = xor_blocks(of_item(prompt_tokens[0]), 1, 4, column)
-    scalars = of_item(jnp.stack([prompt_lengths[0], timesteps[0]]))
-    item_length, item_step = scalars[0], scalars[1]
-    time_full = time_weight
-    for pairs in (SWAP_CORE, SWAP_X, SWAP_Y):
-        time_full = jnp.concatenate([time_full, move(time_full, pairs)], axis=0)
+    item_latents = jnp.where(owner, latents[0], latents_too)
+    item_prompt = jnp.where(owner, prompt_tokens[0], prompt_too)
+    facts_full = facts_full.reshape(8, 8, 128)[:, :2, 0]
+    item_facts = lax.dynamic_index_in_dim(facts_full, d - core + pair, 0, False)
+    item_length, item_step = item_facts[0], item_facts[1]
     feature_width = time_full.shape[0]
     item_features = time_features(item_step[None], feature_width).astype(BF)
-    token_row = dot_nn(xor_blocks(item_features, 1, 8, d), time_full)
+    token_row = dot_nn(item_features, time_full)
     residual_in = jnp.concatenate([token_row, item_latents.astype(F32)], axis=0)
-    residual_in = xor_blocks(xor_blocks(residual_in, 0, 4, shard), 1, 4, column)
-    residual_mine = residual_in[:rows]
-    vectors = xor_blocks(
-        jnp.stack([self_gain, self_bias, cross_gain, cross_bias, feed_gain, feed_bias, down_bias]),
-        1,
-        4,
-        column,
-    )
-    gain_one, bias_one, gain_two, bias_two, gain_three, bias_three, bias_down = [
-        vectors[j] for j in range(7)
-    ]
-    cot_mine = xor_blocks(move(cotangent[0], ROUTE_A), 1, 4, column)
-    cot_all = group_gather(cot_mine)
-
-    normed_one, _, _ = layer_norm(residual_in, gain_one, bias_one)
-    normed_one = normed_one.astype(BF)
-    projected = dot_nn(normed_one, qkv_full)
+    residual_in = xor_blocks(residual_in, 0, 2, core)
+    residual_mine = residual_in[:half_rows]
     cosine, sine = rope_tables(length, HD)
     quarter = HD // 4
     straight = jnp.ones((length, HD // 2), F32)
@@ -972,98 +1934,126 @@
             ),
         ]
     )
-    tables = xor_blocks(tables, 1, 4, shard)
+    tables = xor_blocks(tables, 1, 2, core)
     tables = (tables[0], tables[1], tables[2])
-    queries, keys, values, attended, self_logs = self_attention(projected, tables)
-    residual_one = residual_mine + group_scatter(dot_nt(attended, self_out_full).astype(BF))
-    normed_two, scaled_two, inverse_two = layer_norm(residual_one, gain_two, bias_two)
-    normed_two_all = group_gather(normed_two.astype(BF))
+    normed_one, queries, keys, values, attended, self_logs, gate_up_own = self_attention(
+        6, residual_in, self_gain, self_bias, qkv_full, tables, gate_up_weight.reshape(part_rows, -1)
+    )
+    gate_up_full = plane_gather(gate_up_own)
+    cot_shard = move(after(cotangent[0], attended), ROUTE_A)
+    residual_one, normed_two_all, down_own = exchange(
+        "norm",
+        0,
+        attended,
+        self_out_full,
+        residual_mine,
+        cross_gain,
+        cross_bias,
+        load=Loads((Spread, down_weight.T)),
+    )
+    cot_shard = after(cot_shard, normed_two_all)
+    cot_far = move(cot_shard, SWAP_Z)
+    odd = (z & 1) == 1
     cross_q = dot_nn(normed_two_all, cross_query_full).astype(BF)
     context = dot_nn(item_prompt, context_full).astype(BF)
     slots = prompt_tokens.shape[1]
     mask = jnp.where(jnp.arange(slots, dtype=jnp.int32)[:, None] < item_length, 0.0, NEG)
     mask = mask.astype(F32)
     crossed, cross_logs = cross_attention(cross_q, context, mask)
-    residual_two = residual_one + group_scatter(dot_nt(crossed, cross_out_full).astype(BF))
-    normed_three, scaled_three, inverse_three = layer_norm(residual_two, gain_three, bias_three)
-    normed_three_all = group_gather(normed_three.astype(BF))
-    gate_up = dot_nn(normed_three_all, gate_up_full)
-    hidden_width = gate_up.shape[1] // 2
-    gate, up = gate_up[:, :hidden_width], gate_up[:, hidden_width:]
-    sigmoid_gate = jax.nn.sigmoid(gate)
-    hidden = (gate * sigmoid_gate * up).astype(BF)
-    feed = group_scatter(dot_nt(hidden, down_full).astype(BF))
-    output = xor_blocks((residual_two + feed + bias_down).astype(BF), 1, 4, column)
-    output = move(output, ROUTE_A)
-
-    grad_hidden = dot_nn(cot_all, down_full)
-    grad_up = grad_hidden * gate * sigmoid_gate
-    grad_gate = grad_hidden * up * sigmoid_gate * (1.0 + gate * (1.0 - sigmoid_gate))
-    grad_gate_up = jnp.concatenate([grad_gate.astype(BF), grad_up.astype(BF)], axis=1)
-    grad_normed_three = group_scatter(dot_nt(grad_gate_up, gate_up_full).astype(BF))
-    down_grad = plane_scatter(dot_tn(cot_all, hidden).astype(BF), pair)
-    gate_up_grad = plane_scatter(dot_tn(normed_three_all, grad_gate_up).astype(BF), pair)
-
-    def norm_back_rows(grad_normed, scaled, inverse, gain):
-        grads, gain_part, bias_part = norm_back(grad_normed[None], scaled[None], inverse[None], gain)
-        return grads[0], gain_part, bias_part
-
-    grad_norm, feed_gain_part, feed_bias_part = norm_back_rows(
-        grad_normed_three, scaled_three, inverse_three, gain_three
-    )
-    cot_rows = cot_mine.astype(F32)
-    down_bias_part = jnp.sum(cot_rows, axis=0)
-    grad_two = (cot_rows + grad_norm).astype(BF)
-    grad_two_all = group_gather(grad_two)
+    cot_far = after(cot_far, crossed)
+    cot_mine = jnp.concatenate(
+        [jnp.where(odd, cot_far, cot_shard), jnp.where(odd, cot_shard, cot_far)], axis=0
+    )
+    cot_other = move(cot_mine, SWAP_CORE)
+    residual_two, normed_three_all, down_full = exchange(
+        "norm",
+        1,
+        crossed,
+        cross_out_full,
+        residual_one,
+        feed_gain,
+        feed_bias,
+        load=Loads((Plane, down_own)),
+    )
+    cot_all = jnp.concatenate([cot_mine, after(cot_other, normed_three_all)], axis=0)
+    hidden, grad_gate_up = feed_forward(normed_three_all, cot_all, gate_up_full, down_full)
+
+    gate_up_local = dot_tn(normed_three_all, grad_gate_up).astype(BF)
+    gate_up_sums = plane_sum(gate_up_local)
+    split = gate_up_weight.shape[2]
+    gate_sums, up_sums = gate_up_sums[:, :split], gate_up_sums[:, split:]
+    grad_two_all, feed_sums = exchange(
+        "back",
+        2,
+        after(grad_gate_up, gate_up_local),
+        gate_up_full,
+        residual_two,
+        cot_mine,
+        feed_gain,
+    )
+    down_bias_part = jnp.sum(cot_mine.astype(F32), axis=0)
+    hidden = after(hidden, grad_two_all)
+    down_local = dot_tn(cot_all, hidden).astype(BF)
+    down_sums = plane_sum(down_local)
+    feed = dot_nt(hidden, down_full).astype(BF)
     grad_crossed = dot_nn(grad_two_all, cross_out_full).astype(BF)
     grad_cross_q, grad_context = cross_attention_back(
         cross_q, context, mask, grad_crossed, cross_logs
     )
-    grad_normed_two = group_scatter(dot_nt(grad_cross_q, cross_query_full).astype(BF))
     context_grad = dot_tn(item_prompt, grad_context).astype(BF).reshape(side_full.shape[0], -1)
     cross_out_grad = dot_tn(grad_two_all, crossed).astype(BF)
     cross_query_grad = dot_tn(normed_two_all, grad_cross_q).astype(BF)
-    cross_grads = plane_scatter(
-        jnp.concatenate([cross_query_grad, cross_out_grad, context_grad], axis=1), pair
-    )
-    grad_norm, cross_gain_part, cross_bias_part = norm_back_rows(
-        grad_normed_two, scaled_two, inverse_two, gain_two
-    )
-    grad_one = (grad_two.astype(F32) + grad_norm).astype(BF)
-    grad_one_all = group_gather(grad_one)
+    cross_local = jnp.concatenate([cross_query_grad, cross_out_grad, context_grad], axis=1)
+    grad_one_all, cross_sums, gate_near, gate_far, feed_near = exchange(
+        "back",
+        3,
+        after(grad_cross_q, down_local, feed),
+        cross_query_full,
+        residual_one,
+        grad_two_all[:half_rows],
+        cross_gain,
+        load=Loads((Return, gate_sums), (SwapCore, feed[half_rows:])),
+    )
+    feed_half = feed[:half_rows].astype(F32) + feed_near.astype(F32)
+    feed_here = jnp.where(odd, feed_half[rows:], feed_half[:rows])
+    feed_away = jnp.where(odd, feed_half[:rows], feed_half[rows:]).astype(BF)
     grad_attended = dot_nn(grad_one_all, self_out_full).astype(BF)
-    grad_projected = self_attention_back(
-        queries, keys, values, grad_attended, self_logs, tables
-    )
-    grad_normed_one = group_scatter(dot_nt(grad_projected, qkv_full).astype(BF))
-    self_out_grad = plane_scatter(dot_tn(grad_one_all, attended).astype(BF), pair)
-    qkv_grad = plane_scatter(dot_tn(normed_one, grad_projected).astype(BF), pair)
-    _, scaled_one, inverse_one = layer_norm(residual_mine, gain_one, bias_one)
-    grad_norm, self_gain_part, self_bias_part = norm_back_rows(
-        grad_normed_one, scaled_one, inverse_one, gain_one
-    )
-    grad_in = (grad_one.astype(F32) + grad_norm).astype(BF)
-    grad_in = xor_blocks(grad_in, 1, 4, column)
-
-    from_partner = move(grad_in, PARTNER_TO_OWNER)
-    first = jnp.where(core == 0, grad_in, from_partner)
-    second = jnp.where(core == 0, from_partner, grad_in)
-    half = jnp.concatenate([first, second], axis=0)
-    far_half = move(half, OWNER_TO_PAIR)
-    own_z = move(half, OWNER_Z)
-    here = jnp.where(owner, half, far_half)
-    there = jnp.where(owner, own_z, move(far_half, PARTNER_Z))
-    even = jnp.where((z & 1) == 0, here, there)
-    odd = jnp.where((z & 1) == 0, there, here)
-    whole = jnp.concatenate([even[:rows], odd[:rows], even[rows:], odd[rows:]], axis=0)
+    grad_projected, up_near, up_far, feed_far = self_attention_back(
+        7,
+        queries,
+        keys,
+        values,
+        grad_attended,
+        self_logs,
+        tables,
+        Loads((Return, up_sums), (SwapNear, feed_away)),
+    )
+    residual_here = jnp.where(odd, residual_two[rows:], residual_two[:rows])
+    output_here = (residual_here + feed_here + feed_far.astype(F32) + down_bias).astype(BF)
+    cross_total = plane_sum(cross_local)
+    self_out_local = dot_tn(grad_one_all, attended).astype(BF)
+    self_out_total = plane_sum(after(self_out_local, cross_total))
+    qkv_local = dot_tn(normed_one, grad_projected).astype(BF)
+    qkv_total = plane_sum(qkv_local)
+    side_total = jnp.concatenate([cross_total, self_out_total], axis=1)
+    grad_in, self_sums, down_near, down_far, side_near, side_far, output_far = exchange(
+        "half",
+        4,
+        after(grad_projected, qkv_local),
+        qkv_full,
+        residual_mine,
+        grad_one_all[:half_rows],
+        self_gain,
+        load=Loads((Return, down_sums), (Return, side_total), (SwapRoute, output_here)),
+    )
+    whole, token_rows, qkv_near, qkv_far = spread_gradient(
+        8, grad_in, Loads((Return, qkv_total))
+    )
+    output = jnp.where(owner, output_here, output_far)
     latents_grad = whole[1:]
 
-    token_rows = whole[:1]
-    steps = timesteps
-    for pairs in (SWAP_CORE, SWAP_X, SWAP_Y):
-        token_rows = jnp.concatenate([token_rows, move(token_rows, pairs)], axis=0)
-        steps = jnp.concatenate([steps, move(steps, pairs)], axis=0)
-    all_features = time_features(steps, feature_width).astype(BF)
+    token_rows = token_rows.reshape(8, 16, -1)[:, 0]
+    all_features = time_features(facts_full[:, 1], feature_width).astype(BF)
     my_features = jnp.zeros((8, feature_width // 8), F32)
     for j in range(8):
         piece = all_features[:, j * (feature_width // 8) : (j + 1) * (feature_width // 8)]
@@ -1072,45 +2062,46 @@
         my_features.astype(BF), token_rows, (((0,), (0,)), ((), ())), preferred_element_type=F32
     )
 
-    parts = jnp.stack(
+    sums = jnp.concatenate(
         [
-            self_gain_part,
-            self_bias_part,
-            cross_gain_part,
-            cross_bias_part,
-            feed_gain_part,
-            feed_bias_part,
-            down_bias_part,
-        ]
-    )
-    block = width // 4
-    got = move(jnp.concatenate([parts[:, block : 2 * block], parts[:, 3 * block :]], axis=1), SWAP_X)
-    keep = jnp.concatenate([parts[:, :block], parts[:, 2 * block : 3 * block]], axis=1) + got
-    mine = keep[:, :block] + move(keep[:, block:], SWAP_Y)
-    low_half, high_half = mine[:, : block // 2], mine[:, block // 2 :]
-    other = move(jnp.where(core == 0, high_half, low_half), SWAP_CORE)
-    mine = jnp.where(core == 0, low_half, high_half) + other
-    mine = mine + move(mine, SWAP_Z)
-    mine = mine + move(mine, SWAP_PAIR)
-
+            jnp.sum(self_sums, axis=1),
+            jnp.sum(cross_sums, axis=1),
+            jnp.sum(feed_sums, axis=1),
+            down_bias_part[None],
+        ],
+        axis=0,
+    )
+    sums = xor_blocks(sums, 1, 8, d)
+    for pairs in (SWAP_Y, SWAP_X, SWAP_CORE):
+        middle = sums.shape[1] // 2
+        sums = sums[:, :middle] + move(sums[:, middle:], pairs)
+    sums = sums + move(sums, SWAP_PAIR)
+
+    side_grads = returned(side_total, side_near, side_far, core, owner)
+    qkv_grad = returned(qkv_total, qkv_near, qkv_far, core, owner)
+    gate_grad = returned(gate_sums, gate_near, gate_far, core, owner)
+    up_grad = returned(up_sums, up_near, up_far, core, owner)
+    down_grad = returned(down_sums, down_near, down_far, core, owner)
     return (
         output[None],
         latents_grad[None],
         time_grad,
-        mine[0],
-        mine[1],
+        sums[0],
+        sums[1],
         qkv_grad.reshape(qkv_weight.shape),
-        self_out_grad.T,
-        mine[2],
-        mine[3],
-        cross_grads[:, :n],
-        cross_grads[:, 2 * n :].reshape(context_weight.shape),
-        cross_grads[:, n : 2 * n].T,
-        mine[4],
-        mine[5],
-        gate_up_grad.reshape(gate_up_weight.shape),
+        side_grads[:, 2 * n + context_weight.size // part_rows :].T,
+        sums[2],
+        sums[3],
+        side_grads[:, :n],
+        side_grads[:, 2 * n : 2 * n + context_weight.size // part_rows].reshape(
+            context_weight.shape
+        ),
+        side_grads[:, n : 2 * n].T,
+        sums[4],
+        sums[5],
+        jnp.stack([gate_grad, up_grad], axis=1),
         down_grad.T,
-        mine[6],
+        sums[6],
     )
 
 

time: 938 us -> 791 us (0.84)
  Pallas kernels: 70.5 us -> 584 us
  waiting for transfers between devices: 371 us -> 21 us
  starting transfers between devices: 188 us -> 8.3 us
  matrix products: 142 us -> 69.9 us
  other arithmetic: 89 us -> 35.2 us
  local copies, waits for them, and re-layouts: 60.5 us -> 48.7 us
  between operations: 5.48 us -> 17.1 us
    pallas_call x2 -> x10, Pallas kernels: 32.4 us -> 540 us  [the longest x5 321 us: exchange(): pl.pallas_call(functools.partial(exchange_kernel, kind, chunks, load), in...]
    ppermute x99 -> x7, waiting for transfers between devices: 371 us -> 5.41 us  [move(): return lax.ppermute(values, AXES, pairs)]
    ppermute x99 -> x7, starting transfers between devices: 188 us -> 7.31 us  [move(): return lax.ppermute(values, AXES, pairs)]
    dot_general x8 -> x5, matrix products: 57.3 us -> 15.1 us  [dot_nn(): lax.dot_general(left, right, (((1,), (0,)), ((), ())), preferred_element_...]
    dot_general x6 -> x1, matrix products: 39.6 us -> 7.62 us  [dot_nt(): lax.dot_general(left, right, (((1,), (1,)), ((), ())), preferred_element_...]
    reduce_scatter x0 -> x5, waiting for transfers between devices: none -> 14.9 us  [plane_sum(): lax.psum_scatter(grad, 'dp', scatter_dimension=0, tiled=True, axis_index_...]
    unnamed x10 -> x0, other arithmetic: 13.7 us -> none
    unnamed x216 -> x86, local copies, waits for them, and re-layouts: 26.6 us -> 12.9 us
  transfers between devices with their start and end apart: 99 -> 14, of which waited for: 40 -> 4; matrix products, arithmetic and copies ran while one was open for 24% -> 15% of each run, Pallas kernels for 5% -> 55%
where the time goes in v2:
time: 791 us; the launch traced here: 784 us
  Pallas kernels  584 us (74%)
  matrix products  69.9 us (9%)
  local copies, waits for them, and re-layouts  48.7 us (6%)
  other arithmetic  35.2 us (4%)
  waiting for transfers between devices  21 us (3%)
  between operations  17.1 us (2%)
  starting transfers between devices  8.3 us (1%)
    pallas_call x5, Pallas kernels, exchange(): pl.pallas_call(functools.partial(exchange_kernel, kind, chunks, load), in...  321 us
    pallas_call x1, Pallas kernels, spread_gradient(): pl.pallas_call(functools.partial(spread_kernel, load, chunks), in_specs=[...  72.8 us
    pallas_call x1, Pallas kernels, self_attention(): pl.pallas_call(functools.partial(self_attention_kernel, load), grid=(pair...  60.7 us
    pallas_call x1, Pallas kernels, front(): pl.pallas_call(front_kernel, in_specs=[place] * 6, out_specs=[place] * 6,...  52.2 us
    dot_general x7, matrix products, dot_tn(): lax.dot_general(left, right, (((0,), (0,)), ((), ())), preferred_element_...  46.2 us
    pallas_call x1, Pallas kernels, self_attention_back(): pl.pallas_call(functools.partial(attention_backward_kernel, HD, 256, True...  36.3 us
    pallas_call x1, Pallas kernels, feed_forward(): pl.pallas_call(feed_kernel, grid=(steps,), in_specs=[fixed, fixed, pl.Blo...  26.3 us
  transfers between devices with their start and end apart: 14, of which 4 were waited for; matrix products, arithmetic and copies ran while one was open for 15% of the time, Pallas kernels for 55%

profile of v2, /device:TPU:1, one launch (start us, length us, event | category | flops | bytes accessed | tf_op | source)
XLA Modules:
  0.0 783.9 jit_solution(9178712310409465675)
XLA Ops:
  8.2 1.8 copy.58
  11.4 1.9 pad_maximum_fusion.7.side_part
  13.4 52.2 %front.1 = (bf16[1536,1152]{1,0:T(8,128)(2,1)}, bf16[384,1536]{1,0:T(8,128)(2,1)}, bf16[1023,1536]{1,0:T(8,128)(2,1)}, bf16[128,768]{1,0:T(8,128)(2,1)}, bf16[256,1536]{1,0:T(8,128)(2,1)}, /*index=5*/s32[64,128]{1,0:T(8,128)}) custom-call(bf16[192,1152]{1,0:T(8,128)(2,1)} %bitcast.90, bf16[192,1536]{1,0:T(8,128)(2,1)} %pad_maximum_fusion.7.side_part, ...), custom_call_target="tpu_custom_call" | custom-call | bytes 100000000 | tf_op jit(solution)/shard_map/front/pallas_call | solution.py:1822
  69.9 1.2 copy.59
  71.9 1.2 fusion.8
  73.4 1.4 copy-done.1
  74.8 1.3 copy-done.11
  76.5 1.1 slice_select_fusion.1
  77.6 3.4 pad_maximum_fusion.refs_0_
  81.3 60.7 %self_attention.1 = (bf16[1024,1536]{1,0:T(8,128)(2,1)}, bf16[1024,384]{1,0:T(8,128)(2,1)}, bf16[1024,384]{1,0:T(8,128)(2,1)}, bf16[1024,384]{1,0:T(8,128)(2,1)}...) custom-call(f32[1024,1536]{1,0:T(8,128)} %pad_maximum_fusion.refs_0_, ...), custom_call_target="tpu_custom_call" | custom-call | flops 5234491392 | bytes 100000000 | tf_op jit(solution)/shard_map/self_attention/pallas_call | solution.py:769
  142.1 2.1 collective-permute-start
  145.5 5.2 fusion.40
  150.7 65.7 %exchange_norm.2 = (f32[512,1536]{1,0:T(8,128)}, bf16[1024,1536]{1,0:T(8,128)(2,1)}, bf16[384,1536]{1,0:T(8,128)(2,1)}) custom-call(bf16[1024,384]{1,0:T(8,128)(2,1)} %get-tuple-element.101.refs_0_, bf16[1536,384]{1,0:T(8,128)(2,1)} %get-tuple-element.202.refs_1_, f32[512,1536]{1,0:T(8,128)} %copy-done, f32[1,1536]{1,0:T(1,128)} %broadcast_in_dim.70.refs_3_.refs_4_, ...), custom_call_target="tpu_custom_call" | custom-call | flops 1207959552 | bytes 100000000 | tf_op jit(solution)/shard_map/exchange_norm/pallas_call | solution.py:1409
  216.5 1.3 fusion.12.bias_ref.refs_5_
  218.2 1.0 convolution_convert_fusion.11.k_ref.v_ref.refs_1_.refs_2_
  219.3 4.9 convolution_convert_fusion.10.q_ref.refs_0_
  224.1 6.4 cross_attention.1
  230.6 5.0 collective-permute-done.1
  235.6 1.3 broadcast_select_fusion.1
  236.9 1.3 pad_maximum_fusion.6.refs_3_
  238.2 1.0 collective-permute-start.2
  240.4 48.4 %exchange_norm.3 = (f32[512,1536]{1,0:T(8,128)}, bf16[1024,1536]{1,0:T(8,128)(2,1)}, bf16[1536,1536]{1,0:T(8,128)(2,1)}) custom-call(bf16[1024,384]{1,0:T(8,128)(2,1)} %get-tuple-element.105.refs_0_, bf16[1536,384]{1,0:T(8,128)(2,1)} %get-tuple-element.200.refs_1_, f32[512,1536]{1,0:T(8,128)} %get-tuple-element.106.refs_2_, ...), custom_call_target="tpu_custom_call" | custom-call | flops 1207959552 | bytes 100000000 | tf_op jit(solution)/shard_map/exchange_norm/pallas_call | solution.py:1409
  288.8 3.4 pad_maximum_fusion.3.cot_ref
  292.1 26.3 %feed_forward.1 = (bf16[1024,1536]{1,0:T(8,128)(2,1)}, bf16[1024,3072]{1,0:T(8,128)(2,1)}) custom-call(bf16[1024,1536]{1,0:T(8,128)(2,1)} %get-tuple-element.109.n_ref, bf16[1024,1536]{1,0:T(8,128)(2,1)} %pad_maximum_fusion.3.cot_ref, bf16[1536,3072]{1,0:T(8,128)(2,1)} %all-gather.5.cloned.1.call-done.gate_ref.up_ref.refs_1_, ...), custom_call_target="tpu_custom_call" | custom-call | flops 14495514624 | bytes 30000000 | tf_op jit(solution)/shard_map/feed_forward/pallas_call | solution.py:1590
  318.5 15.3 %convolution_convert_fusion = bf16[1536,3072]{1,0:T(8,128)(2,1)} fusion(bf16[1024,1536]{1,0:T(8,128)(2,1)} %get-tuple-element.109.n_ref, bf16[1024,3072]{1,0:T(8,128)(2,1)} %get-tuple-element.118.refs_0_), kind=kOutput, calls=%fused_computation | convolution fusion | flops 9668395008 | bytes 18874368 | tf_op jit(solution)/shard_map/dot_general | solution.py:884
  334.0 57.2 %exchange_back.2 = (bf16[1024,1536]{1,0:T(8,128)(2,1)}, f32[2,8,1536]{2,1,0:T(8,128)}) custom-call(bf16[1024,3072]{1,0:T(8,128)(2,1)} %get-tuple-element.118.refs_0_, bf16[1536,3072]{1,0:T(8,128)(2,1)} %all-gather.5.cloned.1.call-done.gate_ref.up_ref.refs_1_, f32[512,1536]{1,0:T(8,128)} %get-tuple-element.108.refs_2_, ...), custom_call_target="tpu_custom_call" | custom-call | flops 9663676416 | bytes 100000000 | tf_op jit(solution)/shard_map/exchange_back/pallas_call | solution.py:1409
  391.3 4.9 convolution_convert_fusion.9.refs_3_
  396.2 7.5 cross_attention_back.1
  403.7 2.5 convolution_convert_fusion.7
  406.2 2.3 reshape.176
  408.5 4.3 convolution_convert_fusion.5
  412.9 1.9 convolution_convert_fusion.6
  414.7 2.0 pad_maximum_fusion.1
  417.3 2.8 slice.229.refs_3_
  420.1 7.6 convolution_convert_fusion.3
  427.7 1.7 copy-done.9
  429.4 1.3 slice.283.refs_6_
  430.7 8.3 %convolution_convert_fusion.2 = bf16[1536,1536]{1,0:T(8,128)(2,1)} fusion(bf16[1024,1536]{1,0:T(8,128)(2,1)S(1)} %copy-done.40, bf16[512,1536]{1,0:T(8,128)(2,1)} %collective-permute-done.2, bf16[256,1536]{1,0:T(8,128)(2,1)S(1)} %get-tuple-element.208, bf16[256,1536]{1,0:T(8,128)(2,1)S(1)} %get-tuple-element.207), kind=kOutput, calls=%fused_computation.2 | convolution fusion | flops 4843634688 | bytes 11010048 | tf_op jit(solution)/shard_map/dot_general | solution.py:884
  439.0 3.2 fusion.41
  442.2 61.8 %exchange_back.3 = (bf16[1024,1536]{1,0:T(8,128)(2,1)}, f32[2,8,1536]{2,1,0:T(8,128)}, bf16[192,1536]{1,0:T(8,128)(2,1)}, bf16[192,1536]{1,0:T(8,128)(2,1)}, bf16[512,1536]{1,0:T(8,128)(2,1)}) custom-call(bf16[1024,384]{1,0:T(8,128)(2,1)} %get-tuple-element.123.refs_0_, bf16[1536,384]{1,0:T(8,128)(2,1)} %get-tuple-element.199.refs_1_, ...), custom_call_target="tpu_custom_call" | custom-call | flops 1207959552 | bytes 100000000 | tf_op jit(solution)/shard_map/exchange_back/pallas_call | solution.py:1409
  504.0 4.9 convolution_convert_fusion.4
  509.5 1.2 copy-done.18
  510.7 4.1 convolution_convert_fusion.8.refs_3_
  515.3 1.0 select_convert_fusion.1.refs_9_
  516.3 36.3 %self_attention_back.1 = (bf16[1024,1152]{1,0:T(8,128)(2,1)}, bf16[192,1536]{1,0:T(8,128)(2,1)}, bf16[192,1536]{1,0:T(8,128)(2,1)}, bf16[256,1536]{1,0:T(8,128)(2,1)}) custom-call(bf16[1024,384]{1,0:T(8,128)(2,1)} %get-tuple-element.125.refs_0_, bf16[1024,384]{1,0:T(8,128)(2,1)} %get-tuple-element.126.refs_1_, bf16[1024,384]{1,0:T(8,128)(2,1)} %get-tuple-element.127.refs_2_, ...), custom_call_target="tpu_custom_call" | custom-call | flops 4026531840 | bytes 100000000 | tf_op jit(solution)/shard_map/self_attention_back/pallas_call | solution.py:798
  552.6 9.1 %convolution_convert_fusion.1 = bf16[1536,1152]{1,0:T(8,128)(2,1)} fusion(bf16[1024,1536]{1,0:T(8,128)(2,1)} %get-tuple-element.132, bf16[1024,1152]{1,0:T(8,128)(2,1)} %get-tuple-element.133.refs_0_), kind=kOutput, calls=%fused_computation.1 | convolution fusion | flops 3625648128 | bytes 9043968 | tf_op jit(solution)/shard_map/dot_general | solution.py:884
  562.5 1.7 convert_reduce_fusion
  564.9 2.3 constant_dynamic-update-slice_fusion.1
  567.2 2.7 slice.235.refs_3_
  570.6 3.2 copy.52
  574.5 3.7 add_convert_fusion.refs_7_
  578.2 1.8 constant_dynamic-update-slice_fusion.refs_6_
  580.0 14.9 %reduce-scatter.8.cloned.1.call-done.refs_5_ = bf16[384,1536]{1,0:T(8,128)(2,1)} async-done(((bf16[1536,1536]{1,0:T(8,128)(2,1)}), bf16[384,1536]{1,0:T(8,128)(2,1)}) %reduce-scatter.8.cloned.1.call-update) | async-done | bytes 1179664 | tf_op jit(solution)/shard_map/reduce_scatter | solution.py:912
  595.0 88.2 %exchange_half.1 = (bf16[512,1536]{1,0:T(8,128)(2,1)}, f32[2,8,1536]{2,1,0:T(8,128)}, bf16[192,1536]{1,0:T(8,128)(2,1)}, bf16[192,1536]{1,0:T(8,128)(2,1)}, bf16...) custom-call(bf16[1024,1152]{1,0:T(8,128)(2,1)} %get-tuple-element.133.refs_0_, ...), custom_call_target="tpu_custom_call" | custom-call | flops 3623878656 | bytes 100000000 | tf_op jit(solution)/shard_map/exchange_half/pallas_call | solution.py:1409
  683.2 1.7 reduce_sum.36
  685.9 1.1 collective-permute-start.3
  686.9 1.6 convert_add_fusion.1
  688.7 1.0 collective-permute-start.4
  689.7 1.3 add_bitcast_fusion
  692.5 2.0 collective-permute-start.6
  696.9 72.8 %spread_gradient.1 = (bf16[1024,1536]{1,0:T(8,128)(2,1)}, bf16[128,1536]{1,0:T(8,128)(2,1)}, bf16[192,1152]{1,0:T(8,128)(2,1)}, bf16[192,1152]{1,0:T(8,128)(2,1)}) custom-call(bf16[512,1536]{1,0:T(8,128)(2,1)} %get-tuple-element.137.refs_0_, bf16[384,1152]{1,0:T(8,128)(2,1)} %reduce-scatter.14.cloned.1.call-done.refs_1_), custom_call_target="tpu_custom_call" | custom-call | bytes 100000000 | tf_op jit(solution)/shard_map/spread_gradient/pallas_call | solution.py:1536
  769.8 1.8 convert_add_fusion.2
  773.5 2.4 slice_bitcast_fusion
  775.9 1.0 fusion.14
  (171 shorter events, 20.9 us)
Async XLA Ops:
  7.2 138.3 %all-gather.3.cloned.1.call-start = ((), (), s32[]{:S(2)}) async-start(), calls=%async_computation.5 | async-start | bytes 5898240 | tf_op jit(solution)/shard_map/all_gather | solution.py:908
  11.4 1.9 copy-start.29
  65.6 226.5 %all-gather.5.cloned.1.call-start = ((), (), s32[]{:S(2)}) async-start(), calls=%async_computation.6 | async-start | bytes 11796480 | tf_op jit(solution)/shard_map/all_gather | solution.py:908
  68.4 0.9 copy-start.32
  68.4 1.5 copy-start.14
  68.8 2.3 copy-start.33
  71.7 1.5 copy-start.19
  71.8 3.0 copy-start.1
  71.8 4.3 copy-start.11
  77.6 3.7 copy-start
  81.3 60.8 %copy-start.39 = (bf16[1,256,1536]{2,1,0:T(8,128)(2,1)S(1)}, bf16[1,256,1536]{2,1,0:T(8,128)(2,1)}, u32[]{:S(2)}) copy-start(bf16[1,256,1536]{2,1,0:T(8,128)(2,1)} %param.43) | copy-start | bytes 2359300
  81.3 62.9 %copy-start.34 = (f32[1536]{0:T(1024)S(1)}, f32[1536]{0:T(1024)}, u32[]{:S(2)}) copy-start(f32[1536]{0:T(1024)} %param.33) | copy-start | bytes 18436
  81.3 63.5 %copy-start.35 = (f32[1536]{0:T(1024)S(1)}, f32[1536]{0:T(1024)}, u32[]{:S(2)}) copy-start(f32[1536]{0:T(1024)} %param.34) | copy-start | bytes 18436
  142.0 296.9 %reduce-scatter.6.cloned.1.call-start = ((), (), s32[]{:S(2)}) async-start(), calls=%async_computation.7 | async-start | bytes 11796480 | tf_op jit(solution)/shard_map/reduce_scatter | solution.py:912
  142.1 74.3 %collective-permute-start = (bf16[256,1536]{1,0:T(8,128)(2,1)S(1)}, bf16[256,1536]{1,0:T(8,128)(2,1)S(1)}, u32[]{:S(2)}, u32[]{:S(2)}) collective-permute-start(bf16[256,1536]{1,0:T(8,128)(2,1)S(1)} %bitcast.109), channel_id=1, source_target_pairs={{0,0},{1,1},{2,4},{3,5},{4,2},{5,3},{6,6},{7,7},{8,8},{9,9},{10,12... | collective-permute-start | bytes 2359304 | tf_op jit(solution)/shard_map/ppermute | solution.py:547
  150.7 67.5 %copy-start.12 = (bf16[1,128,768]{2,1,0:T(8,128)(2,1)S(1)}, bf16[1,128,768]{2,1,0:T(8,128)(2,1)}, u32[]{:S(2)}) copy-start(bf16[1,128,768]{2,1,0:T(8,128)(2,1)} %param.25) | copy-start | bytes 589828
  150.7 67.5 %copy-start.20 = (bf16[128,768]{1,0:T(8,128)(2,1)S(1)}, bf16[128,768]{1,0:T(8,128)(2,1)}, u32[]{:S(2)}) copy-start(bf16[128,768]{1,0:T(8,128)(2,1)} %get-tuple-element.104) | copy-start | bytes 589828
  216.4 19.2 %collective-permute-start.1 = (bf16[256,1536]{1,0:T(8,128)(2,1)S(1)}, bf16[256,1536]{1,0:T(8,128)(2,1)}, u32[]{:S(2)}, u32[]{:S(2)}) collective-permute-start(bf16[256,1536]{1,0:T(8,128)(2,1)S(1)} %collective-permute-done), channel_id=1, source_target_pairs={{0,1},{1,0},{2,3},{3,2},{4,5},{5,4},{6,7},{7,6},{8,9},{9,8},{10,11... | collective-permute-start | bytes 2359304 | tf_op jit(solution)/shard_map/ppermute | solution.py:547
  235.6 3.6 copy-start.36
  235.6 4.2 copy-start.37
  236.9 193.8 %copy-start.2 = (bf16[256,1536]{1,0:T(8,128)(2,1)}, bf16[256,1536]{1,0:T(8,128)(2,1)S(1)}, u32[]{:S(2)}) copy-start(bf16[256,1536]{1,0:T(8,128)(2,1)S(1)} %get-tuple-element.207) | copy-start | bytes 2359300
  236.9 193.8 %copy-start.3 = (bf16[256,1536]{1,0:T(8,128)(2,1)}, bf16[256,1536]{1,0:T(8,128)(2,1)S(1)}, u32[]{:S(2)}) copy-start(bf16[256,1536]{1,0:T(8,128)(2,1)S(1)} %get-tuple-element.208) | copy-start | bytes 2359300
  238.2 50.5 %collective-permute-start.2 = (bf16[512,1536]{1,0:T(8,128)(2,1)}, bf16[512,1536]{1,0:T(8,128)(2,1)}, u32[]{:S(2)}, u32[]{:S(2)}) collective-permute-start(bf16[512,1536]{1,0:T(8,128)(2,1)} %pad_maximum_fusion.6.refs_3_), channel_id=1, source_target_pairs={{0,4},{1,5},{2,6},{3,7},{4,0},{5,1},{6,2},{7,3},{8,12},{9,13},{10,... | collective-permute-start | bytes 4718600 | tf_op jit(solution)/shard_map/ppermute | solution.py:547
  333.7 175.1 %reduce-scatter.10.cloned.1.call-start = ((), (), s32[]{:S(2)}) async-start(), calls=%async_computation.9 | async-start | bytes 4423680 | tf_op jit(solution)/shard_map/reduce_scatter | solution.py:912
  408.5 4.4 copy-start.17
  408.5 4.4 copy-start.38
  416.7 161.5 %reduce-scatter.12.cloned.1.call-start = ((), (), s32[]{:S(2)}) async-start(), calls=%async_computation.10 | async-start | bytes 1474560 | tf_op jit(solution)/shard_map/reduce_scatter | solution.py:912
  417.3 2.8 copy-start.40
  427.7 1.7 copy-start.9
  442.2 61.8 %copy-start.15 = (bf16[1024,384]{1,0:T(8,128)(2,1)S(1)}, bf16[1024,384]{1,0:T(8,128)(2,1)}, u32[]{:S(2)}) copy-start(bf16[1024,384]{1,0:T(8,128)(2,1)} %get-tuple-element.101.refs_0_) | copy-start | bytes 2359300
  508.8 1.9 copy-start.18
  508.9 86.1 %reduce-scatter.8.cloned.1.call-start = ((), (), s32[]{:S(2)}) async-start(), calls=%async_computation.8 | async-start | bytes 5898240 | tf_op jit(solution)/shard_map/reduce_scatter | solution.py:912
  509.4 187.5 %reduce-scatter.14.cloned.1.call-start = ((), (), s32[]{:S(2)}) async-start(), calls=%async_computation.11 | async-start | bytes 4423680 | tf_op jit(solution)/shard_map/reduce_scatter | solution.py:912
  510.7 4.1 copy-start.10
  510.7 4.1 copy-start.13
  561.7 3.0 copy-start.27
  564.8 5.0 copy-start.4
  564.8 5.0 copy-start.21
  564.8 5.0 copy-start.22
  564.8 5.0 copy-start.25
  564.9 5.0 copy-start.26
  570.6 3.3 copy-start.28
  570.6 3.9 copy-start.30
  580.0 106.9 %copy-start.5 = (bf16[384,1536]{1,0:T(8,128)(2,1)S(1)}, bf16[384,1536]{1,0:T(8,128)(2,1)}, u32[]{:S(2)}) copy-start(bf16[384,1536]{1,0:T(8,128)(2,1)} %constant_dynamic-update-slice_fusion.refs_6_) | copy-start | bytes 3538948
  683.2 6.5 copy-start.7
  683.2 6.5 copy-start.23
  683.2 6.5 copy-start.24
  685.9 2.7 collective-permute-start.3
  686.9 4.4 copy-start.6
  686.9 4.4 copy-start.16
  688.7 2.6 collective-permute-start.4
  691.3 1.2 collective-permute-start.5
  692.5 3.8 collective-permute-start.6
  769.7 3.7 copy-start.8
  773.5 2.4 copy-start.31
Sparse Core Ops, SparseCore 0:
  65.7 56.2 all-gather.2
  142.1 93.2 all-gather.4
  333.9 92.0 reduce-scatter.5
  428.9 47.2 reduce-scatter.9
  509.0 26.0 reduce-scatter.11
  538.0 56.9 reduce-scatter.7
  598.0 47.2 reduce-scatter.13

commit v3 on v2

--- a/solution.py
+++ b/solution.py
@@ -3,6 +3,7 @@
 
 import jax
 import jax.numpy as jnp
+import numpy as np
 from jax import lax
 from jax.experimental import pallas as pl
 from jax.experimental.pallas import tpu as pltpu
@@ -597,75 +598,12 @@
     attend_pair(HD, 512, q_ref, k_ref, v_ref, bias_ref, o_ref, log_ref)
 
 
-def self_attention_kernel(load, *refs):
-    res_ref, gain_ref, bias_ref, w_ref, cos_ref, low_ref, high_ref, part_ref = refs[:8]
-    n_ref, q_ref, k_ref, v_ref, o_ref, log_ref, own_ref = refs[8:15]
-    projected = refs[15]
-    here = pl.program_id(0)
-    place = Place()
-    carried = load.begin(place, [part_ref], [own_ref], refs[16:])
-    length, width = res_ref.shape
-    total = w_ref.shape[1]
-    block = 256
-
-    @pl.when(here == 0)
-    def _():
-        greet(load.peers(place, [place.core_peer]))
-        for each in carried:
-            each.start()
-
-        @pl.loop(0, length // 16)
-        def _(step):
-            rows = pl.ds(pl.multiple_of(step * 16, 16), 16)
-            values = res_ref[rows, :]
-            centered = values - jnp.mean(values, axis=-1, keepdims=True)
-            inverse = lax.rsqrt(jnp.mean(centered * centered, axis=-1, keepdims=True) + EPS)
-            n_ref[rows, :] = (centered * inverse * gain_ref[...] + bias_ref[...]).astype(BF)
-
-        for part in range(3):
-            columns = pl.ds(part * (total // 3), total // 3)
-
-            @pl.loop(0, length // block)
-            def _(step):
-                rows = pl.ds(pl.multiple_of(step * block, block), block)
-                projected[rows, columns] = jnp.dot(
-                    n_ref[rows, :], w_ref[:, columns], preferred_element_type=F32
-                )
-
-    half = HD // 4
-
-    def turn(first, target):
-        columns = pl.ds(pl.multiple_of(first + here * 128, 128), 128)
-
-        @pl.loop(0, length // block)
-        def _(step):
-            rows = pl.ds(pl.multiple_of(step * block, block), block)
-            values = projected[rows, columns]
-            target[rows, :] = (
-                values * cos_ref[rows, :]
-                + pltpu.roll(values, 128 - half, 1) * low_ref[rows, :]
-                + pltpu.roll(values, half, 1) * high_ref[rows, :]
-            ).astype(BF)
-
-    turn(0, q_ref)
-    turn(total // 3, k_ref)
-    v_ref[...] = projected[
-        :, pl.ds(pl.multiple_of(2 * (total // 3) + here * 128, 128), 128)
-    ].astype(BF)
-    attend_pair(HD, block, q_ref, k_ref, v_ref, None, o_ref, log_ref)
-
-    @pl.when(here == pl.num_programs(0) - 1)
-    def _():
-        for each in carried:
-            each.finish()
-
-
 def attention_backward_kernel(head_size, query_block, turned, load, *refs):
     if turned:
         refs = list(refs)
-        q_ref, k_ref, v_ref, d_ref, log_ref, cos_ref, low_ref, high_ref = refs[:8]
+        q_ref, k_ref, v_ref, d_ref, log_ref, base_ref, steps_ref = refs[:7]
         more = (len(load.operands), len(load.outs_like))
-        refs = refs[8:]
+        refs = refs[7:]
         load_ins, g_ref, refs = refs[: more[0]], refs[more[0]], refs[more[0] + 1 :]
         load_outs, refs = refs[: more[1]], refs[more[1] :]
         dk_acc, dv_acc = refs[:2]
@@ -683,7 +621,6 @@
     length, width = q_ref.shape
     key_count = k_ref.shape[0]
     here = pl.program_id(0)
-    half = head_size // 4
     key_rows = k_ref[...]
     value_rows = v_ref[...]
     keys_turned = key_rows.astype(F32).T.astype(BF)
@@ -691,12 +628,10 @@
     dk_acc[...] = jnp.zeros_like(dk_acc)
     dv_acc[...] = jnp.zeros_like(dv_acc)
 
-    def back_turn(values, rows):
-        return (
-            values * cos_ref[rows, :]
-            - pltpu.roll(values, width - half, 1) * low_ref[rows, :]
-            - pltpu.roll(values, half, 1) * high_ref[rows, :]
-        )
+    def back_turn(values, step):
+        blocks = length // query_block
+        index = lax.rem(step + place.core * (blocks // 2), blocks)
+        return turned_block(values, base_ref, steps_ref, index, -1)
 
     @pl.loop(0, length // query_block)
     def _(step):
@@ -732,7 +667,7 @@
         grad_query = jnp.concatenate(parts, axis=0).T * scale
         if turned:
             columns = pl.ds(pl.multiple_of(here * width, width), width)
-            g_ref[rows, columns] = back_turn(grad_query, rows).astype(BF)
+            g_ref[rows, columns] = back_turn(grad_query, step).astype(BF)
         else:
             dq_ref[rows, :] = grad_query.astype(BF)
 
@@ -745,7 +680,7 @@
         @pl.loop(0, key_count // query_block)
         def _(step):
             rows = pl.ds(pl.multiple_of(step * query_block, query_block), query_block)
-            g_ref[rows, key_columns] = back_turn(dk_acc[rows, :] * scale, rows).astype(BF)
+            g_ref[rows, key_columns] = back_turn(dk_acc[rows, :] * scale, step).astype(BF)
             g_ref[rows, value_columns] = dv_acc[rows, :].astype(BF)
 
         @pl.when(here == pl.num_programs(0) - 1)
@@ -757,50 +692,18 @@
         g_ref[:, value_columns] = dv_acc[...].astype(BF)
 
 
-def self_attention(place, residual, gain, bias, weight, tables, part):
-    length, width = residual.shape
-    total = weight.shape[1]
-    pairs = total // 3 // 128
-    load = Loads((Spread, part))
-    block = pl.BlockSpec((length, 128), lambda i: (0, i))
-    fixed = pl.BlockSpec((length, 128), lambda i: (0, 0))
-    whole = pl.BlockSpec(memory_space=pltpu.VMEM)
-    wide = jax.ShapeDtypeStruct((length, total // 3), BF)
-    return pl.pallas_call(
-        functools.partial(self_attention_kernel, load),
-        grid=(pairs,),
-        in_specs=[whole] * 4 + [fixed] * 3 + [ANYWHERE],
-        out_specs=[pl.BlockSpec((length, width), lambda i: (0, 0))]
-        + [block] * 4
-        + [pl.BlockSpec((1, 2, length), lambda i: (i, 0, 0)), ANYWHERE],
-        out_shape=[jax.ShapeDtypeStruct((length, width), BF)]
-        + [wide] * 4
-        + [jax.ShapeDtypeStruct((pairs, 2, length), F32)]
-        + load.outs_like,
-        scratch_shapes=[pltpu.VMEM((length, total), F32)] + load.scratch,
-        compiler_params=pltpu.CompilerParams(
-            collective_id=place, has_side_effects=True, vmem_limit_bytes=60 * 2**20
-        ),
-        cost_estimate=pl.CostEstimate(
-            flops=4 * length * length * total // 3 + 2 * length * width * total,
-            transcendentals=length * length * total // 192,
-            bytes_accessed=100_000_000,
-        ),
-        name="self_attention",
-    )(residual, gain[None], bias[None], weight, *tables, part)
-
-
-def self_attention_back(place, queries, keys, values, grads, logs, tables, load):
+def self_attention_back(place, queries, keys, values, grads, logs, load):
     length, total = queries.shape
     pairs = total // 128
     block = pl.BlockSpec((length, 128), lambda i: (0, i))
-    fixed = pl.BlockSpec((length, 128), lambda i: (0, 0))
+    whole = pl.BlockSpec(memory_space=pltpu.VMEM)
+    tables = turn_tables(length, 256)
     return pl.pallas_call(
         functools.partial(attention_backward_kernel, HD, 256, True, load),
         grid=(pairs,),
         in_specs=[block] * 4
         + [pl.BlockSpec((1, 2, length), lambda i: (i, 0, 0))]
-        + [fixed] * 3
+        + [whole] * 2
         + [ANYWHERE] * len(load.operands),
         out_specs=[pl.BlockSpec((length, 3 * total), lambda i: (0, 0))]
         + [ANYWHERE] * len(load.outs_like),
@@ -1215,6 +1118,16 @@
     way = "core"
 
 
+class SwapCoreHalf(SwapCore):
+    @staticmethod
+    def outs(values):
+        return [jax.ShapeDtypeStruct((values.shape[0] // 2,) + values.shape[1:], values.dtype)]
+
+    def __init__(self, place, ins, outs, sems):
+        rows = outs[0].shape[0]
+        super().__init__(place, [ins[0].at[pl.ds(rows, rows)]], outs, sems)
+
+
 class SwapNear(Swap):
     way = "z"
 
@@ -1253,6 +1166,83 @@
         return result
 
 
+class Works:
+    def __init__(self, *works):
+        self.kinds = [kind for kind, _, _ in works]
+        self.operands = [operand for _, left, right in works for operand in (left, right)]
+        self.unique = []
+        for operand in self.operands:
+            if not any(operand is other for other in self.unique):
+                self.unique.append(operand)
+        self.places = [
+            [at for at, other in enumerate(self.unique) if other is operand][0]
+            for operand in self.operands
+        ]
+        self.outs_like = []
+        for kind, left, right in works:
+            if kind == "nt":
+                shape = (left.shape[0], right.shape[0])
+            else:
+                shape = (left.shape[1], right.shape[1])
+            self.outs_like.append(jax.ShapeDtypeStruct(shape, BF))
+        self.scratch = (
+            [pltpu.VMEM(operand.shape, BF) for operand in self.unique]
+            + [pltpu.VMEM(out.shape, BF) for out in self.outs_like]
+            + [pltpu.SemaphoreType.DMA((max(1, len(self.unique) + len(works)),))]
+        )
+
+    def begin(self, ins, outs, scratch):
+        self_ins = list(scratch[: len(self.unique)])
+        self_outs = list(scratch[len(self.unique) : -1])
+        sems = scratch[-1]
+        loads = [
+            pltpu.make_async_copy(source, target, sems.at[k])
+            for k, (source, target) in enumerate(zip(ins, self_ins))
+        ]
+        stores = [
+            pltpu.make_async_copy(source, target, sems.at[len(loads) + k])
+            for k, (source, target) in enumerate(zip(self_outs, outs))
+        ]
+        return loads, stores, self_ins, self_outs
+
+    def run(self, state):
+        loads, stores, ins, outs = state
+        waited = set()
+        for k, kind in enumerate(self.kinds):
+            pair = self.places[2 * k : 2 * k + 2]
+            for at in pair:
+                if at not in waited:
+                    loads[at].wait()
+                    waited.add(at)
+            left, right, out = ins[pair[0]], ins[pair[1]], outs[k]
+            if kind == "nt":
+                columns = out.shape[1] // 256
+
+                @pl.loop(0, (out.shape[0] // 256) * columns)
+                def _(step):
+                    first = pl.ds(pl.multiple_of((step // columns) * 256, 256), 256)
+                    second = pl.ds(pl.multiple_of(lax.rem(step, columns) * 256, 256), 256)
+                    out[first, second] = lax.dot_general(
+                        left[first, :],
+                        right[second, :],
+                        (((1,), (1,)), ((), ())),
+                        preferred_element_type=F32,
+                    ).astype(BF)
+            else:
+
+                @pl.loop(0, out.shape[0] // 256)
+                def _(step):
+                    spot = pl.ds(pl.multiple_of(step * 256, 256), 256)
+                    out[spot, :] = lax.dot_general(
+                        left[:, spot],
+                        right[...],
+                        (((0,), (0,)), ((), ())),
+                        preferred_element_type=F32,
+                    ).astype(BF)
+
+            stores[k].start()
+
+
 ANYWHERE = pl.BlockSpec(memory_space=pl.ANY)
 
 
@@ -1262,28 +1252,74 @@
     return jnp.where(owner, mine, near).astype(F32) + far.astype(F32)
 
 
-def exchange_kernel(kind, chunks, load, *refs):
+def exchange_kernel(kind, chunks, window, load, works, *refs):
     refs = list(refs)
     place = Place()
     more = (len(load.operands), len(load.outs_like))
-    ins, refs = refs[:5], refs[5:]
+    todo = (len(works.unique), len(works.outs_like), len(works.scratch))
+    w_count = len(refs) - 1 - 4 - more[0] - more[1] - todo[0] - todo[1] - todo[2]
+    w_count -= 2 + 11 + 4 + (kind != "norm") + len(load.scratch) - 1
+    w_from, refs = refs[1 : 1 + w_count], refs[:1] + refs[1 + w_count :]
+    ins, refs = refs[:4], refs[4:]
     load_ins, refs = refs[: more[0]], refs[more[0] :]
+    work_ins, refs = refs[: todo[0]], refs[todo[0] :]
     outs, refs = refs[:2], refs[2:]
     load_outs, refs = refs[: more[1]], refs[more[1] :]
+    work_outs, refs = refs[: todo[1]], refs[todo[1] :]
     rest, refs = refs[:11], refs[11:]
+    (a_ref, w_ref, res_ref, loads), refs = refs[:4], refs[4:]
     if kind == "norm":
-        a_ref, w_ref, res_ref, gain_ref, bias_ref = ins
+        a_from, res_from, gain_ref, bias_ref = ins
         res_out, all_ref = outs
     else:
-        a_ref, w_ref, res_ref, up_ref, gain_ref = ins
+        a_from, res_from, up_from, gain_ref = ins
         all_ref, sum_ref = outs
+        up_ref, refs = refs[0], refs[1:]
     carried = load.begin(place, load_ins, load_outs, refs)
+    working = works.begin(work_ins, work_outs, refs[len(load.scratch) :])
     mine, given, near, half, far, send_near, got_near, send_far, got_far, send_all, got_all = rest
     rows = mine.shape[0]
     width = mine.shape[1]
     chunk = rows // chunks
     core_peer, far_peer = place.core_peer, place.near_z
     copy = send
+    depth = a_ref.shape[1]
+    block = 2 * chunk
+    tile = 256
+    tiles = width // tile
+
+    def load_rows(k):
+        first = (k // 2) * block + (0 if k % 2 else rows)
+        spot = pl.ds(first, block)
+        return pltpu.make_async_copy(a_from.at[spot], a_ref.at[spot], loads.at[2 * tiles + k])
+
+    def load_weight(k):
+        spot = pl.ds(k * tile, tile)
+        share = depth // len(w_from)
+        return [
+            pltpu.make_async_copy(
+                source.at[spot, pl.ds(window * depth, share)],
+                w_ref.at[spot, pl.ds(at * share, share)],
+                loads.at[at * tiles + k],
+            )
+            for at, source in enumerate(w_from)
+        ]
+
+    later = [pltpu.make_async_copy(res_from, res_ref, loads.at[2 * tiles + 2 * chunks])]
+    if kind != "norm":
+        later.append(
+            pltpu.make_async_copy(
+                up_from.at[pl.ds(0, rows)], up_ref, loads.at[2 * tiles + 2 * chunks + 1]
+            )
+        )
+    load_rows(0).start()
+    for k in range(tiles):
+        for each in load_weight(k):
+            each.start()
+    for k in range(1, chunks):
+        load_rows(k).start()
+    for each in later + working[0]:
+        each.start()
     greet(load.peers(place, [core_peer, far_peer]))
     for each in carried:
         if not each.late:
@@ -1306,25 +1342,33 @@
             core_peer,
         )
 
-    block = 2 * chunk
-    tile = 256
+    def tile_product(first, target, start, spot):
+        target[pl.ds(start, block), spot] = lax.dot_general(
+            a_ref[pl.ds(first, block), :],
+            w_ref[spot, :],
+            (((1,), (1,)), ((), ())),
+            preferred_element_type=F32,
+        ).astype(target.dtype)
 
     def product(first, target, start):
-        @pl.loop(0, width // tile)
+        @pl.loop(0, tiles)
         def _(step):
-            columns = pl.ds(pl.multiple_of(step * tile, tile), tile)
-            target[pl.ds(start, block), columns] = lax.dot_general(
-                a_ref[pl.ds(first, block), :],
-                w_ref[columns, :],
-                (((1,), (1,)), ((), ())),
-                preferred_element_type=F32,
-            ).astype(target.dtype)
+            spot = pl.ds(pl.multiple_of(step * tile, tile), tile)
+            tile_product(first, target, start, spot)
 
     step_rows = 16
     for m in range(chunks // 2):
-        product(rows + m * block, given, m * block)
+        load_rows(2 * m).wait()
+        if m == 0:
+            for k in range(tiles):
+                for each in load_weight(k):
+                    each.wait()
+                tile_product(rows, given, 0, pl.ds(k * tile, tile))
+        else:
+            product(rows + m * block, given, m * block)
         for k in (2 * m, 2 * m + 1):
             near_copy(k).start()
+        load_rows(2 * m + 1).wait()
         product(m * block, mine, m * block)
         for k in (2 * m, 2 * m + 1):
             near_copy(k).wait_recv()
@@ -1338,6 +1382,9 @@
     for each in carried:
         if each.late:
             each.start()
+    works.run(working)
+    for each in later:
+        each.wait()
     if kind != "norm":
         sum_ref[...] = jnp.zeros_like(sum_ref)
     for k in range(chunks):
@@ -1380,34 +1427,48 @@
             all_copy(k).wait_recv()
     for each in carried:
         each.finish()
-
-
-def exchange(kind, place, a, w, residual, *others, load=Loads()):
+    for each in working[1]:
+        each.wait()
+
+
+def exchange(kind, place, a, w, residual, *others, load=Loads(), window=0, works=Works()):
     length, depth = a.shape
-    width = w.shape[0]
+    w = w if isinstance(w, tuple) else (w,)
+    width = w[0].shape[0]
     rows = length // 2
     chunks = 4
     whole = pl.BlockSpec(memory_space=pltpu.VMEM)
     if kind == "norm":
         gain, bias = others
-        operands = (a, w, residual, gain[None], bias[None])
+        operands = (a, *w, residual, gain[None], bias[None])
         outs = [
             jax.ShapeDtypeStruct((rows, width), F32),
             jax.ShapeDtypeStruct((length, width), BF),
         ]
     else:
         up, gain = others
-        operands = (a, w, residual, up, gain[None])
+        operands = (a, *w, residual, up, gain[None])
         outs = [
             jax.ShapeDtypeStruct((rows if kind == "half" else length, width), BF),
             jax.ShapeDtypeStruct((2, 8, width), F32),
         ]
-    specs = [whole] * 5 + [ANYWHERE] * len(load.operands)
-    out_specs = [whole] * 2 + [ANYWHERE] * len(load.outs_like)
-    operands += tuple(load.operands)
-    outs = outs + load.outs_like
+    plain = 2 if kind == "norm" else 1
+    specs = [ANYWHERE] * (len(operands) - plain) + [whole] * plain
+    specs += [ANYWHERE] * (len(load.operands) + len(works.unique))
+    tiles = width // 256
+    more = [
+        pltpu.VMEM((length, depth), BF),
+        pltpu.VMEM((width, depth), BF),
+        pltpu.VMEM((rows, width), F32),
+        pltpu.SemaphoreType.DMA((2 * tiles + 2 * chunks + 2,)),
+    ]
+    if kind != "norm":
+        more.append(pltpu.VMEM((rows, width), BF))
+    out_specs = [whole] * 2 + [ANYWHERE] * (len(load.outs_like) + len(works.outs_like))
+    operands += tuple(load.operands) + tuple(works.unique)
+    outs = outs + load.outs_like + works.outs_like
     return pl.pallas_call(
-        functools.partial(exchange_kernel, kind, chunks, load),
+        functools.partial(exchange_kernel, kind, chunks, window, load, works),
         in_specs=specs,
         out_specs=out_specs,
         out_shape=outs,
@@ -1419,7 +1480,9 @@
             pltpu.VMEM((rows, width), BF),
         ]
         + [pltpu.SemaphoreType.DMA((chunks,))] * 6
-        + load.scratch,
+        + more
+        + load.scratch
+        + works.scratch,
         compiler_params=pltpu.CompilerParams(
             collective_id=place, has_side_effects=True, vmem_limit_bytes=60 * 2**20
         ),
@@ -1435,17 +1498,18 @@
 def spread_kernel(load, chunks, *refs):
     refs = list(refs)
     more = (len(load.operands), len(load.outs_like))
-    half_ref, refs = refs[0], refs[1:]
+    (half_ref, pieces_ref), refs = refs[:2], refs[2:]
     load_ins, refs = refs[: more[0]], refs[more[0] :]
-    (out_ref, token_ref), refs = refs[:2], refs[2:]
+    (out_ref, token_ref, share_ref), refs = refs[:3], refs[3:]
     load_outs, refs = refs[: more[1]], refs[more[1] :]
-    (sent, got, send_token, got_token), refs = refs[:4], refs[4:]
+    (sent, got, send_token, got_token, send_share, got_share), refs = refs[:6], refs[6:]
     place = Place()
     carried = load.begin(place, load_ins, load_outs, refs)
     d, core, pair = place.d, place.core, place.pair
     inner_z = lax.rem(place.z, 2)
     plane_peers = [(lax.rem(d + j, 8), place.z) for j in range(1, 8)]
-    greet([place.near_z, place.far_same, place.far_other] + plane_peers)
+    far_peers = [(lax.rem(d + j, 8), place.far_z) for j in range(8)]
+    greet([place.near_z] + far_peers + plane_peers)
     rows = half_ref.shape[0]
     chunk = rows // chunks
 
@@ -1462,14 +1526,26 @@
 
     def pass_copy(k, which):
         return send(spot(which, k), spot(which, k), sent.at[2, k], got.at[2, k], place.near_z)
+
+    def share_copy(far, j):
+        return send(
+            pieces_ref.at[pl.ds(pl.multiple_of(lax.rem(d + j, 8) * 8, 8), 8)],
+            share_ref.at[pl.ds((8 * far + j) * 8, 8)],
+            send_share.at[far, j],
+            got_share.at[far, j],
+            far_peers[j] if far else plane_peers[j - 1],
+        )
+
+    for j in range(8):
+        share_copy(1, j).start()
+        if j:
+            share_copy(0, j).start()
+    share_ref[pl.ds(0, 8), :] = pieces_ref[pl.ds(pl.multiple_of(d * 8, 8), 8), :]
 
     @pl.when(core == inner_z)
     def _():
         for k in range(chunks):
             pair_copy(k, core).start()
-
-    for each in carried:
-        each.start()
 
     @pl.when(core != pair)
     def _():
@@ -1488,11 +1564,22 @@
         for k in range(chunks):
             owner_copy(k, 1 - core).wait_recv()
 
+    def pass_on(k):
+        pair_copy(k, inner_z).wait_recv()
+        pass_copy(k, inner_z).start()
+
     @pl.when(core != pair)
     def _():
-        for k in range(chunks):
-            pair_copy(k, inner_z).wait_recv()
-            pass_copy(k, inner_z).start()
+        for k in range(chunks // 2):
+            pass_on(k)
+
+    for each in carried:
+        each.start()
+
+    @pl.when(core != pair)
+    def _():
+        for k in range(chunks // 2, chunks):
+            pass_on(k)
         for k in range(chunks):
             pass_copy(k, 1 - inner_z).wait_recv()
 
@@ -1525,21 +1612,26 @@
     for j in range(1, 8):
         token_copy(j, d).wait_send()
         token_copy(j, lax.rem(d + 8 - j, 8)).wait_recv()
+    for j in range(8):
+        share_copy(1, j).wait()
+        if j:
+            share_copy(0, j).wait()
     for each in carried:
         each.finish()
 
 
-def spread_gradient(place, half, load):
+def spread_gradient(place, half, pieces, load):
     rows, width = half.shape
     chunks = 4
     whole = pl.BlockSpec(memory_space=pltpu.VMEM)
     return pl.pallas_call(
         functools.partial(spread_kernel, load, chunks),
-        in_specs=[whole] + [ANYWHERE] * len(load.operands),
-        out_specs=[whole] * 2 + [ANYWHERE] * len(load.outs_like),
+        in_specs=[whole] * 2 + [ANYWHERE] * len(load.operands),
+        out_specs=[whole] * 3 + [ANYWHERE] * len(load.outs_like),
         out_shape=[
             jax.ShapeDtypeStruct((2 * rows, width), BF),
             jax.ShapeDtypeStruct((8 * 16, width), BF),
+            jax.ShapeDtypeStruct((2 * pieces.shape[0], pieces.shape[1]), F32),
         ]
         + load.outs_like,
         scratch_shapes=[
@@ -1547,6 +1639,8 @@
             pltpu.SemaphoreType.DMA((3, chunks)),
             pltpu.SemaphoreType.DMA((7,)),
             pltpu.SemaphoreType.DMA((7,)),
+            pltpu.SemaphoreType.DMA((2, 8)),
+            pltpu.SemaphoreType.DMA((2, 8)),
         ]
         + load.scratch,
         compiler_params=pltpu.CompilerParams(
@@ -1554,7 +1648,7 @@
         ),
         cost_estimate=pl.CostEstimate(flops=0, transcendentals=0, bytes_accessed=100_000_000),
         name="spread_gradient",
-    )(half, *load.operands)
+    )(half, pieces, *load.operands)
 
 
 def feed_kernel(n_ref, cot_ref, gate_ref, up_ref, down_ref, hidden_ref, grad_ref):
@@ -1615,239 +1709,387 @@
     )(normed, cot, gate_up, gate_up, down)
 
 
-def front_kernel(
-    qkv_part,
-    side_part,
-    latents,
-    prompt,
-    time_part,
-    facts,
-    qkv_full,
-    side_own,
-    latents_too,
-    prompt_too,
-    time_full,
-    facts_full,
-    send_far,
-    got_far,
-    send_near,
-    got_near,
-    here,
-    send_plane,
-    got_plane,
-    send_swap,
-    got_swap,
-    send_small,
-    got_small,
-):
-    d = lax.axis_index("dp")
-    z = lax.axis_index("mp")
-    core = lax.rem(d, 2)
-    column = d // 2
-    pair = z // 2
-    far_z = z + 2 - 4 * pair
-    core_peer = (d + 1 - 2 * core, z)
-    x_peer = (d + 2 - 4 * lax.rem(column, 2), z)
-    y_peer = (d + 4 - 8 * (column // 2), z)
-    x_column = column + 1 - 2 * lax.rem(column, 2)
-    y_column = column + 2 - 4 * (column // 2)
-    owner = core == pair
-    barrier = pltpu.get_barrier_semaphore()
-    plane_peers = [(lax.rem(d + j, 8), z) for j in range(1, 8)]
-    peers = [(d, far_z), (core_peer[0], far_z)] + plane_peers
-    for peer in peers:
-        pl.semaphore_signal(
-            barrier, inc=1, device_id=peer, device_id_type=pl.DeviceIdType.MESH
-        )
-    pl.semaphore_wait(barrier, len(peers))
+def turn_tables(length, block):
+    rotated = HD // 2
+    angles = np.exp(-np.log(10000.0) * np.arange(rotated // 2) * 2.0 / rotated)
+    lanes = np.concatenate([angles, angles, np.zeros(HD - rotated)])
+    lanes = np.concatenate([lanes, lanes])
+    base = np.arange(block)[:, None] * lanes[None]
+    steps = np.zeros((8, 128))
+    steps[: length // block] = np.arange(0, length, block)[:, None] * lanes[None]
+    pack = lambda table: np.stack([np.cos(table), np.sin(table)]).astype(np.float32)
+    return jnp.asarray(pack(base)), jnp.asarray(pack(steps))
+
+
+def turned_block(values, base_ref, steps_ref, here, sign):
+    half = HD // 4
+    first_cos, first_sin = steps_ref[0, pl.ds(here, 1), :], steps_ref[1, pl.ds(here, 1), :]
+    cosine = first_cos * base_ref[0] - first_sin * base_ref[1]
+    sine = first_sin * base_ref[0] + first_cos * base_ref[1]
+    lane = lax.rem(lax.broadcasted_iota(jnp.int32, values.shape, 1), HD)
+    lower = jnp.where(lane < half, sine, 0.0)
+    upper = jnp.where((lane >= half) & (lane < 2 * half), sine, 0.0)
+    ahead = pltpu.roll(values, 128 - half, 1)
+    behind = pltpu.roll(values, half, 1)
+    if sign > 0:
+        return values * cosine - ahead * lower + behind * upper
+    return values * cosine + ahead * lower - behind * upper
+
+
+def opening_kernel(*refs):
+    (qkv_part, side_part, feed_part, latents, prompt, time_part, feat, facts) = refs[:8]
+    gain_ref, bias_ref, base_ref, steps_ref = refs[8:12]
+    (n_ref, q_ref, k_ref, v_ref, o_ref, log_ref, res_ref, qkv_out) = refs[12:20]
+    side_full, feed_own, prompt_too, facts_too, feat_out = refs[20:25]
+    projected, item, time_full, qkv_full, feat_full = refs[25:30]
+    sent_far, got_far, sent_near, got_near, here = refs[30:35]
+    sent_plane, got_plane, sent_side, got_side = refs[35:39]
+    sent_small, got_small, sent_swap, got_swap = refs[39:43]
+    place = Place()
+    d, core, column, owner = place.d, place.core, place.column, place.owner
+    step_here = pl.program_id(0)
+    plane_peers = [(lax.rem(d + j, 8), place.z) for j in range(1, 8)]
     rows = qkv_part.shape[0]
     piece = rows // 2
-
-    def copy(source, target, send, got, peer):
-        return pltpu.make_async_remote_copy(
-            src_ref=source,
-            dst_ref=target,
-            send_sem=send,
-            recv_sem=got,
-            device_id=peer,
-            device_id_type=pl.DeviceIdType.MESH,
-        )
-
-    def part_copy(k, sender, send, got, peer):
+    length, width = item.shape
+    total = qkv_full.shape[1]
+    block = 256
+    parts = range(4)
+
+    def at(ref, index, count):
+        return ref.at[pl.ds(pl.multiple_of(index * count, count), count)]
+
+    def ends(k, sender):
         if k < 2:
-            return copy(
-                qkv_part.at[pl.ds(k * piece, piece)],
-                qkv_full.at[pl.ds((2 * column + sender) * rows + k * piece, piece)],
-                send,
-                got,
-                peer,
-            )
-        return copy(side_part, side_own.at[pl.ds(sender * rows, rows)], send, got, peer)
-
-    user = 2 * column + pair
-    swaps = [
-        copy(latents, latents_too, send_swap.at[0], got_swap.at[0], core_peer),
-        copy(prompt, prompt_too, send_swap.at[1], got_swap.at[1], core_peer),
-    ]
-    swaps[0].start()
-    far_parts = [
-        part_copy(k, core, send_far.at[k], got_far.at[core, k], (user, far_z)) for k in range(3)
-    ]
-    for part in far_parts:
-        part.start()
-    near_parts = [
-        part_copy(k, core, send_near.at[k], got_near.at[k], core_peer) for k in range(3)
-    ]
-    own_parts = [
-        pltpu.make_async_copy(
-            qkv_part, qkv_full.at[pl.ds((2 * column + core) * rows, rows)], here.at[0]
-        ),
-        pltpu.make_async_copy(side_part, side_own.at[pl.ds(core * rows, rows)], here.at[1]),
-    ]
-
-    @pl.when(owner)
-    def _():
-        for part in own_parts:
-            part.start()
-
-    @pl.when(jnp.logical_not(owner))
-    def _():
-        for part in near_parts:
-            part.start()
-
-    swaps[1].start()
-
-    def small_copies(sender, j, peer):
-        result = []
-        for which, (part, whole) in enumerate(((time_part, time_full), (facts, facts_full))):
-            count = part.shape[0]
-            place = whole.at[pl.ds(sender * count, count)]
-            result.append(
-                copy(part, place, send_small.at[which, j - 1], got_small.at[which, j - 1], peer)
-            )
-        return result
-
-    small_own = [
-        pltpu.make_async_copy(
-            part, whole.at[pl.ds(d * part.shape[0], part.shape[0])], here.at[2 + which]
-        )
-        for which, (part, whole) in enumerate(((time_part, time_full), (facts, facts_full)))
-    ]
-    for part in small_own:
-        part.start()
-    for j in range(1, 8):
-        for part in small_copies(d, j, plane_peers[j - 1]):
-            part.start()
+            source = qkv_part.at[pl.ds(k * piece, piece)]
+            spot = pl.multiple_of((2 * column + sender) * rows + k * piece, piece)
+            return source, qkv_full.at[pl.ds(spot, piece)]
+        if k == 2:
+            return side_part, at(side_full, 2 * column + sender, rows)
+        return feed_part, at(feed_own, sender, rows)
+
+    def far(k, sender):
+        source, target = ends(k, sender)
+        return send(source, target, sent_far.at[k], got_far.at[sender, k], place.user)
+
+    def near(k, sender):
+        source, target = ends(k, sender)
+        return send(source, target, sent_near.at[k], got_near.at[k], place.core_peer)
+
+    def local(k):
+        source, target = ends(k, core)
+        return pltpu.make_async_copy(source, target, here.at[k])
 
     def await_part(k, sender):
         @pl.when(owner)
         def _():
             @pl.when(core == sender)
             def _():
-                if k == 0:
-                    own_parts[0].wait()
-                if k == 2:
-                    own_parts[1].wait()
+                local(k).wait()
 
             @pl.when(core != sender)
             def _():
-                part_copy(k, sender, send_near.at[k], got_near.at[k], core_peer).wait_recv()
+                near(k, sender).wait_recv()
 
         @pl.when(jnp.logical_not(owner))
         def _():
-            part_copy(k, sender, send_far.at[k], got_far.at[sender, k], core_peer).wait_recv()
-
-    def plane_copy(stage, way, k, sender):
-        peer = x_peer if way == 0 else y_peer
-        if stage == 0:
-            source = column
-        else:
-            source = y_column if way == 0 else x_column
-        place = pl.ds((2 * source + sender) * rows + k * piece, piece)
+            far(k, sender).wait_recv()
+
+    item_copy = send(latents, item, sent_swap.at[0], got_swap.at[0], place.core_peer)
+    item_local = pltpu.make_async_copy(latents, item, here.at[4])
+    outward = [
+        pltpu.make_async_copy(qkv_full, qkv_out, here.at[7]),
+        pltpu.make_async_copy(feat_full, feat_out, here.at[8]),
+    ]
+    swaps = [
+        send(prompt, prompt_too, sent_swap.at[1], got_swap.at[1], place.core_peer),
+        send(facts, facts_too, sent_swap.at[2], got_swap.at[2], place.core_peer),
+    ]
+    smalls = ((time_part, time_full), (feat, feat_full))
+
+    def small(which, j, sender):
+        part, whole = smalls[which]
+        return send(
+            part,
+            at(whole, sender, part.shape[0]),
+            sent_small.at[which, j - 1],
+            got_small.at[which, j - 1],
+            plane_peers[j - 1],
+        )
+
+    def small_local(which):
+        part, whole = smalls[which]
+        return pltpu.make_async_copy(part, at(whole, d, part.shape[0]), here.at[5 + which])
+
+    def plane(stage, way, k, sender):
+        peer = place.x_peer if way == 0 else place.y_peer
+        source = column if stage == 0 else (place.y_column if way == 0 else place.x_column)
+        spot = qkv_full.at[
+            pl.ds(pl.multiple_of((2 * source + sender) * rows + k * piece, piece), piece)
+        ]
         slot = 4 * stage + 2 * sender + k
-        return copy(
-            qkv_full.at[place],
-            qkv_full.at[place],
-            send_plane.at[way, slot],
-            got_plane.at[way, slot],
-            peer,
+        return send(spot, spot, sent_plane.at[way, slot], got_plane.at[way, slot], peer)
+
+    def side(stage, way, sender):
+        peer = place.x_peer if way == 0 else place.y_peer
+        source = column if stage == 0 else (place.y_column if way == 0 else place.x_column)
+        spot = at(side_full, 2 * source + sender, rows)
+        slot = 2 * stage + sender
+        return send(spot, spot, sent_side.at[way, slot], got_side.at[way, slot], peer)
+
+    def side_one():
+        for sender in range(2):
+            await_part(2, sender)
+            side(0, sender, sender).start()
+        for sender in range(2):
+            side(0, 1 - sender, sender).start()
+
+    def side_two():
+        side(0, 0, 0).wait_recv()
+        side(1, 1, 0).start()
+        side(0, 1, 1).wait_recv()
+        side(1, 0, 1).start()
+
+    @pl.when(step_here == 0)
+    def _():
+        greet([place.far_same, place.far_other] + plane_peers)
+        for k in parts:
+            far(k, core).start()
+
+        @pl.when(owner)
+        def _():
+            item_copy.start()
+            item_local.start()
+            for k in parts:
+                local(k).start()
+
+        for which in range(2):
+            small_local(which).start()
+        for j in range(1, 8):
+            for which in range(2):
+                small(which, j, d).start()
+
+        @pl.when(jnp.logical_not(owner))
+        def _():
+            for k in parts:
+                near(k, core).start()
+
+        for swap in swaps:
+            swap.start()
+        for which in range(2):
+            small_local(which).wait()
+        for j in range(1, 8):
+            for which in range(2):
+                small(which, j, lax.rem(d + 8 - j, 8)).wait_recv()
+
+        @pl.when(owner)
+        def _():
+            item_local.wait()
+
+        @pl.when(jnp.logical_not(owner))
+        def _():
+            item_copy.wait_recv()
+
+        user = 2 * column + place.pair
+        token_row = jnp.dot(
+            feat_full[pl.ds(pl.multiple_of(user * 16, 16), 16), :],
+            time_full[...],
+            preferred_element_type=F32,
         )
-
-    for k in range(2):
+        row_number = lax.broadcasted_iota(jnp.int32, (16, width), 0)
+
+        def norm_rows(step, keep):
+            local_row = pl.multiple_of(step * 16, 16)
+            spot = pl.multiple_of(lax.rem(local_row + core * (length // 2), length), 16)
+            values = item[pl.ds(spot, 16), :].astype(F32)
+            values = jnp.where(row_number + spot == 0, token_row, values)
+            if keep:
+                res_ref[pl.ds(local_row, 16), :] = values
+            centered = values - jnp.mean(values, axis=-1, keepdims=True)
+            inverse = lax.rsqrt(jnp.mean(centered * centered, axis=-1, keepdims=True) + EPS)
+            n_ref[pl.ds(local_row, 16), :] = (
+                centered * inverse * gain_ref[...] + bias_ref[...]
+            ).astype(BF)
+
+        def forward(k):
+            for sender in range(2):
+                await_part(k, sender)
+                plane(0, 0, k, sender).start()
+                plane(0, 1, k, sender).start()
+
+        steps = length // 16
+        forward(0)
+
+        @pl.loop(0, steps // 2)
+        def _(step):
+            norm_rows(step, True)
+
+        forward(1)
+
+        @pl.loop(steps // 2, steps)
+        def _(step):
+            norm_rows(step, False)
+
+        for k in range(2):
+            plane(0, 0, k, 0).wait_recv()
+            plane(1, 1, k, 0).start()
+            plane(0, 1, k, 1).wait_recv()
+            plane(1, 0, k, 1).start()
+            plane(0, 0, k, 1).wait_recv()
+            plane(0, 1, k, 0).wait_recv()
+        for k in range(2):
+            plane(1, 1, k, 0).wait_recv()
+            plane(1, 0, k, 1).wait_recv()
+
+        side_one()
+
+        for each in outward:
+            each.start()
+        third = total // 3
+        for part in range(3):
+            columns = pl.ds(part * third, third)
+
+            @pl.loop(0, length // block)
+            def _(step):
+                spot = pl.ds(pl.multiple_of(step * block, block), block)
+                projected[spot, columns] = jnp.dot(
+                    n_ref[spot, :], qkv_full[:, columns], preferred_element_type=F32
+                )
+
+    @pl.when(step_here == 1)
+    def _():
+        side_two()
+
+    def turn(first, target):
+        columns = pl.ds(pl.multiple_of(first + step_here * 128, 128), 128)
+
+        @pl.loop(0, length // block)
+        def _(step):
+            spot = pl.ds(pl.multiple_of(step * block, block), block)
+            index = lax.rem(step + core * (length // block // 2), length // block)
+            target[spot, :] = turned_block(
+                projected[spot, columns], base_ref, steps_ref, index, 1
+            ).astype(BF)
+
+    turn(0, q_ref)
+    turn(total // 3, k_ref)
+    v_ref[...] = projected[
+        :, pl.ds(pl.multiple_of(2 * (total // 3) + step_here * 128, 128), 128)
+    ].astype(BF)
+    attend_pair(HD, block, q_ref, k_ref, v_ref, None, o_ref, log_ref)
+
+    @pl.when(step_here == pl.num_programs(0) - 1)
+    def _():
         for sender in range(2):
-            await_part(k, sender)
-            plane_copy(0, 0, k, sender).start()
-            plane_copy(0, 1, k, sender).start()
-    for k in range(2):
-        plane_copy(0, 0, k, 0).wait_recv()
-        plane_copy(1, 1, k, 0).start()
-        plane_copy(0, 1, k, 1).wait_recv()
-        plane_copy(1, 0, k, 1).start()
-        plane_copy(0, 0, k, 1).wait_recv()
-        plane_copy(0, 1, k, 0).wait_recv()
-    for k in range(2):
-        plane_copy(1, 1, k, 0).wait_recv()
-        plane_copy(1, 0, k, 1).wait_recv()
-    for sender in range(2):
-        await_part(2, sender)
-    for part in swaps:
-        part.wait()
-    for part in small_own:
-        part.wait()
-    for j in range(1, 8):
-        sender = lax.rem(d + 8 - j, 8)
-        for part in small_copies(sender, j, plane_peers[j - 1]):
-            part.wait_recv()
-        for part in small_copies(d, j, plane_peers[j - 1]):
-            part.wait_send()
-    for part in far_parts:
-        part.wait_send()
-
-    @pl.when(jnp.logical_not(owner))
-    def _():
-        for part in near_parts:
-            part.wait_send()
-
-    for k in range(2):
+            side(0, 1 - sender, sender).wait_recv()
+        side(1, 1, 0).wait_recv()
+        side(1, 0, 1).wait_recv()
         for sender in range(2):
-            plane_copy(0, 0, k, sender).wait_send()
-            plane_copy(0, 1, k, sender).wait_send()
-        plane_copy(1, 1, k, 0).wait_send()
-        plane_copy(1, 0, k, 1).wait_send()
-
-
-def front(qkv_part, side_part, latents, prompt, time_part, facts):
-    place = pl.BlockSpec(memory_space=pl.ANY)
+            await_part(3, sender)
+        for each in outward:
+            each.wait()
+        for swap in swaps:
+            swap.wait()
+        for j in range(1, 8):
+            for which in range(2):
+                small(which, j, d).wait_send()
+        for k in parts:
+            far(k, core).wait_send()
+
+        @pl.when(owner)
+        def _():
+            item_copy.wait_send()
+
+        @pl.when(jnp.logical_not(owner))
+        def _():
+            for k in parts:
+                near(k, core).wait_send()
+
+        for sender in range(2):
+            for way in range(2):
+                side(0, way, sender).wait_send()
+                for k in range(2):
+                    plane(0, way, k, sender).wait_send()
+        side(1, 1, 0).wait_send()
+        side(1, 0, 1).wait_send()
+        for k in range(2):
+            plane(1, 1, k, 0).wait_send()
+            plane(1, 0, k, 1).wait_send()
+
+
+def opening(place, qkv_part, side_part, feed_part, latents, prompt, time_part, feat, facts, gain, bias):
+    length, width = latents.shape
+    total = qkv_part.shape[1]
     rows = qkv_part.shape[0]
+    pairs = total // 3 // 128
+    base, steps = turn_tables(length, 256)
+    block = pl.BlockSpec((length, 128), lambda i: (0, i))
+    whole = pl.BlockSpec(memory_space=pltpu.VMEM)
+    wide = jax.ShapeDtypeStruct((length, total // 3), BF)
+    dma = pltpu.SemaphoreType.DMA
     return pl.pallas_call(
-        front_kernel,
-        in_specs=[place] * 6,
-        out_specs=[place] * 6,
-        out_shape=(
-            jax.ShapeDtypeStruct((8 * rows, qkv_part.shape[1]), BF),
-            jax.ShapeDtypeStruct((2 * rows, side_part.shape[1]), BF),
-            jax.ShapeDtypeStruct(latents.shape, BF),
+        opening_kernel,
+        grid=(pairs,),
+        in_specs=[ANYWHERE] * 8 + [whole] * 4,
+        out_specs=[whole]
+        + [block] * 4
+        + [pl.BlockSpec((1, 2, length), lambda i: (i, 0, 0)), whole]
+        + [ANYWHERE] * 6,
+        out_shape=[jax.ShapeDtypeStruct((length, width), BF)]
+        + [wide] * 4
+        + [
+            jax.ShapeDtypeStruct((pairs, 2, length), F32),
+            jax.ShapeDtypeStruct((length // 2, width), F32),
+            jax.ShapeDtypeStruct((8 * rows, total), BF),
+            jax.ShapeDtypeStruct((8 * rows, side_part.shape[1]), BF),
+            jax.ShapeDtypeStruct((2 * rows, feed_part.shape[1]), BF),
             jax.ShapeDtypeStruct(prompt.shape, BF),
-            jax.ShapeDtypeStruct((8 * time_part.shape[0], time_part.shape[1]), BF),
-            jax.ShapeDtypeStruct((8 * facts.shape[0], facts.shape[1]), facts.dtype),
+            jax.ShapeDtypeStruct(facts.shape, facts.dtype),
+            jax.ShapeDtypeStruct((8 * feat.shape[0], feat.shape[1]), BF),
+        ],
+        scratch_shapes=[
+            pltpu.VMEM((length, total), F32),
+            pltpu.VMEM((length, width), BF),
+            pltpu.VMEM((8 * time_part.shape[0], width), BF),
+            pltpu.VMEM((8 * rows, total), BF),
+            pltpu.VMEM((8 * feat.shape[0], feat.shape[1]), BF),
+            dma((4,)),
+            dma((2, 4)),
+            dma((4,)),
+            dma((4,)),
+            dma((9,)),
+            dma((2, 8)),
+            dma((2, 8)),
+            dma((2, 4)),
+            dma((2, 4)),
+            dma((2, 7)),
+            dma((2, 7)),
+            dma((3,)),
+            dma((3,)),
+        ],
+        compiler_params=pltpu.CompilerParams(
+            collective_id=place, has_side_effects=True, vmem_limit_bytes=60 * 2**20
         ),
-        scratch_shapes=[
-            pltpu.SemaphoreType.DMA((3,)),
-            pltpu.SemaphoreType.DMA((2, 3)),
-            pltpu.SemaphoreType.DMA((3,)),
-            pltpu.SemaphoreType.DMA((3,)),
-            pltpu.SemaphoreType.DMA((4,)),
-            pltpu.SemaphoreType.DMA((2, 8)),
-            pltpu.SemaphoreType.DMA((2, 8)),
-            pltpu.SemaphoreType.DMA((2,)),
-            pltpu.SemaphoreType.DMA((2,)),
-            pltpu.SemaphoreType.DMA((2, 7)),
-            pltpu.SemaphoreType.DMA((2, 7)),
-        ],
-        compiler_params=pltpu.CompilerParams(collective_id=5, has_side_effects=True),
-        cost_estimate=pl.CostEstimate(flops=0, transcendentals=0, bytes_accessed=100_000_000),
-        name="front",
-    )(qkv_part, side_part, latents, prompt, time_part, facts)
+        cost_estimate=pl.CostEstimate(
+            flops=4 * length * length * total // 3 + 2 * length * width * total,
+            transcendentals=length * length * total // 192,
+            bytes_accessed=200_000_000,
+        ),
+        name="opening",
+    )(
+        qkv_part,
+        side_part,
+        feed_part,
+        latents,
+        prompt,
+        time_part,
+        feat,
+        facts,
+        gain[None],
+        bias[None],
+        base,
+        steps,
+    )
 
 
 def per_device_paired(
@@ -1891,67 +2133,55 @@
         ],
         axis=1,
     )
-    facts = jnp.zeros((8, 128), jnp.int32)
-    facts = facts.at[0].set(prompt_lengths[0]).at[1].set(timesteps[0])
-    qkv_full, side_own, latents_too, prompt_too, time_full, facts_full = front(
+    feature_width = 8 * time_weight.shape[0]
+    features = time_features(timesteps, feature_width).astype(BF)
+    (
+        normed_one,
+        queries,
+        keys,
+        values,
+        attended,
+        self_logs,
+        residual_mine,
+        qkv_full,
+        side_full,
+        gate_up_own,
+        prompt_too,
+        facts_too,
+        features_full,
+    ) = opening(
+        5,
         qkv_weight.reshape(part_rows, -1),
         side_part,
-        latents[0],
+        gate_up_weight.reshape(part_rows, -1),
+        jnp.pad(latents[0], ((1, 0), (0, 0))),
         prompt_tokens[0],
         time_weight,
-        facts,
-    )
-    side_full = plane_gather(side_own)
+        jnp.broadcast_to(features, (16, feature_width)),
+        jnp.broadcast_to(prompt_lengths[:, None], (8, 128)),
+        self_gain,
+        self_bias,
+    )
+    gate_up_full = plane_gather(gate_up_own)
     self_out_full = side_full[:, :n]
     cross_query_full = side_full[:, n : 2 * n]
     cross_out_full = side_full[:, 2 * n : 3 * n]
     context_full = side_full[:, 3 * n :].reshape(context_weight.shape[0] * 8, -1)
 
-    item_latents = jnp.where(owner, latents[0], latents_too)
     item_prompt = jnp.where(owner, prompt_tokens[0], prompt_too)
-    facts_full = facts_full.reshape(8, 8, 128)[:, :2, 0]
-    item_facts = lax.dynamic_index_in_dim(facts_full, d - core + pair, 0, False)
-    item_length, item_step = item_facts[0], item_facts[1]
-    feature_width = time_full.shape[0]
-    item_features = time_features(item_step[None], feature_width).astype(BF)
-    token_row = dot_nn(item_features, time_full)
-    residual_in = jnp.concatenate([token_row, item_latents.astype(F32)], axis=0)
-    residual_in = xor_blocks(residual_in, 0, 2, core)
-    residual_mine = residual_in[:half_rows]
-    cosine, sine = rope_tables(length, HD)
-    quarter = HD // 4
-    straight = jnp.ones((length, HD // 2), F32)
-    blank = jnp.zeros((length, quarter), F32)
-    cosine, sine = cosine[:, 0], sine[:, 0]
-    tables = jnp.stack(
-        [
-            jnp.tile(jnp.concatenate([cosine, straight], axis=1), (1, 2)),
-            jnp.tile(
-                jnp.concatenate([-sine[:, :quarter], blank, blank, blank], axis=1), (1, 2)
-            ),
-            jnp.tile(
-                jnp.concatenate([blank, sine[:, quarter:], blank, blank], axis=1), (1, 2)
-            ),
-        ]
-    )
-    tables = xor_blocks(tables, 1, 2, core)
-    tables = (tables[0], tables[1], tables[2])
-    normed_one, queries, keys, values, attended, self_logs, gate_up_own = self_attention(
-        6, residual_in, self_gain, self_bias, qkv_full, tables, gate_up_weight.reshape(part_rows, -1)
-    )
-    gate_up_full = plane_gather(gate_up_own)
-    cot_shard = move(after(cotangent[0], attended), ROUTE_A)
-    residual_one, normed_two_all, down_own = exchange(
+    item_length = jnp.where(owner, prompt_lengths[0], facts_too[0, 0])
+
+    residual_one, normed_two_all, down_own, cot_too = exchange(
         "norm",
         0,
         attended,
-        self_out_full,
+        side_full,
         residual_mine,
         cross_gain,
         cross_bias,
-        load=Loads((Spread, down_weight.T)),
-    )
-    cot_shard = after(cot_shard, normed_two_all)
+        load=Loads((Spread, down_weight.T), (SwapRoute, cotangent[0])),
+    )
+    cot_shard = jnp.where(owner, cotangent[0], cot_too)
     cot_far = move(cot_shard, SWAP_Z)
     odd = (z & 1) == 1
     cross_q = dot_nn(normed_two_all, cross_query_full).astype(BF)
@@ -1969,51 +2199,58 @@
         "norm",
         1,
         crossed,
-        cross_out_full,
+        side_full,
         residual_one,
         feed_gain,
         feed_bias,
         load=Loads((Plane, down_own)),
+        window=2,
     )
     cot_all = jnp.concatenate([cot_mine, after(cot_other, normed_three_all)], axis=0)
     hidden, grad_gate_up = feed_forward(normed_three_all, cot_all, gate_up_full, down_full)
 
-    gate_up_local = dot_tn(normed_three_all, grad_gate_up).astype(BF)
-    gate_up_sums = plane_sum(gate_up_local)
     split = gate_up_weight.shape[2]
-    gate_sums, up_sums = gate_up_sums[:, :split], gate_up_sums[:, split:]
-    grad_two_all, feed_sums = exchange(
+    gate_local = dot_tn(normed_three_all, grad_gate_up[:, :split]).astype(BF)
+    gate_sums = plane_sum(gate_local)
+    up_local = dot_tn(normed_three_all, after(grad_gate_up, gate_local)[:, split:]).astype(BF)
+    up_sums = plane_sum(up_local)
+    grad_two_all, feed_sums, feed, down_local = exchange(
         "back",
         2,
-        after(grad_gate_up, gate_up_local),
+        after(grad_gate_up, up_local),
         gate_up_full,
         residual_two,
         cot_mine,
         feed_gain,
-    )
-    down_bias_part = jnp.sum(cot_mine.astype(F32), axis=0)
-    hidden = after(hidden, grad_two_all)
-    down_local = dot_tn(cot_all, hidden).astype(BF)
+        works=Works(("nt", hidden, down_full), ("tn", cot_all, hidden)),
+    )
     down_sums = plane_sum(down_local)
-    feed = dot_nt(hidden, down_full).astype(BF)
     grad_crossed = dot_nn(grad_two_all, cross_out_full).astype(BF)
     grad_cross_q, grad_context = cross_attention_back(
         cross_q, context, mask, grad_crossed, cross_logs
     )
-    context_grad = dot_tn(item_prompt, grad_context).astype(BF).reshape(side_full.shape[0], -1)
-    cross_out_grad = dot_tn(grad_two_all, crossed).astype(BF)
-    cross_query_grad = dot_tn(normed_two_all, grad_cross_q).astype(BF)
-    cross_local = jnp.concatenate([cross_query_grad, cross_out_grad, context_grad], axis=1)
-    grad_one_all, cross_sums, gate_near, gate_far, feed_near = exchange(
+    (
+        grad_one_all,
+        cross_sums,
+        gate_near,
+        gate_far,
+        feed_near,
+        cross_query_grad,
+        cross_out_grad,
+    ) = exchange(
         "back",
         3,
-        after(grad_cross_q, down_local, feed),
-        cross_query_full,
+        grad_cross_q,
+        side_full,
         residual_one,
-        grad_two_all[:half_rows],
+        grad_two_all,
         cross_gain,
-        load=Loads((Return, gate_sums), (SwapCore, feed[half_rows:])),
-    )
+        load=Loads((Return, gate_sums), (SwapCoreHalf, feed)),
+        window=1,
+        works=Works(("tn", normed_two_all, grad_cross_q), ("tn", grad_two_all, crossed)),
+    )
+    context_grad = dot_tn(item_prompt, grad_context).astype(BF).reshape(side_full.shape[0], -1)
+    cross_local = jnp.concatenate([cross_query_grad, cross_out_grad, context_grad], axis=1)
     feed_half = feed[:half_rows].astype(F32) + feed_near.astype(F32)
     feed_here = jnp.where(odd, feed_half[rows:], feed_half[:rows])
     feed_away = jnp.where(odd, feed_half[:rows], feed_half[rows:]).astype(BF)
@@ -2025,35 +2262,47 @@
         values,
         grad_attended,
         self_logs,
-        tables,
         Loads((Return, up_sums), (SwapNear, feed_away)),
     )
     residual_here = jnp.where(odd, residual_two[rows:], residual_two[:rows])
     output_here = (residual_here + feed_here + feed_far.astype(F32) + down_bias).astype(BF)
     cross_total = plane_sum(cross_local)
     self_out_local = dot_tn(grad_one_all, attended).astype(BF)
-    self_out_total = plane_sum(after(self_out_local, cross_total))
     qkv_local = dot_tn(normed_one, grad_projected).astype(BF)
-    qkv_total = plane_sum(qkv_local)
-    side_total = jnp.concatenate([cross_total, self_out_total], axis=1)
-    grad_in, self_sums, down_near, down_far, side_near, side_far, output_far = exchange(
+    self_local = jnp.concatenate([qkv_local, self_out_local], axis=1)
+    self_total = plane_sum(self_local)
+    grad_in, self_sums, down_near, down_far, output_far = exchange(
         "half",
         4,
-        after(grad_projected, qkv_local),
+        after(grad_projected, self_local),
         qkv_full,
         residual_mine,
-        grad_one_all[:half_rows],
+        grad_one_all,
         self_gain,
-        load=Loads((Return, down_sums), (Return, side_total), (SwapRoute, output_here)),
-    )
-    whole, token_rows, qkv_near, qkv_far = spread_gradient(
-        8, grad_in, Loads((Return, qkv_total))
-    )
+        load=Loads((Return, down_sums), (SwapRoute, output_here)),
+    )
+    sums = jnp.concatenate(
+        [
+            jnp.sum(self_sums, axis=1),
+            jnp.sum(cross_sums, axis=1),
+            jnp.sum(feed_sums, axis=1),
+            jnp.sum(cot_mine.astype(F32), axis=0)[None],
+            jnp.zeros((1, grad_in.shape[1]), F32),
+        ],
+        axis=0,
+    )
+    share = sums.shape[1] // 8
+    pieces = jnp.swapaxes(sums.reshape(8, 8, share), 0, 1)
+    pieces = jnp.pad(pieces, ((0, 0), (0, 0), (0, 256 - share))).reshape(64, 256)
+    whole, token_rows, sums, cross_near, cross_far, self_near, self_far = spread_gradient(
+        8, grad_in, pieces, Loads((Return, cross_total), (Return, self_total))
+    )
+    sums = jnp.sum(sums.reshape(16, 8, 256), axis=0)[:, :share]
     output = jnp.where(owner, output_here, output_far)
     latents_grad = whole[1:]
 
     token_rows = token_rows.reshape(8, 16, -1)[:, 0]
-    all_features = time_features(facts_full[:, 1], feature_width).astype(BF)
+    all_features = features_full.reshape(8, 16, -1)[:, 0]
     my_features = jnp.zeros((8, feature_width // 8), F32)
     for j in range(8):
         piece = all_features[:, j * (feature_width // 8) : (j + 1) * (feature_width // 8)]
@@ -2062,23 +2311,9 @@
         my_features.astype(BF), token_rows, (((0,), (0,)), ((), ())), preferred_element_type=F32
     )
 
-    sums = jnp.concatenate(
-        [
-            jnp.sum(self_sums, axis=1),
-            jnp.sum(cross_sums, axis=1),
-            jnp.sum(feed_sums, axis=1),
-            down_bias_part[None],
-        ],
-        axis=0,
-    )
-    sums = xor_blocks(sums, 1, 8, d)
-    for pairs in (SWAP_Y, SWAP_X, SWAP_CORE):
-        middle = sums.shape[1] // 2
-        sums = sums[:, :middle] + move(sums[:, middle:], pairs)
-    sums = sums + move(sums, SWAP_PAIR)
-
-    side_grads = returned(side_total, side_near, side_far, core, owner)
-    qkv_grad = returned(qkv_total, qkv_near, qkv_far, core, owner)
+    cross_grads = returned(cross_total, cross_near, cross_far, core, owner)
+    self_grads = returned(self_total, self_near, self_far, core, owner)
+    qkv_columns = qkv_full.shape[1]
     gate_grad = returned(gate_sums, gate_near, gate_far, core, owner)
     up_grad = returned(up_sums, up_near, up_far, core, owner)
     down_grad = returned(down_sums, down_near, down_far, core, owner)
@@ -2088,15 +2323,13 @@
         time_grad,
         sums[0],
         sums[1],
-        qkv_grad.reshape(qkv_weight.shape),
-        side_grads[:, 2 * n + context_weight.size // part_rows :].T,
+        self_grads[:, :qkv_columns].reshape(qkv_weight.shape),
+        self_grads[:, qkv_columns:].T,
         sums[2],
         sums[3],
-        side_grads[:, :n],
-        side_grads[:, 2 * n : 2 * n + context_weight.size // part_rows].reshape(
-            context_weight.shape
-        ),
-        side_grads[:, n : 2 * n].T,
+        cross_grads[:, :n],
+        cross_grads[:, 2 * n :].reshape(context_weight.shape),
+        cross_grads[:, n : 2 * n].T,
         sums[4],
         sums[5],
         jnp.stack([gate_grad, up_grad], axis=1),

time: 791 us -> 714 us (0.903)
  matrix products: 69.9 us -> 42.4 us
  waiting for transfers between devices: 21 us -> 5.74 us
  local copies, waits for them, and re-layouts: 48.7 us -> 34.9 us
  other arithmetic: 35.2 us -> 27 us
    pallas_call x7 -> x6, Pallas kernels: 434 us -> 414 us  [the longest x5 300 us: exchange(): pl.pallas_call(functools.partial(exchange_kernel, kind, chunks, window, l...]
    dot_general x7 -> x5, matrix products: 46.2 us -> 27.5 us  [dot_tn(): lax.dot_general(left, right, (((0,), (0,)), ((), ())), preferred_element_...]
    pallas_call x1, Pallas kernels: 72.8 us -> 89.8 us  [spread_gradient(): pl.pallas_call(functools.partial(spread_kernel, load, chunks), in_specs=[...]
    slice x9 -> x5, local copies, waits for them, and re-layouts: 16.6 us -> 3.38 us  [the longest x1 1.39 us: per_device_paired(): context_full = side_full[:, 3 * n:].reshape(context_weight.shape[0] * 8, -1)]
    reduce_scatter x5, waiting for transfers between devices: 14.9 us -> 3.2 us  [plane_sum(): lax.psum_scatter(grad, 'dp', scatter_dimension=0, tiled=True, axis_index_...]
  transfers between devices with their start and end apart: 14 -> 8, of which waited for: 4 -> 2; matrix products, arithmetic and copies ran while one was open for 15% -> 10% of each run, Pallas kernels for 55% -> 49%
where the time goes in v3:
time: 714 us; the launch traced here: 709 us
  Pallas kernels  581 us (81%)
  matrix products  42.4 us (6%)
  local copies, waits for them, and re-layouts  34.9 us (5%)
  other arithmetic  27 us (4%)
  between operations  17.1 us (2%)
    pallas_call x5, Pallas kernels, exchange(): pl.pallas_call(functools.partial(exchange_kernel, kind, chunks, window, l...  300 us
    pallas_call x1, Pallas kernels, opening(): pl.pallas_call(opening_kernel, grid=(pairs,), in_specs=[ANYWHERE] * 8 + [...  114 us
    pallas_call x1, Pallas kernels, spread_gradient(): pl.pallas_call(functools.partial(spread_kernel, load, chunks), in_specs=[...  89.8 us
    pallas_call x1, Pallas kernels, self_attention_back(): pl.pallas_call(functools.partial(attention_backward_kernel, HD, 256, True...  36.4 us
    dot_general x5, matrix products, dot_tn(): lax.dot_general(left, right, (((0,), (0,)), ((), ())), preferred_element_...  27.5 us
    pallas_call x1, Pallas kernels, feed_forward(): pl.pallas_call(feed_kernel, grid=(steps,), in_specs=[fixed, fixed, pl.Blo...  26.4 us
  transfers between devices with their start and end apart: 8, of which 2 were waited for; matrix products, arithmetic and copies ran while one was open for 10% of the time, Pallas kernels for 49%

profile of v3, /device:TPU:1, one launch (start us, length us, event | category | flops | bytes accessed | tf_op | source)
XLA Modules:
  0.0 708.9 jit_solution(17412796367791388169)
XLA Ops:
  8.9 1.3 broadcast_in_dim.70.refs_8_.refs_4_
  10.2 1.3 broadcast_in_dim.71.refs_9_
  11.5 1.0 reshape.113
  12.4 1.8 copy.60
  14.2 2.4 copy.61
  16.7 2.4 pad.8.refs_3_
  19.1 0.9 pad_maximum_fusion.5.refs_1_
  20.0 0.6 broadcast_in_dim.69.refs_7_
  20.6 0.6 broadcast_in_dim.67.refs_6_
  21.2 114.0 %opening.1 = (bf16[1024,1536]{1,0:T(8,128)(2,1)}, bf16[1024,384]{1,0:T(8,128)(2,1)}, bf16[1024,384]{1,0:T(8,128)(2,1)}, bf16[1024,384]{1,0:T(8,128)(2,1)}, bf16[...) custom-call(bf16[192,1152]{1,0:T(8,128)(2,1)} %bitcast.82, ...), custom_call_target="tpu_custom_call" | custom-call | flops 5234491392 | bytes 200000000 | tf_op jit(solution)/shard_map/opening/pallas_call | solution.py:2030
  135.5 0.6 broadcast_in_dim.72.refs_3_.refs_4_
  136.1 0.6 broadcast_in_dim.73.refs_4_
  136.7 70.2 %exchange_norm.2 = (f32[512,1536]{1,0:T(8,128)}, bf16[1024,1536]{1,0:T(8,128)(2,1)}, bf16[384,1536]{1,0:T(8,128)(2,1)}, bf16[256,1536]{1,0:T(8,128)(2,1)}) custom-call(bf16[1024,384]{1,0:T(8,128)(2,1)} %get-tuple-element.75.refs_0_, bf16[1536,1536]{1,0:T(8,128)(2,1)} %get-tuple-element.76.refs_1_, f32[512,1536]{1,0:T(8,128)} %get-tuple-element.77.refs_2_, ...), custom_call_target="tpu_custom_call" | custom-call | flops 1207959552 | bytes 100000000 | tf_op jit(solution)/shard_map/exchange_norm/pallas_call | solution.py:1470
  206.9 1.3 broadcast_select_fusion.2
  208.2 1.4 slice.146
  209.6 1.2 slice.147
  211.9 0.6 fusion.10.bias_ref.refs_5_
  212.5 1.0 convolution_convert_fusion.8.k_ref.v_ref.refs_1_.refs_2_
  213.6 4.9 convolution_convert_fusion.7.q_ref.refs_0_
  218.4 6.4 cross_attention.1
  224.9 2.4 collective-permute-done
  227.3 1.3 broadcast_select_fusion.1
  228.8 0.8 broadcast_in_dim.76.refs_3_.refs_4_
  229.6 0.6 broadcast_in_dim.77.refs_4_
  230.2 47.6 %exchange_norm.3 = (f32[512,1536]{1,0:T(8,128)}, bf16[1024,1536]{1,0:T(8,128)(2,1)}, bf16[1536,1536]{1,0:T(8,128)(2,1)}) custom-call(bf16[1024,384]{1,0:T(8,128)(2,1)} %get-tuple-element.81.refs_0_.refs_10_, bf16[1536,1536]{1,0:T(8,128)(2,1)} %get-tuple-element.76.refs_1_, f32[512,1536]{1,0:T(8,128)} %get-tuple-element.82.refs_2_, ...), custom_call_target="tpu_custom_call" | custom-call | flops 1207959552 | bytes 100000000 | tf_op jit(solution)/shard_map/exchange_norm/pallas_call | solution.py:1470
  277.9 3.3 pad_maximum_fusion.2.cot_ref.refs_7_
  281.2 26.4 %feed_forward.1 = (bf16[1024,1536]{1,0:T(8,128)(2,1)}, bf16[1024,3072]{1,0:T(8,128)(2,1)}) custom-call(bf16[1024,1536]{1,0:T(8,128)(2,1)} %get-tuple-element.85.n_ref, bf16[1024,1536]{1,0:T(8,128)(2,1)} %pad_maximum_fusion.2.cot_ref.refs_7_, bf16[1536,3072]{1,0:T(8,128)(2,1)} %all-gather.2.cloned.1.call-done.gate_ref.up_ref.refs_1_, ...), custom_call_target="tpu_custom_call" | custom-call | flops 14495514624 | bytes 30000000 | tf_op jit(solution)/shard_map/feed_forward/pallas_call | solution.py:1684
  307.6 8.6 %convolution_convert_fusion.2 = bf16[1536,1536]{1,0:T(8,128)(2,1)} fusion(bf16[1024,1536]{1,0:T(8,128)(2,1)S(1)} %copy-done.38, bf16[1024,3072]{1,0:T(8,128)(2,1)} %get-tuple-element.93.refs_0_), kind=kOutput, calls=%fused_computation.2 | convolution fusion | flops 4834197504 | bytes 11010048 | tf_op jit(solution)/shard_map/dot_general | solution.py:787
  316.3 8.8 %convolution_convert_fusion.1 = bf16[1536,1536]{1,0:T(8,128)(2,1)} fusion(bf16[1024,1536]{1,0:T(8,128)(2,1)S(1)} %copy-done.38, bf16[1024,3072]{1,0:T(8,128)(2,1)} %get-tuple-element.93.refs_0_), kind=kOutput, calls=%fused_computation.1 | convolution fusion | flops 4834197504 | bytes 11010048 | tf_op jit(solution)/shard_map/dot_general | solution.py:787
  325.4 54.9 %exchange_back.2 = (bf16[1024,1536]{1,0:T(8,128)(2,1)}, f32[2,8,1536]{2,1,0:T(8,128)}, bf16[1024,1536]{1,0:T(8,128)(2,1)}, bf16[1536,1536]{1,0:T(8,128)(2,1)}) custom-call(bf16[1024,3072]{1,0:T(8,128)(2,1)} %get-tuple-element.93.refs_0_, bf16[1536,3072]{1,0:T(8,128)(2,1)} %all-gather.2.cloned.1.call-done.gate_ref.up_ref.refs_1_, ...), custom_call_target="tpu_custom_call" | custom-call | flops 9663676416 | bytes 100000000 | tf_op jit(solution)/shard_map/exchange_back/pallas_call | solution.py:1470
  380.3 2.6 copy-done.2
  382.9 3.9 convolution_convert_fusion.6.refs_3_
  386.8 7.7 %cross_attention_back.1 = (bf16[1024,384]{1,0:T(8,128)(2,1)}, bf16[128,768]{1,0:T(8,128)(2,1)}) custom-call(bf16[1024,384]{1,0:T(8,128)(2,1)} %convolution_convert_fusion.7.q_ref.refs_0_, bf16[128,768]{1,0:T(8,128)(2,1)} %convolution_convert_fusion.8.k_ref.v_ref.refs_1_.refs_2_, bf16[128,768]{1,0:T(8,128)(2,1)} %convolution_convert_fusion.8.k_ref.v_ref.refs_1_.refs_2_, ...), custom_call_target="tpu_custom_call" | custom-call | flops 503316480 | bytes 3145728 | tf_op jit(solution)/shard_map/cross_attention_back/pallas_call | solution.py:752
  394.5 1.4 convolution_convert_fusion.4
  396.4 59.5 %exchange_back.3 = (bf16[1024,1536]{1,0:T(8,128)(2,1)}, f32[2,8,1536]{2,1,0:T(8,128)}, bf16[192,1536]{1,0:T(8,128)(2,1)}, bf16[192,1536]{1,0:T(8,128)(2,1)}, bf1...) custom-call(bf16[1024,384]{1,0:T(8,128)(2,1)} %get-tuple-element.98.refs_0_.refs_8_, ...), custom_call_target="tpu_custom_call" | custom-call | flops 1207959552 | bytes 100000000 | tf_op jit(solution)/shard_map/exchange_back/pallas_call | solution.py:1470
  455.9 3.2 pad_maximum_fusion.1
  459.3 1.9 copy-done.12
  461.2 4.1 convolution_convert_fusion.5.refs_3_
  465.7 1.0 select_convert_fusion.refs_8_
  466.7 36.4 %self_attention_back.1 = (bf16[1024,1152]{1,0:T(8,128)(2,1)}, bf16[192,1536]{1,0:T(8,128)(2,1)}, bf16[192,1536]{1,0:T(8,128)(2,1)}, bf16[256,1536]{1,0:T(8,128)(2,1)}) custom-call(bf16[1024,384]{1,0:T(8,128)(2,1)} %get-tuple-element.100.refs_0_, bf16[1024,384]{1,0:T(8,128)(2,1)} %get-tuple-element.101.refs_1_, bf16[1024,384]{1,0:T(8,128)(2,1)} %get-tuple-element.102.refs_2_, ...), custom_call_target="tpu_custom_call" | custom-call | flops 4026531840 | bytes 100000000 | tf_op jit(solution)/shard_map/self_attention_back/pallas_call | solution.py:701
  503.1 4.1 convolution_convert_fusion.3
  507.2 4.6 convolution_convert_fusion
  511.8 2.5 pad_maximum_fusion
  514.4 0.8 slice.192
  515.2 1.7 convert_reduce_fusion
  517.2 2.1 add_bitcast_fusion.2
  520.1 3.2 copy.53
  523.3 1.6 add_convert_fusion.refs_6_
  525.0 68.1 %exchange_half.1 = (bf16[512,1536]{1,0:T(8,128)(2,1)}, f32[2,8,1536]{2,1,0:T(8,128)}, bf16[192,1536]{1,0:T(8,128)(2,1)}, bf16[192,1536]{1,0:T(8,128)(2,1)}, bf16[256,1536]{1,0:T(8,128)(2,1)}) custom-call(bf16[1024,1152]{1,0:T(8,128)(2,1)} %get-tuple-element.108.refs_0_, bf16[1536,1152]{1,0:T(8,128)(2,1)} %get-tuple-element.109.refs_1_, ...), custom_call_target="tpu_custom_call" | custom-call | flops 3623878656 | bytes 100000000 | tf_op jit(solution)/shard_map/exchange_half/pallas_call | solution.py:1470
  593.1 1.1 reduce_sum.45
  594.3 0.6 pad_bitcast_fusion.refs_1_
  595.0 2.1 select_bitcast_fusion
  597.1 1.3 add_bitcast_fusion
  598.4 3.2 reduce-scatter.14.cloned.1.call-done.refs_3_
  601.6 89.8 %spread_gradient.1 = (bf16[1024,1536]{1,0:T(8,128)(2,1)}, bf16[128,1536]{1,0:T(8,128)(2,1)}, f32[128,256]{1,0:T(8,128)}, bf16[192,1152]{1,0:T(8,128)(2,1)}, bf16...) custom-call(bf16[512,1536]{1,0:T(8,128)(2,1)} %get-tuple-element.112.refs_0_, ...), custom_call_target="tpu_custom_call" | custom-call | bytes 100000000 | tf_op jit(solution)/shard_map/spread_gradient/pallas_call | solution.py:1627
  691.3 1.7 convert_add_fusion.1
  693.0 0.8 slice_bitcast_fusion.2
  693.8 2.4 slice_bitcast_fusion
  696.2 1.0 slice.201
  697.5 0.9 slice_bitcast_fusion.1
  698.4 0.6 fusion.32
  699.0 0.9 reshape.122
  699.9 1.0 copy.66
  700.9 1.0 fusion.11
  (123 shorter events, 3.9 us)
Async XLA Ops:
  7.2 9.5 %copy-start.9 = (bf16[1,1023,1536]{2,1,0:T(8,128)(2,1)S(1)}, bf16[1,1023,1536]{2,1,0:T(8,128)(2,1)}, u32[]{:S(2)}) copy-start(bf16[1,1023,1536]{2,1,0:T(8,128)(2,1)} %param.24) | copy-start | bytes 9427972
  7.2 274.0 %all-gather.2.cloned.1.call-start = ((), (), s32[]{:S(2)}) async-start(), calls=%async_computation.5 | async-start | bytes 11796480 | tf_op jit(solution)/shard_map/all_gather | solution.py:811
  16.7 2.4 copy-start.27
  16.7 2.4 copy-start.28
  16.7 2.4 copy-start.29
  21.2 114.3 %copy-start.34 = (f32[1536]{0:T(1024)S(1)}, f32[1536]{0:T(1024)}, u32[]{:S(2)}) copy-start(f32[1536]{0:T(1024)} %param.33) | copy-start | bytes 18436
  21.2 114.9 %copy-start.35 = (f32[1536]{0:T(1024)S(1)}, f32[1536]{0:T(1024)}, u32[]{:S(2)}) copy-start(f32[1536]{0:T(1024)} %param.34) | copy-start | bytes 18436
  135.2 261.2 %reduce-scatter.6.cloned.1.call-start = ((), (), s32[]{:S(2)}) async-start(), calls=%async_computation.6 | async-start | bytes 5898240 | tf_op jit(solution)/shard_map/reduce_scatter | solution.py:815
  136.7 70.2 %copy-start.13 = (bf16[1,256,1536]{2,1,0:T(8,128)(2,1)S(1)}, bf16[1,256,1536]{2,1,0:T(8,128)(2,1)}, u32[]{:S(2)}) copy-start(bf16[1,256,1536]{2,1,0:T(8,128)(2,1)} %param.43) | copy-start | bytes 2359300
  206.9 5.7 copy-start.19
  206.9 5.7 copy-start.20
  208.2 19.2 %collective-permute-start = (bf16[256,1536]{1,0:T(8,128)(2,1)S(1)}, bf16[256,1536]{1,0:T(8,128)(2,1)}, u32[]{:S(2)}, u32[]{:S(2)}) collective-permute-start(bf16[256,1536]{1,0:T(8,128)(2,1)S(1)} %broadcast_select_fusion.2), channel_id=1, source_target_pairs={{0,1},{1,0},{2,3},{3,2},{4,5},{5,4},{6,7},{7,6},{8,9},{9,8},{10,11... | collective-permute-start | bytes 2359304 | tf_op jit(solution)/shard_map/ppermute | solution.py:548
  227.3 1.5 copy-start.36
  227.3 2.3 copy-start.37
  228.6 49.3 %copy-start = (bf16[256,1536]{1,0:T(8,128)(2,1)}, bf16[256,1536]{1,0:T(8,128)(2,1)S(1)}, u32[]{:S(2)}) copy-start(bf16[256,1536]{1,0:T(8,128)(2,1)S(1)} %get-tuple-element.167) | copy-start | bytes 2359300
  228.6 49.3 %copy-start.1 = (bf16[256,1536]{1,0:T(8,128)(2,1)}, bf16[256,1536]{1,0:T(8,128)(2,1)S(1)}, u32[]{:S(2)}) copy-start(bf16[256,1536]{1,0:T(8,128)(2,1)S(1)} %get-tuple-element.168) | copy-start | bytes 2359300
  228.7 49.2 %copy-start.15 = (bf16[512,1536]{1,0:T(8,128)(2,1)}, bf16[512,1536]{1,0:T(8,128)(2,1)S(1)}, u32[]{:S(2)}) copy-start(bf16[512,1536]{1,0:T(8,128)(2,1)S(1)} %pad_maximum_fusion.4.refs_3_) | copy-start | bytes 4718596
  228.7 49.2 %collective-permute-start.1 = (bf16[512,1536]{1,0:T(8,128)(2,1)S(1)}, bf16[512,1536]{1,0:T(8,128)(2,1)}, u32[]{:S(2)}, u32[]{:S(2)}) collective-permute-start(bf16[512,1536]{1,0:T(8,128)(2,1)S(1)} %pad_maximum_fusion.4.refs_3_), channel_id=1, source_target_pairs={{0,4},{1,5},{2,6},{3,7},{4,0},{5,1},{6,2},{7,3},{8,12},{9,13},{10,... | collective-permute-start | bytes 4718600 | tf_op jit(solution)/shard_map/ppermute | solution.py:548
  281.2 26.4 %copy-start.38 = (bf16[1024,1536]{1,0:T(8,128)(2,1)S(1)}, bf16[1024,1536]{1,0:T(8,128)(2,1)}, u32[]{:S(2)}) copy-start(bf16[1024,1536]{1,0:T(8,128)(2,1)} %get-tuple-element.85.n_ref) | copy-start | bytes 9437188
  316.3 150.5 %reduce-scatter.8.cloned.1.call-start = ((), (), s32[]{:S(2)}) async-start(), calls=%async_computation.7 | async-start | bytes 5898240 | tf_op jit(solution)/shard_map/reduce_scatter | solution.py:815
  325.1 199.9 %reduce-scatter.10.cloned.1.call-start = ((), (), s32[]{:S(2)}) async-start(), calls=%async_computation.8 | async-start | bytes 5898240 | tf_op jit(solution)/shard_map/reduce_scatter | solution.py:815
  380.2 2.7 copy-start.2
  380.2 218.1 %reduce-scatter.12.cloned.1.call-start = ((), (), s32[]{:S(2)}) async-start(), calls=%async_computation.9 | async-start | bytes 4423680 | tf_op jit(solution)/shard_map/reduce_scatter | solution.py:815
  459.2 2.0 copy-start.12
  459.2 142.4 %reduce-scatter.14.cloned.1.call-start = ((), (), s32[]{:S(2)}) async-start(), calls=%async_computation.10 | async-start | bytes 5898240 | tf_op jit(solution)/shard_map/reduce_scatter | solution.py:815
  461.2 4.1 copy-start.4
  461.2 4.1 copy-start.16
  503.1 4.1 copy-start.14
  503.1 4.1 copy-start.39
  514.4 2.6 copy-start.31
  514.4 2.8 copy-start.32
  517.2 2.1 copy-start.17
  517.2 2.2 copy-start.21
  517.2 2.4 copy-start.22
  520.1 3.3 copy-start.10
  520.1 3.3 copy-start.18
  520.1 3.2 copy-start.33
  525.0 70.0 %copy-start.3 = (bf16[256,1536]{1,0:T(8,128)(2,1)S(1)}, bf16[256,1536]{1,0:T(8,128)(2,1)}, u32[]{:S(2)}) copy-start(bf16[256,1536]{1,0:T(8,128)(2,1)} %add_convert_fusion.refs_6_) | copy-start | bytes 2359300
  593.1 4.0 copy-start.7
  593.1 4.0 copy-start.23
  593.1 4.0 copy-start.24
  601.6 89.8 %copy-start.5 = (bf16[384,1536]{1,0:T(8,128)(2,1)S(1)}, bf16[384,1536]{1,0:T(8,128)(2,1)}, u32[]{:S(2)}) copy-start(bf16[384,1536]{1,0:T(8,128)(2,1)} %reduce-scatter.14.cloned.1.call-done.refs_3_) | copy-start | bytes 3538948
  691.3 2.5 copy-start.11
  693.0 3.2 copy-start.6
  693.8 3.5 copy-start.8
  693.8 3.5 copy-start.25
  693.8 3.5 copy-start.26
  696.2 2.2 copy-start.30
  696.2 3.7 slice-start
Sparse Core Ops, SparseCore 0:
  135.3 95.8 all-gather.1
  316.4 54.7 reduce-scatter.5
  374.2 57.1 reduce-scatter.7
  434.2 57.1 reduce-scatter.9
  494.3 47.2 reduce-scatter.11
  544.5 57.0 reduce-scatter.13

commit v4 on v3

--- a/solution.py
+++ b/solution.py
@@ -1136,12 +1136,126 @@
     way = "route"
 
 
+def scratch_of(kind, operand):
+    return kind.scratch(operand) if callable(kind.scratch) else kind.scratch
+
+
+class PlaneSum:
+    late = False
+
+    @staticmethod
+    def scratch(grad):
+        rows, width = grad.shape[0] // 4, grad.shape[1]
+        return [
+            pltpu.VMEM((rows, width), BF),
+            pltpu.VMEM((2, rows, width), BF),
+            pltpu.VMEM((2, rows, width), BF),
+            pltpu.VMEM((rows, width), BF),
+            pltpu.SemaphoreType.DMA((2, 2)),
+            pltpu.SemaphoreType.DMA((2, 2)),
+            pltpu.SemaphoreType.DMA((4,)),
+        ]
+
+    @staticmethod
+    def outs(grad):
+        return [jax.ShapeDtypeStruct((grad.shape[0] // 4, grad.shape[1]), BF)]
+
+    @staticmethod
+    def peers(place):
+        return [place.x_peer, place.y_peer]
+
+    def __init__(self, place, ins, outs, scratch):
+        self.place = place
+        (self.grad,), (self.out,) = ins, outs
+        self.first, self.staged, self.second, self.own, self.sent, self.got, self.here = scratch
+        self.rows = self.own.shape[0]
+        self.ways = (place.x_peer, place.y_peer)
+        self.columns = (place.x_column, place.y_column)
+        self.diagonal = place.x_column + 2 - 4 * (place.x_column // 2)
+
+    def block(self, column, start, count):
+        first = pl.multiple_of(column * self.rows + start, count)
+        return self.grad.at[pl.ds(first, count)]
+
+    def one(self, way):
+        count = self.rows // 2
+        return send(
+            self.block(self.diagonal, way * count, count),
+            self.first.at[pl.ds(way * count, count)],
+            self.sent.at[0, way],
+            self.got.at[0, way],
+            self.ways[way],
+        )
+
+    def two(self, way):
+        return send(
+            self.staged.at[way],
+            self.second.at[way],
+            self.sent.at[1, way],
+            self.got.at[1, way],
+            self.ways[way],
+        )
+
+    def load(self, way):
+        source = self.block(self.columns[way], 0, self.rows)
+        return pltpu.make_async_copy(source, self.staged.at[way], self.here.at[way])
+
+    def load_own(self):
+        source = self.block(self.place.column, 0, self.rows)
+        return pltpu.make_async_copy(source, self.own, self.here.at[2])
+
+    def store(self):
+        return pltpu.make_async_copy(self.own, self.out, self.here.at[3])
+
+    def start(self):
+        for way in range(2):
+            self.one(way).start()
+        for way in range(2):
+            self.load(way).start()
+        self.load_own().start()
+
+    def middle(self):
+        count = self.rows // 2
+        for way in range(2):
+            self.one(way).wait_recv()
+            self.load(1 - way).wait()
+
+            @pl.loop(0, count // 16)
+            def _(step):
+                rows = pl.ds(pl.multiple_of(way * count + step * 16, 16), 16)
+                self.staged[1 - way, rows, :] = (
+                    self.staged[1 - way, rows, :].astype(F32) + self.first[rows, :].astype(F32)
+                ).astype(BF)
+
+            self.two(1 - way).start()
+
+    def finish(self):
+        self.load_own().wait()
+        for way in range(2):
+            self.two(way).wait_recv()
+
+        @pl.loop(0, self.rows // 16)
+        def _(step):
+            rows = pl.ds(pl.multiple_of(step * 16, 16), 16)
+            self.own[rows, :] = (
+                self.own[rows, :].astype(F32)
+                + self.second[0, rows, :].astype(F32)
+                + self.second[1, rows, :].astype(F32)
+            ).astype(BF)
+
+        self.store().start()
+        for way in range(2):
+            self.one(way).wait_send()
+            self.two(way).wait_send()
+        self.store().wait()
+
+
 class Loads:
     def __init__(self, *loads):
         self.loads = loads
         self.operands = [operand for _, operand in loads]
         self.outs_like = [out for kind, operand in loads for out in kind.outs(operand)]
-        self.scratch = [sem for kind, _ in loads for sem in kind.scratch]
+        self.scratch = [item for kind, operand in loads for item in scratch_of(kind, operand)]
 
     def peers(self, place, base):
         found = {id(peer): peer for peer in base}
@@ -1153,7 +1267,7 @@
     def begin(self, place, ins, outs, sems):
         result, at, sem_at = [], 0, 0
         for (kind, operand), source in zip(self.loads, ins):
-            count, sem_count = len(kind.outs(operand)), len(kind.scratch)
+            count, sem_count = len(kind.outs(operand)), len(scratch_of(kind, operand))
             result.append(
                 kind(
                     place,
@@ -1414,7 +1528,7 @@
                 sum_ref[0] += product_rows[:8] + product_rows[8:]
                 sum_ref[1] += total[:8] + total[8:]
 
-        if k == 1:
+        if k == chunks // 4:
             for each in carried:
                 each.middle()
         if kind != "half":
@@ -1436,7 +1550,7 @@
     w = w if isinstance(w, tuple) else (w,)
     width = w[0].shape[0]
     rows = length // 2
-    chunks = 4
+    chunks = 8 if depth < 2048 else 4
     whole = pl.BlockSpec(memory_space=pltpu.VMEM)
     if kind == "norm":
         gain, bias = others
@@ -2237,6 +2351,7 @@
         feed_near,
         cross_query_grad,
         cross_out_grad,
+        context_grad,
     ) = exchange(
         "back",
         3,
@@ -2247,10 +2362,12 @@
         cross_gain,
         load=Loads((Return, gate_sums), (SwapCoreHalf, feed)),
         window=1,
-        works=Works(("tn", normed_two_all, grad_cross_q), ("tn", grad_two_all, crossed)),
-    )
-    context_grad = dot_tn(item_prompt, grad_context).astype(BF).reshape(side_full.shape[0], -1)
-    cross_local = jnp.concatenate([cross_query_grad, cross_out_grad, context_grad], axis=1)
+        works=Works(
+            ("tn", normed_two_all, grad_cross_q),
+            ("tn", grad_two_all, crossed),
+            ("tn", item_prompt, grad_context),
+        ),
+    )
     feed_half = feed[:half_rows].astype(F32) + feed_near.astype(F32)
     feed_here = jnp.where(odd, feed_half[rows:], feed_half[:rows])
     feed_away = jnp.where(odd, feed_half[:rows], feed_half[rows:]).astype(BF)
@@ -2266,12 +2383,20 @@
     )
     residual_here = jnp.where(odd, residual_two[rows:], residual_two[:rows])
     output_here = (residual_here + feed_here + feed_far.astype(F32) + down_bias).astype(BF)
-    cross_total = plane_sum(cross_local)
     self_out_local = dot_tn(grad_one_all, attended).astype(BF)
     qkv_local = dot_tn(normed_one, grad_projected).astype(BF)
     self_local = jnp.concatenate([qkv_local, self_out_local], axis=1)
     self_total = plane_sum(self_local)
-    grad_in, self_sums, down_near, down_far, output_far = exchange(
+    (
+        grad_in,
+        self_sums,
+        down_near,
+        down_far,
+        output_far,
+        cross_query_total,
+        cross_out_total,
+        context_total,
+    ) = exchange(
         "half",
         4,
         after(grad_projected, self_local),
@@ -2279,7 +2404,13 @@
         residual_mine,
         grad_one_all,
         self_gain,
-        load=Loads((Return, down_sums), (SwapRoute, output_here)),
+        load=Loads(
+            (Return, down_sums),
+            (SwapRoute, output_here),
+            (PlaneSum, cross_query_grad),
+            (PlaneSum, cross_out_grad),
+            (PlaneSum, context_grad),
+        ),
     )
     sums = jnp.concatenate(
         [
@@ -2294,9 +2425,14 @@
     share = sums.shape[1] // 8
     pieces = jnp.swapaxes(sums.reshape(8, 8, share), 0, 1)
     pieces = jnp.pad(pieces, ((0, 0), (0, 0), (0, 256 - share))).reshape(64, 256)
-    whole, token_rows, sums, cross_near, cross_far, self_near, self_far = spread_gradient(
-        8, grad_in, pieces, Loads((Return, cross_total), (Return, self_total))
-    )
+    totals = (cross_query_total, cross_out_total, context_total, self_total)
+    whole, token_rows, sums, *ends = spread_gradient(
+        8, grad_in, pieces, Loads(*[(Return, total) for total in totals])
+    )
+    cross_query_grad, cross_out_grad, context_grad, self_grads = [
+        returned(total, ends[2 * k], ends[2 * k + 1], core, owner)
+        for k, total in enumerate(totals)
+    ]
     sums = jnp.sum(sums.reshape(16, 8, 256), axis=0)[:, :share]
     output = jnp.where(owner, output_here, output_far)
     latents_grad = whole[1:]
@@ -2311,8 +2447,6 @@
         my_features.astype(BF), token_rows, (((0,), (0,)), ((), ())), preferred_element_type=F32
     )
 
-    cross_grads = returned(cross_total, cross_near, cross_far, core, owner)
-    self_grads = returned(self_total, self_near, self_far, core, owner)
     qkv_columns = qkv_full.shape[1]
     gate_grad = returned(gate_sums, gate_near, gate_far, core, owner)
     up_grad = returned(up_sums, up_near, up_far, core, owner)
@@ -2327,9 +2461,9 @@
         self_grads[:, qkv_columns:].T,
         sums[2],
         sums[3],
-        cross_grads[:, :n],
-        cross_grads[:, 2 * n :].reshape(context_weight.shape),
-        cross_grads[:, n : 2 * n].T,
+        cross_query_grad,
+        context_grad.reshape(context_weight.shape),
+        cross_out_grad.T,
         sums[4],
         sums[5],
         jnp.stack([gate_grad, up_grad], axis=1),

time: 714 us -> 705 us (0.987)
    dot_general x5 -> x4, matrix products: 27.5 us -> 26.2 us  [dot_tn(): lax.dot_general(left, right, (((0,), (0,)), ((), ())), preferred_element_...]
  transfers between devices with their start and end apart: 8 -> 7, of which waited for: 2 -> 1; matrix products, arithmetic and copies ran while one was open for 10% -> 9% of each run, Pallas kernels for 49% -> 50%
where the time goes in v4:
time: 705 us; the launch traced here: 699 us
  Pallas kernels  578 us (82%)
  matrix products  42.3 us (6%)
  local copies, waits for them, and re-layouts  33.6 us (5%)
  other arithmetic  25.9 us (4%)
  between operations  16.8 us (2%)
    pallas_call x5, Pallas kernels, exchange(): pl.pallas_call(functools.partial(exchange_kernel, kind, chunks, window, l...  298 us
    pallas_call x1, Pallas kernels, opening(): pl.pallas_call(opening_kernel, grid=(pairs,), in_specs=[ANYWHERE] * 8 + [...  114 us
    pallas_call x1, Pallas kernels, spread_gradient(): pl.pallas_call(functools.partial(spread_kernel, load, chunks), in_specs=[...  89.6 us
    pallas_call x1, Pallas kernels, self_attention_back(): pl.pallas_call(functools.partial(attention_backward_kernel, HD, 256, True...  35.7 us
    pallas_call x1, Pallas kernels, feed_forward(): pl.pallas_call(feed_kernel, grid=(steps,), in_specs=[fixed, fixed, pl.Blo...  26.4 us
    dot_general x4, matrix products, dot_tn(): lax.dot_general(left, right, (((0,), (0,)), ((), ())), preferred_element_...  26.2 us
    dot_general x4, matrix products, dot_nn(): lax.dot_general(left, right, (((1,), (0,)), ((), ())), preferred_element_...  15.1 us
  transfers between devices with their start and end apart: 7, of which 1 were waited for; matrix products, arithmetic and copies ran while one was open for 9% of the time, Pallas kernels for 50%

profile of v4, /device:TPU:1, one launch (start us, length us, event | category | flops | bytes accessed | tf_op | source)
XLA Modules:
  0.0 698.8 jit_solution(2364622089975746774)
XLA Ops:
  8.9 1.3 broadcast_in_dim.70.refs_8_.refs_4_
  10.2 1.3 broadcast_in_dim.71.refs_9_
  11.4 1.0 reshape.110
  12.4 1.8 copy.60
  14.2 2.4 copy.61
  16.7 2.4 pad.8.refs_3_
  19.1 0.9 pad_maximum_fusion.4.refs_1_
  20.0 0.6 broadcast_in_dim.69.refs_7_
  20.6 0.6 broadcast_in_dim.67.refs_6_
  21.2 114.0 %opening.1 = (bf16[1024,1536]{1,0:T(8,128)(2,1)}, bf16[1024,384]{1,0:T(8,128)(2,1)}, bf16[1024,384]{1,0:T(8,128)(2,1)}, bf16[1024,384]{1,0:T(8,128)(2,1)}, bf16[...) custom-call(bf16[192,1152]{1,0:T(8,128)(2,1)} %bitcast.74, ...), custom_call_target="tpu_custom_call" | custom-call | flops 5234491392 | bytes 200000000 | tf_op jit(solution)/shard_map/opening/pallas_call | solution.py:2144
  135.5 0.6 broadcast_in_dim.72.refs_3_.refs_4_
  136.1 0.6 broadcast_in_dim.73.refs_4_
  136.7 68.7 %exchange_norm.2 = (f32[512,1536]{1,0:T(8,128)}, bf16[1024,1536]{1,0:T(8,128)(2,1)}, bf16[384,1536]{1,0:T(8,128)(2,1)}, bf16[256,1536]{1,0:T(8,128)(2,1)}) custom-call(bf16[1024,384]{1,0:T(8,128)(2,1)} %get-tuple-element.83.refs_0_, bf16[1536,1536]{1,0:T(8,128)(2,1)} %get-tuple-element.84.refs_1_, f32[512,1536]{1,0:T(8,128)} %get-tuple-element.85.refs_2_, ...), custom_call_target="tpu_custom_call" | custom-call | flops 1207959552 | bytes 100000000 | tf_op jit(solution)/shard_map/exchange_norm/pallas_call | solution.py:1584
  205.3 1.3 broadcast_select_fusion.2
  206.7 1.4 slice.149
  208.1 1.2 slice.150
  209.3 0.4 reshape.112
  210.3 1.0 broadcast_select_fusion.3.refs_11_
  211.3 0.7 fusion.9.bias_ref.refs_5_
  212.0 1.0 convolution_convert_fusion.7.k_ref.v_ref.refs_1_.refs_2_
  213.0 4.9 convolution_convert_fusion.6.q_ref.refs_0_
  217.9 6.4 cross_attention.1
  224.3 1.4 collective-permute-done
  225.8 1.3 broadcast_select_fusion.1
  227.3 0.8 broadcast_in_dim.76.refs_3_.refs_4_
  228.1 0.6 broadcast_in_dim.77.refs_4_
  228.7 46.1 %exchange_norm.3 = (f32[512,1536]{1,0:T(8,128)}, bf16[1024,1536]{1,0:T(8,128)(2,1)}, bf16[1536,1536]{1,0:T(8,128)(2,1)}) custom-call(bf16[1024,384]{1,0:T(8,128)(2,1)} %get-tuple-element.89.refs_0_.refs_10_, bf16[1536,1536]{1,0:T(8,128)(2,1)} %get-tuple-element.84.refs_1_, f32[512,1536]{1,0:T(8,128)} %get-tuple-element.90.refs_2_, ...), custom_call_target="tpu_custom_call" | custom-call | flops 1207959552 | bytes 100000000 | tf_op jit(solution)/shard_map/exchange_norm/pallas_call | solution.py:1584
  274.8 3.3 pad_maximum_fusion.1.cot_ref.refs_7_
  278.1 26.4 %feed_forward.1 = (bf16[1024,1536]{1,0:T(8,128)(2,1)}, bf16[1024,3072]{1,0:T(8,128)(2,1)}) custom-call(bf16[1024,1536]{1,0:T(8,128)(2,1)} %get-tuple-element.93.n_ref, bf16[1024,1536]{1,0:T(8,128)(2,1)} %pad_maximum_fusion.1.cot_ref.refs_7_, bf16[1536,3072]{1,0:T(8,128)(2,1)} %all-gather.2.cloned.1.call-done.gate_ref.up_ref.refs_1_, ...), custom_call_target="tpu_custom_call" | custom-call | flops 14495514624 | bytes 30000000 | tf_op jit(solution)/shard_map/feed_forward/pallas_call | solution.py:1798
  304.5 8.6 %convolution_convert_fusion.2 = bf16[1536,1536]{1,0:T(8,128)(2,1)} fusion(bf16[1024,1536]{1,0:T(8,128)(2,1)S(1)} %copy-done.41, bf16[1024,3072]{1,0:T(8,128)(2,1)} %get-tuple-element.101.refs_0_), kind=kOutput, calls=%fused_computation.2 | convolution fusion | flops 4834197504 | bytes 11010048 | tf_op jit(solution)/shard_map/dot_general | solution.py:787
  313.4 8.8 %convolution_convert_fusion.1 = bf16[1536,1536]{1,0:T(8,128)(2,1)} fusion(bf16[1024,1536]{1,0:T(8,128)(2,1)S(1)} %copy-done.41, bf16[1024,3072]{1,0:T(8,128)(2,1)} %get-tuple-element.101.refs_0_), kind=kOutput, calls=%fused_computation.1 | convolution fusion | flops 4834197504 | bytes 11010048 | tf_op jit(solution)/shard_map/dot_general | solution.py:787
  322.3 54.8 %exchange_back.2 = (bf16[1024,1536]{1,0:T(8,128)(2,1)}, f32[2,8,1536]{2,1,0:T(8,128)}, bf16[1024,1536]{1,0:T(8,128)(2,1)}, bf16[1536,1536]{1,0:T(8,128)(2,1)}) custom-call(bf16[1024,3072]{1,0:T(8,128)(2,1)} %get-tuple-element.101.refs_0_, bf16[1536,3072]{1,0:T(8,128)(2,1)} %all-gather.2.cloned.1.call-done.gate_ref.up_ref.refs_1_, ...), custom_call_target="tpu_custom_call" | custom-call | flops 9663676416 | bytes 100000000 | tf_op jit(solution)/shard_map/exchange_back/pallas_call | solution.py:1584
  377.2 2.6 copy-done.2
  379.7 3.9 convolution_convert_fusion.5.refs_3_
  383.7 8.0 %cross_attention_back.1 = (bf16[1024,384]{1,0:T(8,128)(2,1)}, bf16[128,768]{1,0:T(8,128)(2,1)}) custom-call(bf16[1024,384]{1,0:T(8,128)(2,1)} %convolution_convert_fusion.6.q_ref.refs_0_, bf16[128,768]{1,0:T(8,128)(2,1)} %convolution_convert_fusion.7.k_ref.v_ref.refs_1_.refs_2_, bf16[128,768]{1,0:T(8,128)(2,1)} %convolution_convert_fusion.7.k_ref.v_ref.refs_1_.refs_2_, ...), custom_call_target="tpu_custom_call" | custom-call | flops 503316480 | bytes 3145728 | tf_op jit(solution)/shard_map/cross_attention_back/pallas_call | solution.py:752
  391.7 57.7 %exchange_back.3 = (bf16[1024,1536]{1,0:T(8,128)(2,1)}, f32[2,8,1536]{2,1,0:T(8,128)}, bf16[192,1536]{1,0:T(8,128)(2,1)}, bf16[192,1536]{1,0:T(8,128)(2,1)}, bf1...) custom-call(bf16[1024,384]{1,0:T(8,128)(2,1)} %get-tuple-element.106.r, ...), custom_call_target="tpu_custom_call" | custom-call | flops 1207959552 | bytes 100000000 | tf_op jit(solution)/shard_map/exchange_back/pallas_call | solution.py:1584
  449.5 5.3 convolution_convert_fusion.4.refs_3_
  454.8 0.4 convert_add_fusion
  455.2 1.0 select_convert_fusion.refs_8_
  456.3 35.7 %self_attention_back.1 = (bf16[1024,1152]{1,0:T(8,128)(2,1)}, bf16[192,1536]{1,0:T(8,128)(2,1)}, bf16[192,1536]{1,0:T(8,128)(2,1)}, bf16[256,1536]{1,0:T(8,128)(2,1)}) custom-call(bf16[1024,384]{1,0:T(8,128)(2,1)} %get-tuple-element.109.refs_0_, bf16[1024,384]{1,0:T(8,128)(2,1)} %get-tuple-element.110.refs_1_, bf16[1024,384]{1,0:T(8,128)(2,1)} %get-tuple-element.111.refs_2_, ...), custom_call_target="tpu_custom_call" | custom-call | flops 4026531840 | bytes 100000000 | tf_op jit(solution)/shard_map/self_attention_back/pallas_call | solution.py:701
  492.0 4.1 convolution_convert_fusion.3
  496.1 4.8 convolution_convert_fusion
  500.8 2.5 pad_maximum_fusion
  503.4 0.8 slice.196
  504.2 1.6 convert_reduce_fusion
  506.2 2.0 add_bitcast_fusion.2
  509.0 3.2 copy.53
  512.2 1.6 add_convert_fusion.refs_6_
  513.8 70.5 %exchange_half.1 = (bf16[512,1536]{1,0:T(8,128)(2,1)}, f32[2,8,1536]{2,1,0:T(8,128)}, bf16[192,1536]{1,0:T(8,128)(2,1)}, bf16[192,1536]{1,0:T(8,128)(2,1)}, bf16...) custom-call(bf16[1024,1152]{1,0:T(8,128)(2,1)} %get-tuple-element.117.ref, ...), custom_call_target="tpu_custom_call" | custom-call | flops 3623878656 | bytes 100000000 | tf_op jit(solution)/shard_map/exchange_half/pallas_call | solution.py:1584
  584.3 1.1 reduce_sum.45
  585.6 0.6 pad_bitcast_fusion.refs_1_
  586.2 2.1 select_bitcast_fusion
  588.3 1.3 add_bitcast_fusion
  589.6 89.6 %spread_gradient.1 = (bf16[1024,1536]{1,0:T(8,128)(2,1)}, bf16[128,1536]{1,0:T(8,128)(2,1)}, f32[128,256]{1,0:T(8,128)}, bf16[192,384]{1,0:T(8,128)(2,1)}, bf16[...) custom-call(bf16[512,1536]{1,0:T(8,128)(2,1)} %get-tuple-element.124, ...), custom_call_target="tpu_custom_call" | custom-call | bytes 100000000 | tf_op jit(solution)/shard_map/spread_gradient/pallas_call | solution.py:1741
  679.2 1.6 convert_add_fusion.1
  680.8 0.7 slice_bitcast_fusion.1
  681.7 0.9 reshape.118
  682.6 4.4 slice_bitcast_fusion
  687.0 1.0 slice.205
  688.0 0.6 fusion.29
  688.6 1.0 copy.66
  689.6 0.8 add_bitcast_fusion.3
  690.4 0.8 convert_add_fusion.3
  691.1 1.0 fusion.10
  (124 shorter events, 2.5 us)
Async XLA Ops:
  7.2 9.5 %copy-start.7 = (bf16[1,1023,1536]{2,1,0:T(8,128)(2,1)S(1)}, bf16[1,1023,1536]{2,1,0:T(8,128)(2,1)}, u32[]{:S(2)}) copy-start(bf16[1,1023,1536]{2,1,0:T(8,128)(2,1)} %param.24) | copy-start | bytes 9427972
  7.2 270.9 %all-gather.2.cloned.1.call-start = ((), (), s32[]{:S(2)}) async-start(), calls=%async_computation.4 | async-start | bytes 11796480 | tf_op jit(solution)/shard_map/all_gather | solution.py:811
  16.7 2.4 copy-start.24
  16.7 2.4 copy-start.25
  16.7 2.4 copy-start.26
  21.2 114.3 %copy-start.37 = (f32[1536]{0:T(1024)S(1)}, f32[1536]{0:T(1024)}, u32[]{:S(2)}) copy-start(f32[1536]{0:T(1024)} %param.33) | copy-start | bytes 18436
  21.2 114.9 %copy-start.38 = (f32[1536]{0:T(1024)S(1)}, f32[1536]{0:T(1024)}, u32[]{:S(2)}) copy-start(f32[1536]{0:T(1024)} %param.34) | copy-start | bytes 18436
  135.2 256.5 %reduce-scatter.5.cloned.1.call-start = ((), (), s32[]{:S(2)}) async-start(), calls=%async_computation.5 | async-start | bytes 5898240 | tf_op jit(solution)/shard_map/reduce_scatter | solution.py:815
  136.7 68.7 %copy-start.9 = (bf16[1,256,1536]{2,1,0:T(8,128)(2,1)S(1)}, bf16[1,256,1536]{2,1,0:T(8,128)(2,1)}, u32[]{:S(2)}) copy-start(bf16[1,256,1536]{2,1,0:T(8,128)(2,1)} %param.43) | copy-start | bytes 2359300
  205.3 5.0 copy-start.23
  206.6 19.2 %collective-permute-start = (bf16[256,1536]{1,0:T(8,128)(2,1)S(1)}, bf16[256,1536]{1,0:T(8,128)(2,1)}, u32[]{:S(2)}, u32[]{:S(2)}) collective-permute-start(bf16[256,1536]{1,0:T(8,128)(2,1)S(1)} %broadcast_select_fusion.2), channel_id=1, source_target_pairs={{0,1},{1,0},{2,3},{3,2},{4,5},{5,4},{6,7},{7,6},{8,9},{9,8},{10,11... | collective-permute-start | bytes 2359304 | tf_op jit(solution)/shard_map/ppermute | solution.py:548
  211.3 6.6 copy-start.11
  225.8 1.5 copy-start.39
  225.8 2.3 copy-start.40
  227.0 47.8 %copy-start = (bf16[256,1536]{1,0:T(8,128)(2,1)}, bf16[256,1536]{1,0:T(8,128)(2,1)S(1)}, u32[]{:S(2)}) copy-start(bf16[256,1536]{1,0:T(8,128)(2,1)S(1)} %get-tuple-element.183) | copy-start | bytes 2359300
  227.1 47.8 %copy-start.1 = (bf16[256,1536]{1,0:T(8,128)(2,1)}, bf16[256,1536]{1,0:T(8,128)(2,1)S(1)}, u32[]{:S(2)}) copy-start(bf16[256,1536]{1,0:T(8,128)(2,1)S(1)} %get-tuple-element.184) | copy-start | bytes 2359300
  227.2 47.6 %copy-start.12 = (bf16[512,1536]{1,0:T(8,128)(2,1)}, bf16[512,1536]{1,0:T(8,128)(2,1)S(1)}, u32[]{:S(2)}) copy-start(bf16[512,1536]{1,0:T(8,128)(2,1)S(1)} %pad_maximum_fusion.3.refs_3_) | copy-start | bytes 4718596
  227.2 47.6 %collective-permute-start.1 = (bf16[512,1536]{1,0:T(8,128)(2,1)S(1)}, bf16[512,1536]{1,0:T(8,128)(2,1)}, u32[]{:S(2)}, u32[]{:S(2)}) collective-permute-start(bf16[512,1536]{1,0:T(8,128)(2,1)S(1)} %pad_maximum_fusion.3.refs_3_), channel_id=1, source_target_pairs={{0,4},{1,5},{2,6},{3,7},{4,0},{5,1},{6,2},{7,3},{8,12},{9,13},{10,... | collective-permute-start | bytes 4718600 | tf_op jit(solution)/shard_map/ppermute | solution.py:548
  278.1 26.4 %copy-start.41 = (bf16[1024,1536]{1,0:T(8,128)(2,1)S(1)}, bf16[1024,1536]{1,0:T(8,128)(2,1)}, u32[]{:S(2)}) copy-start(bf16[1024,1536]{1,0:T(8,128)(2,1)} %get-tuple-element.93.n_ref) | copy-start | bytes 9437188
  313.2 143.1 %reduce-scatter.7.cloned.1.call-start = ((), (), s32[]{:S(2)}) async-start(), calls=%async_computation.6 | async-start | bytes 5898240 | tf_op jit(solution)/shard_map/reduce_scatter | solution.py:815
  322.2 191.6 %reduce-scatter.9.cloned.1.call-start = ((), (), s32[]{:S(2)}) async-start(), calls=%async_computation.7 | async-start | bytes 5898240 | tf_op jit(solution)/shard_map/reduce_scatter | solution.py:815
  377.1 2.7 copy-start.2
  377.1 212.5 %reduce-scatter.11.cloned.1.call-start = ((), (), s32[]{:S(2)}) async-start(), calls=%async_computation.8 | async-start | bytes 5898240 | tf_op jit(solution)/shard_map/reduce_scatter | solution.py:815
  449.4 5.4 copy-start.4
  449.4 5.3 copy-start.13
  491.9 4.1 copy-start.10
  492.0 4.1 copy-start.42
  503.4 2.6 copy-start.34
  503.4 2.7 copy-start.35
  506.2 2.0 copy-start.17
  506.2 2.1 copy-start.19
  506.2 2.3 copy-start.20
  508.9 3.3 copy-start.8
  508.9 3.3 copy-start.18
  509.0 3.2 copy-start.36
  513.8 72.4 %copy-start.3 = (bf16[256,1536]{1,0:T(8,128)(2,1)S(1)}, bf16[256,1536]{1,0:T(8,128)(2,1)}, u32[]{:S(2)}) copy-start(bf16[256,1536]{1,0:T(8,128)(2,1)} %add_convert_fusion.refs_6_) | copy-start | bytes 2359300
  584.3 4.0 copy-start.5
  584.3 4.0 copy-start.21
  584.3 4.0 copy-start.22
  589.6 89.6 %copy-start.6 = (bf16[384,1536]{1,0:T(8,128)(2,1)S(1)}, bf16[384,1536]{1,0:T(8,128)(2,1)}, u32[]{:S(2)}) copy-start(bf16[384,1536]{1,0:T(8,128)(2,1)} %reduce-scatter.11.cloned.1.call-done.refs_5_) | copy-start | bytes 3538948
  679.2 2.4 copy-start.16
  679.2 2.4 copy-start.31
  679.2 2.4 copy-start.32
  682.6 5.4 copy-start.33
  682.6 7.0 copy-start.15
  682.6 7.0 copy-start.29
  682.6 7.0 copy-start.30
  682.6 7.8 %copy-start.14 = (bf16[384,384]{1,0:T(8,128)(2,1)S(1)}, bf16[384,384]{1,0:T(8,128)(2,1)}, u32[]{:S(2)}) copy-start(bf16[384,384]{1,0:T(8,128)(2,1)} %get-tuple-element.128.refs_2_) | copy-start | bytes 884740
  682.6 7.8 %copy-start.27 = (bf16[192,384]{1,0:T(8,128)(2,1)S(1)}, bf16[192,384]{1,0:T(8,128)(2,1)}, u32[]{:S(2)}) copy-start(bf16[192,384]{1,0:T(8,128)(2,1)} %get-tuple-element.137) | copy-start | bytes 442372
  682.6 7.7 %copy-start.28 = (bf16[192,384]{1,0:T(8,128)(2,1)S(1)}, bf16[192,384]{1,0:T(8,128)(2,1)}, u32[]{:S(2)}) copy-start(bf16[192,384]{1,0:T(8,128)(2,1)} %get-tuple-element.138) | copy-start | bytes 442372
Sparse Core Ops, SparseCore 0:
  135.3 95.8 all-gather.1
  313.3 54.8 reduce-scatter.4
  371.2 57.0 reduce-scatter.6
  431.2 57.2 reduce-scatter.8
  503.5 74.8 reduce-scatter.10

commit v5 on v4

--- a/solution.py
+++ b/solution.py
@@ -1282,20 +1282,18 @@
 
 class Works:
     def __init__(self, *works):
-        self.kinds = [kind for kind, _, _ in works]
-        self.operands = [operand for _, left, right in works for operand in (left, right)]
+        self.works = works
         self.unique = []
-        for operand in self.operands:
-            if not any(operand is other for other in self.unique):
-                self.unique.append(operand)
-        self.places = [
-            [at for at, other in enumerate(self.unique) if other is operand][0]
-            for operand in self.operands
-        ]
+        for kind, left, right in works:
+            for operand in (left,) if kind == "ta" else (left, right):
+                if not any(operand is other for other in self.unique):
+                    self.unique.append(operand)
         self.outs_like = []
         for kind, left, right in works:
             if kind == "nt":
                 shape = (left.shape[0], right.shape[0])
+            elif kind == "ta":
+                shape = (left.shape[1], right[1])
             else:
                 shape = (left.shape[1], right.shape[1])
             self.outs_like.append(jax.ShapeDtypeStruct(shape, BF))
@@ -1319,16 +1317,23 @@
         ]
         return loads, stores, self_ins, self_outs
 
-    def run(self, state):
+    def run(self, state, summed):
         loads, stores, ins, outs = state
         waited = set()
-        for k, kind in enumerate(self.kinds):
-            pair = self.places[2 * k : 2 * k + 2]
-            for at in pair:
-                if at not in waited:
-                    loads[at].wait()
-                    waited.add(at)
-            left, right, out = ins[pair[0]], ins[pair[1]], outs[k]
+
+        def held(operand):
+            at = [place for place, other in enumerate(self.unique) if other is operand][0]
+            if at not in waited:
+                loads[at].wait()
+                waited.add(at)
+            return ins[at]
+
+        for k, (kind, left, right) in enumerate(self.works):
+            left, out = held(left), outs[k]
+            if kind == "ta":
+                right = summed.at[:, pl.ds(right[0], right[1])]
+            else:
+                right = held(right)
             if kind == "nt":
                 columns = out.shape[1] // 256
 
@@ -1496,7 +1501,7 @@
     for each in carried:
         if each.late:
             each.start()
-    works.run(working)
+    works.run(working, a_ref)
     for each in later:
         each.wait()
     if kind != "norm":
@@ -1598,7 +1603,7 @@
         + load.scratch
         + works.scratch,
         compiler_params=pltpu.CompilerParams(
-            collective_id=place, has_side_effects=True, vmem_limit_bytes=60 * 2**20
+            collective_id=place, has_side_effects=True, vmem_limit_bytes=63 * 2**20
         ),
         cost_estimate=pl.CostEstimate(
             flops=2 * length * depth * width,
@@ -1765,42 +1770,63 @@
     )(half, pieces, *load.operands)
 
 
-def feed_kernel(n_ref, cot_ref, gate_ref, up_ref, down_ref, hidden_ref, grad_ref):
-    here = pl.program_id(0)
+def feed_kernel(
+    n_ref, mine_ref, other_ref, gate_ref, up_ref, down_ref, hidden_ref, grad_ref, cot_out, here
+):
+    step_here = pl.program_id(0)
     length = n_ref.shape[0]
     tile = gate_ref.shape[1]
     half = grad_ref.shape[1] // 2
     block = 256
-    gate_columns = pl.ds(pl.multiple_of(here * tile, tile), tile)
-    up_columns = pl.ds(pl.multiple_of(half + here * tile, tile), tile)
-
-    @pl.loop(0, length // block)
-    def _(step):
-        rows = pl.ds(pl.multiple_of(step * block, block), block)
-        gate = jnp.dot(n_ref[rows, :], gate_ref[...], preferred_element_type=F32)
-        up = jnp.dot(n_ref[rows, :], up_ref[...], preferred_element_type=F32)
-        grad = jnp.dot(cot_ref[rows, :], down_ref[...], preferred_element_type=F32)
-        sigmoid = jax.nn.sigmoid(gate)
-        silu = gate * sigmoid
-        hidden_ref[rows, :] = (silu * up).astype(BF)
-        grad_ref[rows, gate_columns] = (
-            grad * up * sigmoid * (1.0 + gate * (1.0 - sigmoid))
-        ).astype(BF)
-        grad_ref[rows, up_columns] = (grad * silu).astype(BF)
-
-
-def feed_forward(normed, cot, gate_up, down):
+    gate_columns = pl.ds(pl.multiple_of(step_here * tile, tile), tile)
+    up_columns = pl.ds(pl.multiple_of(half + step_here * tile, tile), tile)
+    both = (mine_ref, other_ref)
+    copies = [
+        pltpu.make_async_copy(part, cot_out.at[pl.ds(k * (length // 2), length // 2)], here.at[k])
+        for k, part in enumerate(both)
+    ]
+
+    @pl.when(step_here == 0)
+    def _():
+        for copy in copies:
+            copy.start()
+
+    for k, cot_ref in enumerate(both):
+
+        @pl.loop(0, length // 2 // block)
+        def _(step):
+            source = pl.ds(pl.multiple_of(step * block, block), block)
+            rows = pl.ds(pl.multiple_of(k * (length // 2) + step * block, block), block)
+            gate = jnp.dot(n_ref[rows, :], gate_ref[...], preferred_element_type=F32)
+            up = jnp.dot(n_ref[rows, :], up_ref[...], preferred_element_type=F32)
+            grad = jnp.dot(cot_ref[source, :], down_ref[...], preferred_element_type=F32)
+            sigmoid = jax.nn.sigmoid(gate)
+            silu = gate * sigmoid
+            hidden_ref[rows, :] = (silu * up).astype(BF)
+            grad_ref[rows, gate_columns] = (
+                grad * up * sigmoid * (1.0 + gate * (1.0 - sigmoid))
+            ).astype(BF)
+            grad_ref[rows, up_columns] = (grad * silu).astype(BF)
+
+    @pl.when(step_here == pl.num_programs(0) - 1)
+    def _():
+        for copy in copies:
+            copy.wait()
+
+
+def feed_forward(normed, mine, other, gate_up, down):
     length, width = normed.shape
     hidden_width = down.shape[1]
     tile = 256
     steps = hidden_width // tile
-    fixed = pl.BlockSpec((length, width), lambda j: (0, 0))
+    whole = pl.BlockSpec(memory_space=pltpu.VMEM)
     return pl.pallas_call(
         feed_kernel,
         grid=(steps,),
         in_specs=[
-            fixed,
-            fixed,
+            whole,
+            whole,
+            whole,
             pl.BlockSpec((width, tile), lambda j: (0, j)),
             pl.BlockSpec((width, tile), lambda j: (0, j + steps)),
             pl.BlockSpec((width, tile), lambda j: (0, j)),
@@ -1808,11 +1834,14 @@
         out_specs=[
             pl.BlockSpec((length, tile), lambda j: (0, j)),
             pl.BlockSpec((length, 2 * hidden_width), lambda j: (0, 0)),
+            ANYWHERE,
         ],
         out_shape=[
             jax.ShapeDtypeStruct((length, hidden_width), BF),
             jax.ShapeDtypeStruct((length, 2 * hidden_width), BF),
+            jax.ShapeDtypeStruct((length, width), BF),
         ],
+        scratch_shapes=[pltpu.SemaphoreType.DMA((2,))],
         compiler_params=pltpu.CompilerParams(vmem_limit_bytes=60 * 2**20),
         cost_estimate=pl.CostEstimate(
             flops=6 * length * width * hidden_width,
@@ -1820,7 +1849,7 @@
             bytes_accessed=30_000_000,
         ),
         name="feed_forward",
-    )(normed, cot, gate_up, gate_up, down)
+    )(normed, mine, other, gate_up, gate_up, down)
 
 
 def turn_tables(length, block):
@@ -2320,25 +2349,33 @@
         load=Loads((Plane, down_own)),
         window=2,
     )
-    cot_all = jnp.concatenate([cot_mine, after(cot_other, normed_three_all)], axis=0)
-    hidden, grad_gate_up = feed_forward(normed_three_all, cot_all, gate_up_full, down_full)
+    hidden, grad_gate_up, cot_all = feed_forward(
+        normed_three_all,
+        cot_mine,
+        after(cot_other, normed_three_all),
+        gate_up_full,
+        down_full,
+    )
 
     split = gate_up_weight.shape[2]
     gate_local = dot_tn(normed_three_all, grad_gate_up[:, :split]).astype(BF)
     gate_sums = plane_sum(gate_local)
-    up_local = dot_tn(normed_three_all, after(grad_gate_up, gate_local)[:, split:]).astype(BF)
-    up_sums = plane_sum(up_local)
-    grad_two_all, feed_sums, feed, down_local = exchange(
+    grad_two_all, feed_sums, feed, down_local, up_local = exchange(
         "back",
         2,
-        after(grad_gate_up, up_local),
+        after(grad_gate_up, gate_local),
         gate_up_full,
         residual_two,
         cot_mine,
         feed_gain,
-        works=Works(("nt", hidden, down_full), ("tn", cot_all, hidden)),
-    )
-    down_sums = plane_sum(down_local)
+        works=Works(
+            ("nt", hidden, down_full),
+            ("tn", cot_all, hidden),
+            ("ta", normed_three_all, (split, split)),
+        ),
+    )
+    up_sums = plane_sum(up_local)
+    down_sums = plane_sum(after(down_local, up_local))
     grad_crossed = dot_nn(grad_two_all, cross_out_full).astype(BF)
     grad_cross_q, grad_context = cross_attention_back(
         cross_q, context, mask, grad_crossed, cross_logs
@@ -2385,8 +2422,7 @@
     output_here = (residual_here + feed_here + feed_far.astype(F32) + down_bias).astype(BF)
     self_out_local = dot_tn(grad_one_all, attended).astype(BF)
     qkv_local = dot_tn(normed_one, grad_projected).astype(BF)
-    self_local = jnp.concatenate([qkv_local, self_out_local], axis=1)
-    self_total = plane_sum(self_local)
+    qkv_total = plane_sum(qkv_local)
     (
         grad_in,
         self_sums,
@@ -2396,10 +2432,11 @@
         cross_query_total,
         cross_out_total,
         context_total,
+        self_out_total,
     ) = exchange(
         "half",
         4,
-        after(grad_projected, self_local),
+        after(grad_projected, qkv_local),
         qkv_full,
         residual_mine,
         grad_one_all,
@@ -2410,6 +2447,7 @@
             (PlaneSum, cross_query_grad),
             (PlaneSum, cross_out_grad),
             (PlaneSum, context_grad),
+            (PlaneSum, self_out_local),
         ),
     )
     sums = jnp.concatenate(
@@ -2425,11 +2463,11 @@
     share = sums.shape[1] // 8
     pieces = jnp.swapaxes(sums.reshape(8, 8, share), 0, 1)
     pieces = jnp.pad(pieces, ((0, 0), (0, 0), (0, 256 - share))).reshape(64, 256)
-    totals = (cross_query_total, cross_out_total, context_total, self_total)
+    totals = (cross_query_total, cross_out_total, context_total, self_out_total, qkv_total)
     whole, token_rows, sums, *ends = spread_gradient(
         8, grad_in, pieces, Loads(*[(Return, total) for total in totals])
     )
-    cross_query_grad, cross_out_grad, context_grad, self_grads = [
+    cross_query_grad, cross_out_grad, context_grad, self_out_grad, qkv_grad = [
         returned(total, ends[2 * k], ends[2 * k + 1], core, owner)
         for k, total in enumerate(totals)
     ]
@@ -2447,7 +2485,6 @@
         my_features.astype(BF), token_rows, (((0,), (0,)), ((), ())), preferred_element_type=F32
     )
 
-    qkv_columns = qkv_full.shape[1]
     gate_grad = returned(gate_sums, gate_near, gate_far, core, owner)
     up_grad = returned(up_sums, up_near, up_far, core, owner)
     down_grad = returned(down_sums, down_near, down_far, core, owner)
@@ -2457,8 +2494,8 @@
         time_grad,
         sums[0],
         sums[1],
-        self_grads[:, :qkv_columns].reshape(qkv_weight.shape),
-        self_grads[:, qkv_columns:].T,
+        qkv_grad.reshape(qkv_weight.shape),
+        self_out_grad.T,
         sums[2],
         sums[3],
         cross_query_grad,

time: 705 us -> 694 us (0.984)
    dot_general x4 -> x3, matrix products: 26.2 us -> 20.2 us  [dot_tn(): lax.dot_general(left, right, (((0,), (0,)), ((), ())), preferred_element_...]
  transfers between devices with their start and end apart: 7 -> 7, of which waited for: 1 -> 1; matrix products, arithmetic and copies ran while one was open for 9% -> 8% of each run, Pallas kernels for 50% -> 51%
where the time goes in v5:
time: 694 us; the launch traced here: 689 us
  Pallas kernels  578 us (83%)
  matrix products  36 us (5%)
  local copies, waits for them, and re-layouts  30.1 us (4%)
  other arithmetic  23.1 us (3%)
  between operations  16.8 us (2%)
    pallas_call x5, Pallas kernels, exchange(): pl.pallas_call(functools.partial(exchange_kernel, kind, chunks, window, l...  299 us
    pallas_call x1, Pallas kernels, opening(): pl.pallas_call(opening_kernel, grid=(pairs,), in_specs=[ANYWHERE] * 8 + [...  114 us
    pallas_call x1, Pallas kernels, spread_gradient(): pl.pallas_call(functools.partial(spread_kernel, load, chunks), in_specs=[...  89.7 us
    pallas_call x1, Pallas kernels, self_attention_back(): pl.pallas_call(functools.partial(attention_backward_kernel, HD, 256, True...  35.6 us
    pallas_call x1, Pallas kernels, feed_forward(): pl.pallas_call(feed_kernel, grid=(steps,), in_specs=[whole, whole, whole,...  26.5 us
    dot_general x3, matrix products, dot_tn(): lax.dot_general(left, right, (((0,), (0,)), ((), ())), preferred_element_...  20.2 us
    dot_general x4, matrix products, dot_nn(): lax.dot_general(left, right, (((1,), (0,)), ((), ())), preferred_element_...  14.8 us
  transfers between devices with their start and end apart: 7, of which 1 were waited for; matrix products, arithmetic and copies ran while one was open for 8% of the time, Pallas kernels for 51%

profile of v5, /device:TPU:1, one launch (start us, length us, event | category | flops | bytes accessed | tf_op | source)
XLA Modules:
  0.0 688.7 jit_solution(13667559590700263551)
XLA Ops:
  8.9 1.3 broadcast_in_dim.70.refs_8_.refs_4_
  10.2 1.3 broadcast_in_dim.71.refs_9_
  11.5 1.0 reshape.110
  12.4 1.8 copy.54
  14.2 2.4 copy.55
  16.7 2.4 pad.8.refs_3_
  19.1 0.9 pad_maximum_fusion.2.refs_1_
  20.0 0.6 broadcast_in_dim.69.refs_7_
  20.6 0.6 broadcast_in_dim.67.refs_6_
  21.2 114.0 %opening.1 = (bf16[1024,1536]{1,0:T(8,128)(2,1)}, bf16[1024,384]{1,0:T(8,128)(2,1)}, bf16[1024,384]{1,0:T(8,128)(2,1)}, bf16[1024,384]{1,0:T(8,128)(2,1)}, bf16[...) custom-call(bf16[192,1152]{1,0:T(8,128)(2,1)} %bitcast.73, ...), custom_call_target="tpu_custom_call" | custom-call | flops 5234491392 | bytes 200000000 | tf_op jit(solution)/shard_map/opening/pallas_call | solution.py:2173
  135.9 0.6 broadcast_in_dim.72.refs_3_.refs_4_
  136.4 0.6 broadcast_in_dim.73.refs_4_
  137.0 68.6 %exchange_norm.2 = (f32[512,1536]{1,0:T(8,128)}, bf16[1024,1536]{1,0:T(8,128)(2,1)}, bf16[384,1536]{1,0:T(8,128)(2,1)}, bf16[256,1536]{1,0:T(8,128)(2,1)}) custom-call(bf16[1024,384]{1,0:T(8,128)(2,1)} %get-tuple-element.88.refs_0_, bf16[1536,1536]{1,0:T(8,128)(2,1)} %get-tuple-element.89.refs_1_, f32[512,1536]{1,0:T(8,128)} %get-tuple-element.90.refs_2_, ...), custom_call_target="tpu_custom_call" | custom-call | flops 1207959552 | bytes 100000000 | tf_op jit(solution)/shard_map/exchange_norm/pallas_call | solution.py:1589
  205.6 1.5 broadcast_select_fusion.2
  207.2 1.4 slice.146
  208.6 1.2 slice.147
  210.9 1.0 broadcast_select_fusion.3.refs_11_
  211.8 0.7 fusion.8.bias_ref.refs_5_
  212.5 1.0 convolution_convert_fusion.6.k_ref.v_ref.refs_1_.refs_2_
  213.5 4.9 convolution_convert_fusion.5.q_ref.refs_0_
  218.4 6.4 cross_attention.1
  224.9 1.7 collective-permute-done
  226.5 1.2 broadcast_select_fusion.1
  227.8 0.8 copy-done.2
  228.7 1.2 pad_maximum_fusion.1.mine_ref.refs_3_
  229.9 0.7 collective-permute-start.1
  230.6 0.6 broadcast_in_dim.76.refs_3_.refs_4_
  231.2 0.6 broadcast_in_dim.77.refs_4_
  231.8 45.6 %exchange_norm.3 = (f32[512,1536]{1,0:T(8,128)}, bf16[1024,1536]{1,0:T(8,128)(2,1)}, bf16[1536,1536]{1,0:T(8,128)(2,1)}) custom-call(bf16[1024,384]{1,0:T(8,128)(2,1)} %get-tuple-element.94.refs_0_.refs_10_, bf16[1536,1536]{1,0:T(8,128)(2,1)} %get-tuple-element.89.refs_1_, f32[512,1536]{1,0:T(8,128)} %get-tuple-element.95.refs_2_, ...), custom_call_target="tpu_custom_call" | custom-call | flops 1207959552 | bytes 100000000 | tf_op jit(solution)/shard_map/exchange_norm/pallas_call | solution.py:1589
  277.5 26.5 %feed_forward.1 = (bf16[1024,1536]{1,0:T(8,128)(2,1)}, bf16[1024,3072]{1,0:T(8,128)(2,1)}, bf16[1024,1536]{1,0:T(8,128)(2,1)}) custom-call(bf16[1024,1536]{1,0:T(8,128)(2,1)} %get-tuple-element.98.n_ref.refs_8_, bf16[512,1536]{1,0:T(8,128)(2,1)} %pad_maximum_fusion.1.mine_ref.refs_3_, bf16[512,1536]{1,0:T(8,128)(2,1)} %collective-permute-done.1.other_ref, ...), custom_call_target="tpu_custom_call" | custom-call | flops 14495514624 | bytes 30000000 | tf_op jit(solution)/shard_map/feed_forward/pallas_call | solution.py:1823
  304.0 8.6 %convolution_convert_fusion.1 = bf16[1536,1536]{1,0:T(8,128)(2,1)} fusion(bf16[1024,1536]{1,0:T(8,128)(2,1)S(1)} %copy-done.42, bf16[1024,3072]{1,0:T(8,128)(2,1)} %get-tuple-element.105.refs_0_), kind=kOutput, calls=%fused_computation.1 | convolution fusion | flops 4834197504 | bytes 11010048 | tf_op jit(solution)/shard_map/dot_general | solution.py:787
  313.0 54.8 %exchange_back.2 = (bf16[1024,1536]{1,0:T(8,128)(2,1)}, f32[2,8,1536]{2,1,0:T(8,128)}, bf16[1024,1536]{1,0:T(8,128)(2,1)}, bf16[1536,1536]{1,0:T(8,128)(2,1)}, bf16[1536,1536]{1,0:T(8,128)(2,1)}) custom-call(bf16[1024,3072]{1,0:T(8,128)(2,1)} %get-tuple-element.105.refs_0_, bf16[1536,3072]{1,0:T(8,128)(2,1)} %all-gather.2.cloned.1.call-done.gate_ref.up_ref.refs_1_, ...), custom_call_target="tpu_custom_call" | custom-call | flops 9663676416 | bytes 100000000 | tf_op jit(solution)/shard_map/exchange_back/pallas_call | solution.py:1589
  367.8 0.5 reduce-scatter.9.cloned.1.call-update
  368.9 0.8 copy-done
  369.7 3.9 convolution_convert_fusion.4.refs_3_
  373.7 7.5 %cross_attention_back.1 = (bf16[1024,384]{1,0:T(8,128)(2,1)}, bf16[128,768]{1,0:T(8,128)(2,1)}) custom-call(bf16[1024,384]{1,0:T(8,128)(2,1)} %convolution_convert_fusion.5.q_ref.refs_0_, bf16[128,768]{1,0:T(8,128)(2,1)} %convolution_convert_fusion.6.k_ref.v_ref.refs_1_.refs_2_, bf16[128,768]{1,0:T(8,128)(2,1)} %convolution_convert_fusion.6.k_ref.v_ref.refs_1_.refs_2_, ...), custom_call_target="tpu_custom_call" | custom-call | flops 503316480 | bytes 3145728 | tf_op jit(solution)/shard_map/cross_attention_back/pallas_call | solution.py:752
  381.2 58.4 %exchange_back.3 = (bf16[1024,1536]{1,0:T(8,128)(2,1)}, f32[2,8,1536]{2,1,0:T(8,128)}, bf16[192,1536]{1,0:T(8,128)(2,1)}, bf16[192,1536]{1,0:T(8,128)(2,1)}, bf1...) custom-call(bf16[1024,384]{1,0:T(8,128)(2,1)} %get-tuple-element.111.r, ...), custom_call_target="tpu_custom_call" | custom-call | flops 1207959552 | bytes 100000000 | tf_op jit(solution)/shard_map/exchange_back/pallas_call | solution.py:1589
  439.6 5.0 convolution_convert_fusion.3.refs_3_
  445.1 1.0 select_convert_fusion.refs_8_
  446.1 35.6 %self_attention_back.1 = (bf16[1024,1152]{1,0:T(8,128)(2,1)}, bf16[192,1536]{1,0:T(8,128)(2,1)}, bf16[192,1536]{1,0:T(8,128)(2,1)}, bf16[256,1536]{1,0:T(8,128)(2,1)}) custom-call(bf16[1024,384]{1,0:T(8,128)(2,1)} %get-tuple-element.114.refs_0_, bf16[1024,384]{1,0:T(8,128)(2,1)} %get-tuple-element.115.refs_1_, bf16[1024,384]{1,0:T(8,128)(2,1)} %get-tuple-element.116.refs_2_, ...), custom_call_target="tpu_custom_call" | custom-call | flops 4026531840 | bytes 100000000 | tf_op jit(solution)/shard_map/self_attention_back/pallas_call | solution.py:701
  481.8 8.7 %convolution_convert_fusion = bf16[1536,1152]{1,0:T(8,128)(2,1)} fusion(bf16[1024,1536]{1,0:T(8,128)(2,1)} %get-tuple-element.122, bf16[1024,1152]{1,0:T(8,128)(2,1)} %get-tuple-element.123.refs_0_), kind=kOutput, calls=%fused_computation | convolution fusion | flops 3625648128 | bytes 9043968 | tf_op jit(solution)/shard_map/dot_general | solution.py:787
  490.5 0.8 slice.192
  491.3 1.6 convert_reduce_fusion
  493.3 2.0 add_bitcast_fusion.2
  496.0 3.2 copy.49
  499.3 2.8 convolution_convert_fusion.2.refs_10_
  502.1 1.6 add_convert_fusion.refs_6_
  503.8 71.3 %exchange_half.1 = (bf16[512,1536]{1,0:T(8,128)(2,1)}, f32[2,8,1536]{2,1,0:T(8,128)}, bf16[192,1536]{1,0:T(8,128)(2,1)}, bf16[192,1536]{1,0:T(8,128)(2,1)}, bf16...) custom-call(bf16[1024,1152]{1,0:T(8,128)(2,1)} %get-tuple-element.12, ...), custom_call_target="tpu_custom_call" | custom-call | flops 3623878656 | bytes 100000000 | tf_op jit(solution)/shard_map/exchange_half/pallas_call | solution.py:1589
  575.1 1.1 reduce_sum.45
  576.3 0.6 pad_bitcast_fusion.refs_1_
  577.0 2.1 select_bitcast_fusion
  579.1 1.3 add_bitcast_fusion
  580.4 89.7 %spread_gradient.1 = (bf16[1024,1536]{1,0:T(8,128)(2,1)}, bf16[128,1536]{1,0:T(8,128)(2,1)}, f32[128,256]{1,0:T(8,128)}, bf16[192,384]{1,0:T(8,128)(2,1)}, bf16[...) custom-call(bf16[512,1536]{1,0:T(8,128)(2,1)} %get-tuple-element.131, ...), custom_call_target="tpu_custom_call" | custom-call | bytes 100000000 | tf_op jit(solution)/shard_map/spread_gradient/pallas_call | solution.py:1746
  670.1 1.1 convert_add_fusion.2
  671.2 0.9 reshape.118
  672.1 1.5 convert_add_fusion.1
  673.6 1.0 copy.60
  674.6 2.4 slice_bitcast_fusion
  677.0 1.0 slice.201
  678.0 0.6 fusion.28
  678.6 0.8 add_bitcast_fusion.3
  679.4 0.8 convert_add_fusion.3
  680.2 0.8 add_bitcast_fusion.4
  681.0 1.0 fusion.9
  (120 shorter events, 4.0 us)
Async XLA Ops:
  7.2 9.5 %copy-start.7 = (bf16[1,1023,1536]{2,1,0:T(8,128)(2,1)S(1)}, bf16[1,1023,1536]{2,1,0:T(8,128)(2,1)}, u32[]{:S(2)}) copy-start(bf16[1,1023,1536]{2,1,0:T(8,128)(2,1)} %param.24) | copy-start | bytes 9427972
  7.2 270.3 %all-gather.2.cloned.1.call-start = ((), (), s32[]{:S(2)}) async-start(), calls=%async_computation.4 | async-start | bytes 11796480 | tf_op jit(solution)/shard_map/all_gather | solution.py:811
  16.7 2.4 copy-start.25
  16.7 2.4 copy-start.26
  16.7 2.4 copy-start.27
  135.2 0.7 copy-start.38
  135.2 1.3 copy-start.39
  135.2 246.0 %reduce-scatter.5.cloned.1.call-start = ((), (), s32[]{:S(2)}) async-start(), calls=%async_computation.5 | async-start | bytes 5898240 | tf_op jit(solution)/shard_map/reduce_scatter | solution.py:815
  207.1 19.5 %collective-permute-start = (bf16[256,1536]{1,0:T(8,128)(2,1)S(1)}, bf16[256,1536]{1,0:T(8,128)(2,1)}, u32[]{:S(2)}, u32[]{:S(2)}) collective-permute-start(bf16[256,1536]{1,0:T(8,128)(2,1)S(1)} %broadcast_select_fusion.2), channel_id=1, source_target_pairs={{0,1},{1,0},{2,3},{3,2},{4,5},{5,4},{6,7},{7,6},{8,9},{9,8},{10,11... | collective-permute-start | bytes 2359304 | tf_op jit(solution)/shard_map/ppermute | solution.py:548
  207.2 3.7 copy-start.24
  211.8 6.6 copy-start.11
  227.8 0.9 copy-start.2
  227.8 2.1 copy-start.3
  227.8 2.8 copy-start.40
  227.8 3.4 copy-start.41
  229.9 47.5 %collective-permute-start.1 = (bf16[512,1536]{1,0:T(8,128)(2,1)}, bf16[512,1536]{1,0:T(8,128)(2,1)}, u32[]{:S(2)}, u32[]{:S(2)}) collective-permute-start(bf16[512,1536]{1,0:T(8,128)(2,1)} %pad_maximum_fusion.1.mine_ref.refs_3_), channel_id=1, source_target_pairs={{0,4},{1,5},{2,6},{3,7},{4,0},{5,1},{6,2},{7,3},{8,12},{9,13},{10,... | collective-permute-start | bytes 4718600 | tf_op jit(solution)/shard_map/ppermute | solution.py:548
  277.5 26.5 %copy-start.42 = (bf16[1024,1536]{1,0:T(8,128)(2,1)S(1)}, bf16[1024,1536]{1,0:T(8,128)(2,1)}, u32[]{:S(2)}) copy-start(bf16[1024,1536]{1,0:T(8,128)(2,1)} %get-tuple-element.98.n_ref.refs_8_) | copy-start | bytes 9437188
  312.7 133.4 %reduce-scatter.7.cloned.1.call-start = ((), (), s32[]{:S(2)}) async-start(), calls=%async_computation.6 | async-start | bytes 5898240 | tf_op jit(solution)/shard_map/reduce_scatter | solution.py:815
  367.8 136.0 %reduce-scatter.9.cloned.1.call-start = ((), (), s32[]{:S(2)}) async-start(), calls=%async_computation.7 | async-start | bytes 5898240 | tf_op jit(solution)/shard_map/reduce_scatter | solution.py:815
  367.8 1.9 copy-start
  368.4 212.0 %reduce-scatter.11.cloned.1.call-start = ((), (), s32[]{:S(2)}) async-start(), calls=%async_computation.8 | async-start | bytes 4423680 | tf_op jit(solution)/shard_map/reduce_scatter | solution.py:815
  439.6 5.1 copy-start.4
  439.6 5.0 copy-start.12
  490.4 2.6 copy-start.35
  490.4 2.7 copy-start.36
  493.3 2.0 copy-start.17
  493.3 2.1 copy-start.20
  493.3 2.3 copy-start.21
  496.0 3.2 copy-start.10
  496.0 3.2 copy-start.19
  499.3 2.9 copy-start.8
  499.3 2.9 copy-start.18
  499.3 2.9 copy-start.37
  503.8 73.2 %copy-start.1 = (bf16[256,1536]{1,0:T(8,128)(2,1)S(1)}, bf16[256,1536]{1,0:T(8,128)(2,1)}, u32[]{:S(2)}) copy-start(bf16[256,1536]{1,0:T(8,128)(2,1)} %add_convert_fusion.refs_6_) | copy-start | bytes 2359300
  575.1 4.0 copy-start.5
  575.1 4.0 copy-start.22
  575.1 4.0 copy-start.23
  580.4 89.7 %copy-start.16 = (bf16[192,768]{1,0:T(8,128)(2,1)S(1)}, bf16[192,768]{1,0:T(8,128)(2,1)}, u32[]{:S(2)}) copy-start(bf16[192,768]{1,0:T(8,128)(2,1)} %get-tuple-element.137.refs_4_) | copy-start | bytes 884740
  580.4 91.7 %copy-start.6 = (bf16[384,1152]{1,0:T(8,128)(2,1)S(1)}, bf16[384,1152]{1,0:T(8,128)(2,1)}, u32[]{:S(2)}) copy-start(bf16[384,1152]{1,0:T(8,128)(2,1)} %reduce-scatter.11.cloned.1.call-done.refs_6_) | copy-start | bytes 2654212
  672.1 2.5 copy-start.9
  674.5 3.4 copy-start.34
  674.5 4.1 copy-start.15
  674.5 4.1 copy-start.32
  674.5 4.1 copy-start.33
  674.6 4.8 copy-start.14
  674.6 4.8 copy-start.30
  674.6 4.8 copy-start.31
  674.6 5.6 copy-start.13
  674.6 5.6 copy-start.28
  674.6 5.6 copy-start.29
Sparse Core Ops, SparseCore 0:
  135.3 95.9 all-gather.1
  312.8 54.7 reduce-scatter.4
  370.6 57.1 reduce-scatter.6
  430.6 57.0 reduce-scatter.8
  490.6 69.1 reduce-scatter.10

commit v6 on v5

--- a/solution.py
+++ b/solution.py
@@ -1741,7 +1741,7 @@
 
 def spread_gradient(place, half, pieces, load):
     rows, width = half.shape
-    chunks = 4
+    chunks = 8
     whole = pl.BlockSpec(memory_space=pltpu.VMEM)
     return pl.pallas_call(
         functools.partial(spread_kernel, load, chunks),

time: 694 us -> 694 us (level)
  no operation moved by 1% of the time
where the time goes in v6:
time: 694 us; the launch traced here: 689 us
  Pallas kernels  579 us (83%)
  matrix products  36 us (5%)
  local copies, waits for them, and re-layouts  30.1 us (4%)
  other arithmetic  23.1 us (3%)
  between operations  16.8 us (2%)
    pallas_call x5, Pallas kernels, exchange(): pl.pallas_call(functools.partial(exchange_kernel, kind, chunks, window, l...  299 us
    pallas_call x1, Pallas kernels, opening(): pl.pallas_call(opening_kernel, grid=(pairs,), in_specs=[ANYWHERE] * 8 + [...  114 us
    pallas_call x1, Pallas kernels, spread_gradient(): pl.pallas_call(functools.partial(spread_kernel, load, chunks), in_specs=[...  89.9 us
    pallas_call x1, Pallas kernels, self_attention_back(): pl.pallas_call(functools.partial(attention_backward_kernel, HD, 256, True...  35.6 us
    pallas_call x1, Pallas kernels, feed_forward(): pl.pallas_call(feed_kernel, grid=(steps,), in_specs=[whole, whole, whole,...  26.5 us
    dot_general x3, matrix products, dot_tn(): lax.dot_general(left, right, (((0,), (0,)), ((), ())), preferred_element_...  20.2 us
    dot_general x4, matrix products, dot_nn(): lax.dot_general(left, right, (((1,), (0,)), ((), ())), preferred_element_...  14.8 us
  transfers between devices with their start and end apart: 7, of which 1 were waited for; matrix products, arithmetic and copies ran while one was open for 8% of the time, Pallas kernels for 51%

profile of v6, /device:TPU:1, one launch (start us, length us, event | category | flops | bytes accessed | tf_op | source)
XLA Modules:
  0.0 688.9 jit_solution(10572630370903105082)
XLA Ops:
  8.9 1.3 broadcast_in_dim.70.refs_8_.refs_4_
  10.2 1.3 broadcast_in_dim.71.refs_9_
  11.5 1.0 reshape.110
  12.4 1.8 copy.54
  14.2 2.4 copy.55
  16.7 2.4 pad.8.refs_3_
  19.1 0.9 pad_maximum_fusion.2.refs_1_
  20.0 0.6 broadcast_in_dim.69.refs_7_
  20.6 0.6 broadcast_in_dim.67.refs_6_
  21.2 114.0 %opening.1 = (bf16[1024,1536]{1,0:T(8,128)(2,1)}, bf16[1024,384]{1,0:T(8,128)(2,1)}, bf16[1024,384]{1,0:T(8,128)(2,1)}, bf16[1024,384]{1,0:T(8,128)(2,1)}, bf16[...) custom-call(bf16[192,1152]{1,0:T(8,128)(2,1)} %bitcast.73, ...), custom_call_target="tpu_custom_call" | custom-call | flops 5234491392 | bytes 200000000 | tf_op jit(solution)/shard_map/opening/pallas_call | solution.py:2173
  135.9 0.6 broadcast_in_dim.72.refs_3_.refs_4_
  136.4 0.6 broadcast_in_dim.73.refs_4_
  137.0 68.6 %exchange_norm.2 = (f32[512,1536]{1,0:T(8,128)}, bf16[1024,1536]{1,0:T(8,128)(2,1)}, bf16[384,1536]{1,0:T(8,128)(2,1)}, bf16[256,1536]{1,0:T(8,128)(2,1)}) custom-call(bf16[1024,384]{1,0:T(8,128)(2,1)} %get-tuple-element.88.refs_0_, bf16[1536,1536]{1,0:T(8,128)(2,1)} %get-tuple-element.89.refs_1_, f32[512,1536]{1,0:T(8,128)} %get-tuple-element.90.refs_2_, ...), custom_call_target="tpu_custom_call" | custom-call | flops 1207959552 | bytes 100000000 | tf_op jit(solution)/shard_map/exchange_norm/pallas_call | solution.py:1589
  205.6 1.5 broadcast_select_fusion.2
  207.2 1.4 slice.146
  208.6 1.2 slice.147
  210.9 1.0 broadcast_select_fusion.3.refs_11_
  211.8 0.7 fusion.8.bias_ref.refs_5_
  212.5 1.0 convolution_convert_fusion.6.k_ref.v_ref.refs_1_.refs_2_
  213.5 4.9 convolution_convert_fusion.5.q_ref.refs_0_
  218.4 6.4 cross_attention.1
  224.9 1.7 collective-permute-done
  226.5 1.2 broadcast_select_fusion.1
  227.8 0.8 copy-done.2
  228.7 1.2 pad_maximum_fusion.1.mine_ref.refs_3_
  229.9 0.7 collective-permute-start.1
  230.6 0.6 broadcast_in_dim.76.refs_3_.refs_4_
  231.2 0.6 broadcast_in_dim.77.refs_4_
  231.8 45.6 %exchange_norm.3 = (f32[512,1536]{1,0:T(8,128)}, bf16[1024,1536]{1,0:T(8,128)(2,1)}, bf16[1536,1536]{1,0:T(8,128)(2,1)}) custom-call(bf16[1024,384]{1,0:T(8,128)(2,1)} %get-tuple-element.94.refs_0_.refs_10_, bf16[1536,1536]{1,0:T(8,128)(2,1)} %get-tuple-element.89.refs_1_, f32[512,1536]{1,0:T(8,128)} %get-tuple-element.95.refs_2_, ...), custom_call_target="tpu_custom_call" | custom-call | flops 1207959552 | bytes 100000000 | tf_op jit(solution)/shard_map/exchange_norm/pallas_call | solution.py:1589
  277.5 26.5 %feed_forward.1 = (bf16[1024,1536]{1,0:T(8,128)(2,1)}, bf16[1024,3072]{1,0:T(8,128)(2,1)}, bf16[1024,1536]{1,0:T(8,128)(2,1)}) custom-call(bf16[1024,1536]{1,0:T(8,128)(2,1)} %get-tuple-element.98.n_ref.refs_8_, bf16[512,1536]{1,0:T(8,128)(2,1)} %pad_maximum_fusion.1.mine_ref.refs_3_, bf16[512,1536]{1,0:T(8,128)(2,1)} %collective-permute-done.1.other_ref, ...), custom_call_target="tpu_custom_call" | custom-call | flops 14495514624 | bytes 30000000 | tf_op jit(solution)/shard_map/feed_forward/pallas_call | solution.py:1823
  304.0 8.6 %convolution_convert_fusion.1 = bf16[1536,1536]{1,0:T(8,128)(2,1)} fusion(bf16[1024,1536]{1,0:T(8,128)(2,1)S(1)} %copy-done.42, bf16[1024,3072]{1,0:T(8,128)(2,1)} %get-tuple-element.105.refs_0_), kind=kOutput, calls=%fused_computation.1 | convolution fusion | flops 4834197504 | bytes 11010048 | tf_op jit(solution)/shard_map/dot_general | solution.py:787
  313.0 54.8 %exchange_back.2 = (bf16[1024,1536]{1,0:T(8,128)(2,1)}, f32[2,8,1536]{2,1,0:T(8,128)}, bf16[1024,1536]{1,0:T(8,128)(2,1)}, bf16[1536,1536]{1,0:T(8,128)(2,1)}, bf16[1536,1536]{1,0:T(8,128)(2,1)}) custom-call(bf16[1024,3072]{1,0:T(8,128)(2,1)} %get-tuple-element.105.refs_0_, bf16[1536,3072]{1,0:T(8,128)(2,1)} %all-gather.2.cloned.1.call-done.gate_ref.up_ref.refs_1_, ...), custom_call_target="tpu_custom_call" | custom-call | flops 9663676416 | bytes 100000000 | tf_op jit(solution)/shard_map/exchange_back/pallas_call | solution.py:1589
  367.8 0.5 reduce-scatter.9.cloned.1.call-update
  368.9 0.8 copy-done
  369.7 3.9 convolution_convert_fusion.4.refs_3_
  373.7 7.5 %cross_attention_back.1 = (bf16[1024,384]{1,0:T(8,128)(2,1)}, bf16[128,768]{1,0:T(8,128)(2,1)}) custom-call(bf16[1024,384]{1,0:T(8,128)(2,1)} %convolution_convert_fusion.5.q_ref.refs_0_, bf16[128,768]{1,0:T(8,128)(2,1)} %convolution_convert_fusion.6.k_ref.v_ref.refs_1_.refs_2_, bf16[128,768]{1,0:T(8,128)(2,1)} %convolution_convert_fusion.6.k_ref.v_ref.refs_1_.refs_2_, ...), custom_call_target="tpu_custom_call" | custom-call | flops 503316480 | bytes 3145728 | tf_op jit(solution)/shard_map/cross_attention_back/pallas_call | solution.py:752
  381.2 58.4 %exchange_back.3 = (bf16[1024,1536]{1,0:T(8,128)(2,1)}, f32[2,8,1536]{2,1,0:T(8,128)}, bf16[192,1536]{1,0:T(8,128)(2,1)}, bf16[192,1536]{1,0:T(8,128)(2,1)}, bf1...) custom-call(bf16[1024,384]{1,0:T(8,128)(2,1)} %get-tuple-element.111.r, ...), custom_call_target="tpu_custom_call" | custom-call | flops 1207959552 | bytes 100000000 | tf_op jit(solution)/shard_map/exchange_back/pallas_call | solution.py:1589
  439.6 5.0 convolution_convert_fusion.3.refs_3_
  445.1 1.0 select_convert_fusion.refs_8_
  446.1 35.6 %self_attention_back.1 = (bf16[1024,1152]{1,0:T(8,128)(2,1)}, bf16[192,1536]{1,0:T(8,128)(2,1)}, bf16[192,1536]{1,0:T(8,128)(2,1)}, bf16[256,1536]{1,0:T(8,128)(2,1)}) custom-call(bf16[1024,384]{1,0:T(8,128)(2,1)} %get-tuple-element.114.refs_0_, bf16[1024,384]{1,0:T(8,128)(2,1)} %get-tuple-element.115.refs_1_, bf16[1024,384]{1,0:T(8,128)(2,1)} %get-tuple-element.116.refs_2_, ...), custom_call_target="tpu_custom_call" | custom-call | flops 4026531840 | bytes 100000000 | tf_op jit(solution)/shard_map/self_attention_back/pallas_call | solution.py:701
  481.8 8.7 %convolution_convert_fusion = bf16[1536,1152]{1,0:T(8,128)(2,1)} fusion(bf16[1024,1536]{1,0:T(8,128)(2,1)} %get-tuple-element.122, bf16[1024,1152]{1,0:T(8,128)(2,1)} %get-tuple-element.123.refs_0_), kind=kOutput, calls=%fused_computation | convolution fusion | flops 3625648128 | bytes 9043968 | tf_op jit(solution)/shard_map/dot_general | solution.py:787
  490.5 0.8 slice.192
  491.3 1.6 convert_reduce_fusion
  493.3 2.0 add_bitcast_fusion.2
  496.0 3.2 copy.49
  499.3 2.8 convolution_convert_fusion.2.refs_10_
  502.1 1.6 add_convert_fusion.refs_6_
  503.8 71.3 %exchange_half.1 = (bf16[512,1536]{1,0:T(8,128)(2,1)}, f32[2,8,1536]{2,1,0:T(8,128)}, bf16[192,1536]{1,0:T(8,128)(2,1)}, bf16[192,1536]{1,0:T(8,128)(2,1)}, bf16...) custom-call(bf16[1024,1152]{1,0:T(8,128)(2,1)} %get-tuple-element.12, ...), custom_call_target="tpu_custom_call" | custom-call | flops 3623878656 | bytes 100000000 | tf_op jit(solution)/shard_map/exchange_half/pallas_call | solution.py:1589
  575.1 1.1 reduce_sum.45
  576.3 0.6 pad_bitcast_fusion.refs_1_
  577.0 2.1 select_bitcast_fusion
  579.1 1.3 add_bitcast_fusion
  580.4 89.9 %spread_gradient.1 = (bf16[1024,1536]{1,0:T(8,128)(2,1)}, bf16[128,1536]{1,0:T(8,128)(2,1)}, f32[128,256]{1,0:T(8,128)}, bf16[192,384]{1,0:T(8,128)(2,1)}, bf16[...) custom-call(bf16[512,1536]{1,0:T(8,128)(2,1)} %get-tuple-element.131, ...), custom_call_target="tpu_custom_call" | custom-call | bytes 100000000 | tf_op jit(solution)/shard_map/spread_gradient/pallas_call | solution.py:1746
  670.3 1.1 convert_add_fusion.2
  671.4 0.9 reshape.118
  672.3 1.5 convert_add_fusion.1
  673.8 1.0 copy.60
  674.8 2.4 slice_bitcast_fusion
  677.2 1.0 slice.201
  678.2 0.6 fusion.28
  678.8 0.8 add_bitcast_fusion.3
  679.6 0.8 convert_add_fusion.3
  680.4 0.8 add_bitcast_fusion.4
  681.2 1.0 fusion.9
  (120 shorter events, 4.0 us)
Async XLA Ops:
  7.2 9.5 %copy-start.7 = (bf16[1,1023,1536]{2,1,0:T(8,128)(2,1)S(1)}, bf16[1,1023,1536]{2,1,0:T(8,128)(2,1)}, u32[]{:S(2)}) copy-start(bf16[1,1023,1536]{2,1,0:T(8,128)(2,1)} %param.24) | copy-start | bytes 9427972
  7.2 270.3 %all-gather.2.cloned.1.call-start = ((), (), s32[]{:S(2)}) async-start(), calls=%async_computation.4 | async-start | bytes 11796480 | tf_op jit(solution)/shard_map/all_gather | solution.py:811
  16.7 2.4 copy-start.25
  16.7 2.4 copy-start.26
  16.7 2.4 copy-start.27
  135.2 0.7 copy-start.38
  135.2 1.3 copy-start.39
  135.2 246.0 %reduce-scatter.5.cloned.1.call-start = ((), (), s32[]{:S(2)}) async-start(), calls=%async_computation.5 | async-start | bytes 5898240 | tf_op jit(solution)/shard_map/reduce_scatter | solution.py:815
  207.1 19.5 %collective-permute-start = (bf16[256,1536]{1,0:T(8,128)(2,1)S(1)}, bf16[256,1536]{1,0:T(8,128)(2,1)}, u32[]{:S(2)}, u32[]{:S(2)}) collective-permute-start(bf16[256,1536]{1,0:T(8,128)(2,1)S(1)} %broadcast_select_fusion.2), channel_id=1, source_target_pairs={{0,1},{1,0},{2,3},{3,2},{4,5},{5,4},{6,7},{7,6},{8,9},{9,8},{10,11... | collective-permute-start | bytes 2359304 | tf_op jit(solution)/shard_map/ppermute | solution.py:548
  207.2 3.7 copy-start.24
  211.8 6.6 copy-start.11
  227.8 0.9 copy-start.2
  227.8 2.1 copy-start.3
  227.8 2.8 copy-start.40
  227.8 3.4 copy-start.41
  229.9 47.5 %collective-permute-start.1 = (bf16[512,1536]{1,0:T(8,128)(2,1)}, bf16[512,1536]{1,0:T(8,128)(2,1)}, u32[]{:S(2)}, u32[]{:S(2)}) collective-permute-start(bf16[512,1536]{1,0:T(8,128)(2,1)} %pad_maximum_fusion.1.mine_ref.refs_3_), channel_id=1, source_target_pairs={{0,4},{1,5},{2,6},{3,7},{4,0},{5,1},{6,2},{7,3},{8,12},{9,13},{10,... | collective-permute-start | bytes 4718600 | tf_op jit(solution)/shard_map/ppermute | solution.py:548
  277.5 26.5 %copy-start.42 = (bf16[1024,1536]{1,0:T(8,128)(2,1)S(1)}, bf16[1024,1536]{1,0:T(8,128)(2,1)}, u32[]{:S(2)}) copy-start(bf16[1024,1536]{1,0:T(8,128)(2,1)} %get-tuple-element.98.n_ref.refs_8_) | copy-start | bytes 9437188
  312.7 133.4 %reduce-scatter.7.cloned.1.call-start = ((), (), s32[]{:S(2)}) async-start(), calls=%async_computation.6 | async-start | bytes 5898240 | tf_op jit(solution)/shard_map/reduce_scatter | solution.py:815
  367.8 136.0 %reduce-scatter.9.cloned.1.call-start = ((), (), s32[]{:S(2)}) async-start(), calls=%async_computation.7 | async-start | bytes 5898240 | tf_op jit(solution)/shard_map/reduce_scatter | solution.py:815
  367.8 1.9 copy-start
  368.4 212.0 %reduce-scatter.11.cloned.1.call-start = ((), (), s32[]{:S(2)}) async-start(), calls=%async_computation.8 | async-start | bytes 4423680 | tf_op jit(solution)/shard_map/reduce_scatter | solution.py:815
  439.6 5.1 copy-start.4
  439.6 5.0 copy-start.12
  490.4 2.6 copy-start.35
  490.4 2.7 copy-start.36
  493.3 2.0 copy-start.17
  493.3 2.1 copy-start.20
  493.3 2.3 copy-start.21
  496.0 3.2 copy-start.10
  496.0 3.2 copy-start.19
  499.3 2.9 copy-start.8
  499.3 2.9 copy-start.18
  499.3 2.9 copy-start.37
  503.8 73.2 %copy-start.1 = (bf16[256,1536]{1,0:T(8,128)(2,1)S(1)}, bf16[256,1536]{1,0:T(8,128)(2,1)}, u32[]{:S(2)}) copy-start(bf16[256,1536]{1,0:T(8,128)(2,1)} %add_convert_fusion.refs_6_) | copy-start | bytes 2359300
  575.1 4.0 copy-start.5
  575.1 4.0 copy-start.22
  575.1 4.0 copy-start.23
  580.4 90.0 %copy-start.16 = (bf16[192,768]{1,0:T(8,128)(2,1)S(1)}, bf16[192,768]{1,0:T(8,128)(2,1)}, u32[]{:S(2)}) copy-start(bf16[192,768]{1,0:T(8,128)(2,1)} %get-tuple-element.137.refs_4_) | copy-start | bytes 884740
  580.4 91.9 %copy-start.6 = (bf16[384,1152]{1,0:T(8,128)(2,1)S(1)}, bf16[384,1152]{1,0:T(8,128)(2,1)}, u32[]{:S(2)}) copy-start(bf16[384,1152]{1,0:T(8,128)(2,1)} %reduce-scatter.11.cloned.1.call-done.refs_6_) | copy-start | bytes 2654212
  672.3 2.5 copy-start.9
  674.7 3.4 copy-start.34
  674.7 4.1 copy-start.15
  674.8 4.1 copy-start.32
  674.8 4.1 copy-start.33
  674.8 4.8 copy-start.14
  674.8 4.8 copy-start.30
  674.8 4.8 copy-start.31
  674.8 5.6 copy-start.13
  674.8 5.6 copy-start.28
  674.8 5.6 copy-start.29
Sparse Core Ops, SparseCore 0:
  135.3 95.9 all-gather.1
  312.8 54.7 reduce-scatter.4
  370.6 57.1 reduce-scatter.6
  430.6 57.0 reduce-scatter.8
  490.6 69.1 reduce-scatter.10
